TPU v7x, 512 devices: a whole 4x4x16 slice. The times are simulated.
512 devices in a mesh: dp: 8 (over z_lo, core), seq: 64 (over y, z_hi, x).
Axes of the slice: x: 4, y: 4, z: 16 (z_hi: 4, z_lo: 4; z = z_hi * 4 + z_lo), core: 2. Of those that a mesh axis runs over, the one named last changes fastest.
Arguments:
- inputs: bfloat16 [8, 32768, 768], P('dp', 'seq'), may hold values from -6 to 6
- cotangent: bfloat16 [8, 32768, 768], P('dp', 'seq'), may hold values from -1.5 to 1.5
- factor_one: bfloat16 [64, 512, 512], P('seq'), may hold values from -0.25 to 0.25
- factor_two: bfloat16 [512, 64, 64], P('seq'), may hold values from -0.75 to 0.75
- up_weight: bfloat16 [2, 384, 1536], P(None, None, 'dp'), may hold values from -0.3125 to 0.3125
- down_weight: bfloat16 [2, 1536, 384], P(None, 'dp'), may hold values from -0.15625 to 0.15625
Outputs:
- outputs: bfloat16 [8, 32768, 768], P('dp', 'seq')
- grad_inputs: bfloat16 [8, 32768, 768], P('dp', 'seq')
- grad_factor_one: float32 [64, 512, 512], P('seq', 'dp')
- grad_factor_two: float32 [512, 64, 64], P('seq', 'dp')
All inputs are finite; a program needn't handle non-finite values.
Results may differ from a plain program's by a relative error of at most 0.0066.
Values may be sent and summed in bfloat16 or wider, within the bound.
No kernel may reach another device: no remote copies, remote signals or barrier semaphores. Data moves between devices by JAX's collectives and lax.ppermute only.
A program may use at most 64 MiB of HBM per device.

v0:
```python
import jax
import jax.numpy as jnp
from jax import lax
from jax.sharding import Mesh
from jax.sharding import PartitionSpec as P

F32 = jnp.float32
BF16 = jnp.bfloat16
SIDE = 4
CORES = 2
TO = ("x", "hi", "y")
WEIGHT_SLICES = 8


def nt(a, b):
    return lax.dot_general(a, b, (((1,), (1,)), ((), ())), preferred_element_type=F32)


def nn(a, b):
    return lax.dot_general(a, b, (((1,), (0,)), ((), ())), preferred_element_type=F32)


def tn(a, b):
    return lax.dot_general(a, b, (((0,), (0,)), ((), ())), preferred_element_type=F32)


def swap(x, axis=0):
    shape = x.shape
    rest = shape[axis] // SIDE**3
    x = x.reshape(shape[:axis] + (SIDE, SIDE, SIDE, rest) + shape[axis + 1 :])
    return jnp.swapaxes(x, axis, axis + 2).reshape(shape)


def exchange(x, blocks):
    out = lax.all_to_all(
        x.reshape(blocks, x.shape[0] // blocks, x.shape[1]), TO, split_axis=0, concat_axis=0, tiled=True
    )
    return out.reshape(x.shape)


def shift(x, axis, step):
    return lax.ppermute(x, axis, [(i, (i + step) % SIDE) for i in range(SIDE)])


def gather_weights(up_weight, down_weight):
    groups, group_ch, own_hid = up_weight.shape
    rows = own_hid // WEIGHT_SLICES
    own = jnp.stack([jnp.swapaxes(up_weight, 1, 2), down_weight], axis=1)
    place = lax.axis_index("y") * 2 + lax.rem(lax.axis_index("x"), 2)
    piece = lax.dynamic_slice_in_dim(own, place * rows, rows, axis=2)
    column = jnp.concatenate([piece] + [shift(piece, "lo", k) for k in (1, 2, 3)], axis=2)
    pair = jnp.concatenate([column, lax.ppermute(column, "x", [(i, i ^ 1) for i in range(SIDE)])], axis=2)
    return pair


def spread_weights(pair):
    plane = jnp.concatenate([pair] + [shift(pair, "y", k) for k in (1, 2, 3)], axis=2)
    other = lax.ppermute(plane, "core", [(0, 1), (1, 0)])
    return plane, other


def shards(inputs, cotangent, factor_one, factor_two, up_weight, down_weight):
    groups, group_ch, _ = up_weight.shape
    block = factor_one.shape[1]
    own_p, blocks, _ = factor_two.shape
    n_dp = SIDE * CORES
    x_nat = inputs[0]
    one = swap(factor_one[0])

    cols_one = exchange(nn(one, x_nat).astype(BF16), blocks)

    eye = jnp.eye(own_p, dtype=BF16)
    two = jnp.transpose(swap(swap(factor_two, 1), 2), (1, 0, 2))
    two = (two[:, :, :, None] * eye[None, :, None, :]).reshape(block, block)
    pair = gather_weights(up_weight, down_weight)
    x_all, cot_all = swap(x_nat), swap(cotangent[0])
    cols_one, pair, two, x_all, cot_all = lax.optimization_barrier((cols_one, pair, two, x_all, cot_all))

    weights = spread_weights(pair)
    mixed = exchange(nn(two, cols_one).astype(BF16), blocks)

    def cols(a, g):
        return lax.slice_in_dim(a, g * group_ch, (g + 1) * group_ch, axis=1)

    mixed_f = mixed.astype(F32)
    silu_vals, silu_back = jax.vjp(jax.nn.silu, x_all.astype(F32))
    gated = (mixed_f * silu_vals).astype(BF16)
    results, grads = [], []
    for g in range(groups):
        cot = cols(cot_all, g)
        result, grad_gated = cols(gated, g).astype(F32), cot.astype(F32)
        for w in weights:
            up, down = w[g, 0], w[g, 1]
            hidden, gelu_back = jax.vjp(jax.nn.gelu, nt(cols(gated, g), up))
            result = result + nn(hidden.astype(BF16), down)
            grad_pre = gelu_back(nt(cot, down))[0].astype(BF16)
            grad_gated = grad_gated + nn(grad_pre, up)
        results.append(result.astype(BF16))
        grads.append(grad_gated)
    grad_gated = jnp.concatenate(grads, axis=1)
    grad_cols = exchange((grad_gated * silu_vals).astype(BF16), blocks)
    outputs = swap(jnp.concatenate(results, axis=1))[None]
    gate_in = swap(silu_back(grad_gated * mixed_f)[0])
    grad_cols, outputs, gate_in = lax.optimization_barrier((grad_cols, outputs, gate_in))

    grad_one = exchange(tn(two, grad_cols).astype(BF16), blocks)

    same = jnp.tile(jnp.eye(own_p, dtype=F32), (blocks, blocks))
    pick = swap(jnp.repeat(jnp.eye(blocks, dtype=BF16), own_p, axis=0))
    term_two = nn((nt(grad_cols, cols_one) * same).astype(BF16), pick).astype(BF16)
    term_two = swap(term_two.reshape(blocks, own_p * blocks)).reshape(n_dp, -1, block)
    grad_one, term_two = lax.optimization_barrier((grad_one, term_two))
    term_one = swap(nt(grad_one, x_nat).astype(BF16)).reshape(n_dp, block // n_dp, block)
    summed = lax.all_to_all(
        jnp.concatenate([term_one, term_two], axis=1), ("lo", "core"), split_axis=0, concat_axis=0, tiled=True
    )
    summed = jnp.sum(summed.astype(F32), axis=0)
    grad_first = summed[: block // n_dp][None]
    grad_second = jnp.transpose(summed[block // n_dp :].reshape(blocks // n_dp, own_p, blocks), (1, 0, 2))

    grad_inputs = (gate_in + tn(one, grad_one)).astype(BF16)[None]
    return outputs, grad_inputs, grad_first, grad_second


def solution(mesh):
    grid = Mesh(mesh.devices.reshape(SIDE, CORES, SIDE, SIDE, SIDE), ("lo", "core", "y", "hi", "x"))
    dp, seq = ("lo", "core"), ("y", "hi", "x")
    in_specs = (P(dp, seq, None), P(dp, seq, None), P(seq, None, None), P(seq, None, None), P(None, None, dp), P(None, dp, None))
    out_specs = (P(dp, seq, None), P(dp, seq, None), P(seq, dp, None), P(seq, dp, None))
    return jax.shard_map(shards, mesh=grid, in_specs=in_specs, out_specs=out_specs, check_vma=False)
```

profile of v0, /device:TPU:1, one launch (start us, length us, event | category | flops | bytes accessed | tf_op | source)
XLA Modules:
  0.0 303.1 jit_solution(2554279958363980042)
XLA Ops:
  0.6 1.1 copy.45
  2.5 2.6 fusion.35
  5.2 21.9 %all-to-all-start = ((bf16[64,8,768]{2,1,0:T(8,128)(2,1)}), bf16[64,8,768]{2,1,0:T(8,128)(2,1)S(1)}, u32[]{:S(2)}, u32[]{:S(2)}) async-start(bf16[64,8,768]{2,1,0:T(8,128)(2,1)} %fusion.35), calls=%async_computation | async-start | bytes 1572864 | tf_op jit(solution)/shard_map/all_to_all | solution.py:35
  27.7 2.6 collective-permute-start
  30.4 3.1 %collective-permute-start.1 = (bf16[2,2,24,384]{3,2,0,1:T(8,128)(2,1)S(1)}, bf16[2,2,24,384]{3,2,0,1:T(8,128)(2,1)S(1)}, u32[]{:S(2)}, u32[]{:S(2)}) collective-permute-start(bf16[2,2,24,384]{3,2,0,1:T(8,128)(2,1)S(1)} %get-tuple-element.37), channel_id=1, source_target_pairs={{0,256},{128,384},{256,0},{384,128},{1,257},{129,385},{257,1},{385... | collective-permute-start | bytes 221192 | tf_op jit(solution)/shard_map/ppermute | solution.py:42
  33.5 3.5 %collective-permute-start.2 = (bf16[2,2,24,384]{3,2,0,1:T(8,128)(2,1)S(1)}, bf16[2,2,24,384]{3,2,0,1:T(8,128)(2,1)S(1)}, u32[]{:S(2)}, u32[]{:S(2)}) collective-permute-start(bf16[2,2,24,384]{3,2,0,1:T(8,128)(2,1)S(1)} %get-tuple-element.37), channel_id=1, source_target_pairs={{0,384},{128,0},{256,128},{384,256},{1,385},{129,1},{257,129},{385... | collective-permute-start | bytes 221192 | tf_op jit(solution)/shard_map/ppermute | solution.py:42
  37.5 1.2 copy.47
  38.9 7.1 %broadcast_multiply_fusion = bf16[64,8,64,8]{3,2,1,0:T(8,128)(2,1)} fusion(bf16[8,8]{1,0:T(8,128)(2,1)S(1)} %fusion.90, bf16[64,8,64]{2,1,0:T(8,128)(2,1)S(1)} %copy.48), kind=kLoop, calls=%fused_computation | loop fusion | flops 262144 | bytes 589952 | tf_op jit(solution)/shard_map/mul | solution.py:74
  46.1 13.6 %mul.218 = bf16[512,512]{1,0:T(8,128)(2,1)} reshape(bf16[64,8,64,8]{3,2,1,0:T(8,128)(2,1)} %broadcast_multiply_fusion) | data formatting | bytes 1048576 | tf_op jit(solution)/shard_map/mul | solution.py:74
  59.7 1.0 copy-done.9
  60.9 4.7 %collective-permute-done.2 = bf16[2,2,24,384]{3,2,0,1:T(8,128)(2,1)S(1)} collective-permute-done((bf16[2,2,24,384]{3,2,0,1:T(8,128)(2,1)S(1)}, bf16[2,2,24,384]{3,2,0,1:T(8,128)(2,1)S(1)}, u32[]{:S(2)}, u32[]{:S(2)}) %collective-permute-start.2) | collective-permute-done | bytes 73760 | tf_op jit(solution)/shard_map/ppermute | solution.py:42
  65.6 3.0 %collective-permute-start.3 = (bf16[2,2,96,384]{3,2,0,1:T(8,128)(2,1)S(1)}, bf16[2,2,96,384]{3,2,0,1:T(8,128)(2,1)S(1)}, u32[]{:S(2)}, u32[]{:S(2)}) collective-permute-start(bf16[2,2,96,384]{3,2,0,1:T(8,128)(2,1)S(1)} %pad_maximum_fusion.3), channel_id=1, source_target_pairs={{0,1},{1,0},{2,3},{3,2},{4,5},{5,4},{6,7},{7,6},{8,9},{9,8},{10,11... | collective-permute-start | bytes 884744 | tf_op jit(solution)/shard_map/ppermute | solution.py:52
  70.6 4.5 %collective-permute-done.3 = bf16[2,2,96,384]{3,2,0,1:T(8,128)(2,1)S(1)} collective-permute-done((bf16[2,2,96,384]{3,2,0,1:T(8,128)(2,1)S(1)}, bf16[2,2,96,384]{3,2,0,1:T(8,128)(2,1)S(1)}, u32[]{:S(2)}, u32[]{:S(2)}) %collective-permute-start.3) | collective-permute-done | bytes 294944 | tf_op jit(solution)/shard_map/ppermute | solution.py:52
  75.8 1.5 fusion.36
  77.2 17.4 %all-to-all-start.1 = ((bf16[64,8,768]{2,1,0:T(8,128)(2,1)}), bf16[64,8,768]{2,1,0:T(8,128)(2,1)S(1)}, u32[]{:S(2)}, u32[]{:S(2)}) async-start(bf16[64,8,768]{2,1,0:T(8,128)(2,1)} %fusion.36), calls=%async_computation.1 | async-start | bytes 1572864 | tf_op jit(solution)/shard_map/all_to_all | solution.py:35
  94.6 2.9 collective-permute-start.4
  97.5 4.3 %collective-permute-start.5 = (bf16[2,2,192,384]{3,2,0,1:T(8,128)(2,1)}, bf16[2,2,192,384]{3,2,0,1:T(8,128)(2,1)S(1)}, u32[]{:S(2)}, u32[]{:S(2)}) collective-permute-start(bf16[2,2,192,384]{3,2,0,1:T(8,128)(2,1)} %constant_dynamic-update-slice_fusion), channel_id=1, source_target_pairs={{0,32},{16,48},{32,0},{48,16},{1,33},{17,49},{33,1},{49,17},{2,34}... | collective-permute-start | bytes 1769480 | tf_op jit(solution)/shard_map/ppermute | solution.py:42
  101.8 3.1 %collective-permute-start.6 = (bf16[2,2,192,384]{3,2,0,1:T(8,128)(2,1)}, bf16[2,2,192,384]{3,2,0,1:T(8,128)(2,1)S(1)}, u32[]{:S(2)}, u32[]{:S(2)}) collective-permute-start(bf16[2,2,192,384]{3,2,0,1:T(8,128)(2,1)} %constant_dynamic-update-slice_fusion), channel_id=1, source_target_pairs={{0,48},{16,0},{32,16},{48,32},{1,49},{17,1},{33,17},{49,33},{2,50}... | collective-permute-start | bytes 1769480 | tf_op jit(solution)/shard_map/ppermute | solution.py:42
  104.9 2.0 constant_dynamic-update-slice_fusion.8
  106.9 9.9 %collective-permute-done.4 = bf16[2,2,192,384]{3,2,0,1:T(8,128)(2,1)S(1)} collective-permute-done((bf16[2,2,192,384]{3,2,0,1:T(8,128)(2,1)}, bf16[2,2,192,384]{3,2,0,1:T(8,128)(2,1)S(1)}, u32[]{:S(2)}, u32[]{:S(2)}) %collective-permute-start.4) | collective-permute-done | bytes 589856 | tf_op jit(solution)/shard_map/ppermute | solution.py:42
  117.7 14.9 %collective-permute-done.5 = bf16[2,2,192,384]{3,2,0,1:T(8,128)(2,1)S(1)} collective-permute-done((bf16[2,2,192,384]{3,2,0,1:T(8,128)(2,1)}, bf16[2,2,192,384]{3,2,0,1:T(8,128)(2,1)S(1)}, u32[]{:S(2)}, u32[]{:S(2)}) %collective-permute-start.5) | collective-permute-done | bytes 589856 | tf_op jit(solution)/shard_map/ppermute | solution.py:42
  134.4 4.3 %collective-permute-start.7 = (bf16[2,2,768,384]{3,2,0,1:T(8,128)(2,1)}, bf16[2,2,768,384]{3,2,0,1:T(8,128)(2,1)}, u32[]{:S(2)}, u32[]{:S(2)}) collective-permute-start(bf16[2,2,768,384]{3,2,0,1:T(8,128)(2,1)} %constant_dynamic-update-slice_fusion.5), channel_id=1, source_target_pairs={{0,64},{64,0},{1,65},{65,1},{2,66},{66,2},{3,67},{67,3},{4,68},{68... | collective-permute-start | bytes 7077896 | tf_op jit(solution)/shard_map/ppermute | solution.py:58
  139.3 2.8 fusion.68
  142.1 2.9 fusion.72
  145.0 2.9 fusion.70
  147.8 4.2 %fusion.65 = f32[512,384]{1,0:T(8,128)} fusion(f32[512,768]{1,0:T(8,128)} %fusion.70, bf16[2,2,768,384]{3,2,0,1:T(8,128)(2,1)} %collective-permute-done.7, bf16[512,768]{1,0:T(8,128)(2,1)S(1)} %bitcast.154), kind=kOutput, calls=%fused_computation.95 | convolution fusion | flops 611844096 | bytes 3932160 | tf_op jit(solution)/shard_map/dot_general | solution.py:20
  152.0 4.5 %fusion.43 = f32[512,384]{1,0:T(8,128)} fusion(f32[512,384]{1,0:T(8,128)} %fusion.65, f32[512,768]{1,0:T(8,128)} %fusion.68, bf16[2,2,768,384]{3,2,0,1:T(8,128)(2,1)} %constant_dynamic-update-slice_fusion.5, bf16[512,768]{1,0:T(8,128)(2,1)S(1)} %bitcast.155), kind=kOutput, calls=%fused_computation.74 | convolution fusion | flops 612433920 | bytes 5111808 | tf_op jit(solution)/shard_map/dot_general | solution.py:20
  156.5 2.8 fusion.74
  159.3 4.2 %fusion.63 = f32[512,384]{1,0:T(8,128)} fusion(f32[512,768]{1,0:T(8,128)} %fusion.74, bf16[2,2,768,384]{3,2,0,1:T(8,128)(2,1)} %collective-permute-done.7, bf16[512,768]{1,0:T(8,128)(2,1)S(1)} %bitcast.156), kind=kOutput, calls=%fused_computation.94 | convolution fusion | flops 611844096 | bytes 3932160 | tf_op jit(solution)/shard_map/dot_general | solution.py:20
  163.4 4.5 %fusion.42 = f32[512,384]{1,0:T(8,128)} fusion(f32[512,384]{1,0:T(8,128)} %fusion.63, f32[512,768]{1,0:T(8,128)} %fusion.72, bf16[2,2,768,384]{3,2,0,1:T(8,128)(2,1)} %constant_dynamic-update-slice_fusion.5, bf16[512,768]{1,0:T(8,128)(2,1)S(1)} %bitcast.157), kind=kOutput, calls=%fused_computation.72 | convolution fusion | flops 612433920 | bytes 5111808 | tf_op jit(solution)/shard_map/dot_general | solution.py:20
  167.9 3.7 %fusion.33 = (f32[512,768]{1,0:T(8,128)}, bf16[64,8,768]{2,1,0:T(8,128)(2,1)}) fusion(bf16[512,768]{1,0:T(8,128)(2,1)S(1)} %bitcast.138, f32[512,384]{1,0:T(8,128)} %fusion.42, f32[512,384]{1,0:T(8,128)} %fusion.43, bf16[64,8,768]{2,1,0:T(8,128)(2,1)S(1)} %all-to-all-done.1), kind=kLoop, calls=%fused_computation.48 | loop fusion | flops 6291456 | bytes 5505024 | tf_op jit(solution)/shard_map/transpose(jvp(jit(silu)))/add_any | solution.py:86
  171.6 14.2 %all-to-all-start.2 = ((bf16[64,8,768]{2,1,0:T(8,128)(2,1)}), bf16[64,8,768]{2,1,0:T(8,128)(2,1)S(1)}, u32[]{:S(2)}, u32[]{:S(2)}) async-start(bf16[64,8,768]{2,1,0:T(8,128)(2,1)} %get-tuple-element.39), calls=%async_computation.2 | async-start | bytes 1572864 | tf_op jit(solution)/shard_map/all_to_all | solution.py:35
  185.8 1.8 fusion.60
  187.6 1.8 fusion.61
  189.5 1.9 fusion.44
  191.4 1.8 fusion.45
  195.0 18.5 %all-to-all-done.2 = bf16[64,8,768]{2,1,0:T(8,128)(2,1)S(1)} async-done(((bf16[64,8,768]{2,1,0:T(8,128)(2,1)}), bf16[64,8,768]{2,1,0:T(8,128)(2,1)S(1)}, u32[]{:S(2)}, u32[]{:S(2)}) %all-to-all-start.2) | async-done | bytes 786464 | tf_op jit(solution)/shard_map/all_to_all | solution.py:35
  213.5 1.5 fusion.37
  214.9 7.7 %all-to-all-start.3 = ((bf16[64,8,768]{2,1,0:T(8,128)(2,1)}), bf16[64,8,768]{2,1,0:T(8,128)(2,1)S(1)}, u32[]{:S(2)}, u32[]{:S(2)}) async-start(bf16[64,8,768]{2,1,0:T(8,128)(2,1)} %fusion.37), calls=%async_computation.3 | async-start | bytes 1572864 | tf_op jit(solution)/shard_map/all_to_all | solution.py:35
  222.7 7.9 %tile.4 = f32[64,8,64,8]{3,2,1,0:T(8,128)} broadcast(f32[8,8]{1,0:T(8,128)S(1)} %fusion.89), dimensions={1,3} | broadcast | bytes 1048832 | tf_op jit(solution)/shard_map/tile | solution.py:108
  230.5 12.6 %tile.10 = f32[512,512]{1,0:T(8,128)S(1)} reshape(f32[64,8,64,8]{3,2,1,0:T(8,128)} %tile.4) | data formatting | bytes 2097152 | tf_op jit(solution)/shard_map/tile | solution.py:108
  243.2 2.8 fusion.47
  247.3 2.0 convolution_convert_fusion.3
  250.2 34.4 %all-to-all-start.4 = ((bf16[8,72,512]{2,1,0:T(8,128)(2,1)}), bf16[8,72,512]{2,1,0:T(8,128)(2,1)}, u32[]{:S(2)}, u32[]{:S(2)}) async-start(bf16[8,72,512]{2,1,0:T(8,128)(2,1)} %pad_maximum_fusion.2), calls=%async_computation.4 | async-start | bytes 1179648 | tf_op jit(solution)/shard_map/all_to_all | solution.py:114
  285.2 1.9 fusion.38
  287.0 1.2 copy.65
  288.2 12.4 %all-to-all-done.4 = bf16[8,72,512]{2,1,0:T(8,128)(2,1)} async-done(((bf16[8,72,512]{2,1,0:T(8,128)(2,1)}), bf16[8,72,512]{2,1,0:T(8,128)(2,1)}, u32[]{:S(2)}, u32[]{:S(2)}) %all-to-all-start.4) | async-done | bytes 589856 | tf_op jit(solution)/shard_map/all_to_all | solution.py:114
  300.6 1.2 convert_reduce_fusion
  (71 shorter events, 14.1 us)
Async XLA Ops:
  1.7 0.8 copy-start.4
  2.5 24.5 %copy-start.13 = (bf16[2,192,384]{2,1,0:T(8,128)(2,1)S(1)}, bf16[2,192,384]{2,1,0:T(8,128)(2,1)}, u32[]{:S(2)}) copy-start(bf16[2,192,384]{2,1,0:T(8,128)(2,1)} %param.11) | copy-start | bytes 884740
  2.5 24.5 %copy-start.14 = (bf16[2,384,192]{1,2,0:T(8,128)(2,1)S(1)}, bf16[2,384,192]{1,2,0:T(8,128)(2,1)}, u32[]{:S(2)}) copy-start(bf16[2,384,192]{1,2,0:T(8,128)(2,1)} %param.10) | copy-start | bytes 884740
  5.2 31.9 %copy-start.15 = (bf16[8,64,64]{2,1,0:T(8,128)(2,1)S(1)}, bf16[8,64,64]{2,1,0:T(8,128)(2,1)}, u32[]{:S(2)}) copy-start(bf16[8,64,64]{2,1,0:T(8,128)(2,1)} %param.9) | copy-start | bytes 196612
  5.2 70.6 %all-to-all-start = ((bf16[64,8,768]{2,1,0:T(8,128)(2,1)}), bf16[64,8,768]{2,1,0:T(8,128)(2,1)S(1)}, u32[]{:S(2)}, u32[]{:S(2)}) async-start(bf16[64,8,768]{2,1,0:T(8,128)(2,1)} %fusion.35), calls=%async_computation | async-start | bytes 1572864 | tf_op jit(solution)/shard_map/all_to_all | solution.py:35
  27.7 33.1 %collective-permute-start = (bf16[2,2,24,384]{3,2,0,1:T(8,128)(2,1)S(1)}, bf16[2,2,24,384]{3,2,0,1:T(8,128)(2,1)S(1)}, u32[]{:S(2)}, u32[]{:S(2)}) collective-permute-start(bf16[2,2,24,384]{3,2,0,1:T(8,128)(2,1)S(1)} %get-tuple-element.37), channel_id=1, source_target_pairs={{0,128},{128,256},{256,384},{384,0},{1,129},{129,257},{257,385},{3... | collective-permute-start | bytes 221192 | tf_op jit(solution)/shard_map/ppermute | solution.py:42
  30.4 30.5 %collective-permute-start.1 = (bf16[2,2,24,384]{3,2,0,1:T(8,128)(2,1)S(1)}, bf16[2,2,24,384]{3,2,0,1:T(8,128)(2,1)S(1)}, u32[]{:S(2)}, u32[]{:S(2)}) collective-permute-start(bf16[2,2,24,384]{3,2,0,1:T(8,128)(2,1)S(1)} %get-tuple-element.37), channel_id=1, source_target_pairs={{0,256},{128,384},{256,0},{384,128},{1,257},{129,385},{257,1},{385... | collective-permute-start | bytes 221192 | tf_op jit(solution)/shard_map/ppermute | solution.py:42
  33.5 32.1 %collective-permute-start.2 = (bf16[2,2,24,384]{3,2,0,1:T(8,128)(2,1)S(1)}, bf16[2,2,24,384]{3,2,0,1:T(8,128)(2,1)S(1)}, u32[]{:S(2)}, u32[]{:S(2)}) collective-permute-start(bf16[2,2,24,384]{3,2,0,1:T(8,128)(2,1)S(1)} %get-tuple-element.37), channel_id=1, source_target_pairs={{0,384},{128,0},{256,128},{384,256},{1,385},{129,1},{257,129},{385... | collective-permute-start | bytes 221192 | tf_op jit(solution)/shard_map/ppermute | solution.py:42
  46.0 13.6 %copy-start.10 = (bf16[1,512,768]{2,1,0:T(8,128)(2,1)S(1)}, bf16[1,512,768]{2,1,0:T(8,128)(2,1)}, u32[]{:S(2)}) copy-start(bf16[1,512,768]{2,1,0:T(8,128)(2,1)} %param.6) | copy-start | bytes 2359300
  59.6 1.1 copy-start.9
  60.8 15.0 %copy-start.11 = (bf16[512,512]{1,0:T(8,128)(2,1)S(1)}, bf16[512,512]{1,0:T(8,128)(2,1)}, u32[]{:S(2)}) copy-start(bf16[512,512]{1,0:T(8,128)(2,1)} %mul.218) | copy-start | bytes 1572868
  65.6 9.4 %collective-permute-start.3 = (bf16[2,2,96,384]{3,2,0,1:T(8,128)(2,1)S(1)}, bf16[2,2,96,384]{3,2,0,1:T(8,128)(2,1)S(1)}, u32[]{:S(2)}, u32[]{:S(2)}) collective-permute-start(bf16[2,2,96,384]{3,2,0,1:T(8,128)(2,1)S(1)} %pad_maximum_fusion.3), channel_id=1, source_target_pairs={{0,1},{1,0},{2,3},{3,2},{4,5},{5,4},{6,7},{7,6},{8,9},{9,8},{10,11... | collective-permute-start | bytes 884744 | tf_op jit(solution)/shard_map/ppermute | solution.py:52
  75.8 1.5 copy-start.2
  77.2 61.5 %all-to-all-start.1 = ((bf16[64,8,768]{2,1,0:T(8,128)(2,1)}), bf16[64,8,768]{2,1,0:T(8,128)(2,1)S(1)}, u32[]{:S(2)}, u32[]{:S(2)}) async-start(bf16[64,8,768]{2,1,0:T(8,128)(2,1)} %fusion.36), calls=%async_computation.1 | async-start | bytes 1572864 | tf_op jit(solution)/shard_map/all_to_all | solution.py:35
  94.6 22.2 %collective-permute-start.4 = (bf16[2,2,192,384]{3,2,0,1:T(8,128)(2,1)}, bf16[2,2,192,384]{3,2,0,1:T(8,128)(2,1)S(1)}, u32[]{:S(2)}, u32[]{:S(2)}) collective-permute-start(bf16[2,2,192,384]{3,2,0,1:T(8,128)(2,1)} %constant_dynamic-update-slice_fusion), channel_id=1, source_target_pairs={{0,16},{16,32},{32,48},{48,0},{1,17},{17,33},{33,49},{49,1},{2,18}... | collective-permute-start | bytes 1769480 | tf_op jit(solution)/shard_map/ppermute | solution.py:42
  97.5 35.0 %collective-permute-start.5 = (bf16[2,2,192,384]{3,2,0,1:T(8,128)(2,1)}, bf16[2,2,192,384]{3,2,0,1:T(8,128)(2,1)S(1)}, u32[]{:S(2)}, u32[]{:S(2)}) collective-permute-start(bf16[2,2,192,384]{3,2,0,1:T(8,128)(2,1)} %constant_dynamic-update-slice_fusion), channel_id=1, source_target_pairs={{0,32},{16,48},{32,0},{48,16},{1,33},{17,49},{33,1},{49,17},{2,34}... | collective-permute-start | bytes 1769480 | tf_op jit(solution)/shard_map/ppermute | solution.py:42
  101.8 31.7 %collective-permute-start.6 = (bf16[2,2,192,384]{3,2,0,1:T(8,128)(2,1)}, bf16[2,2,192,384]{3,2,0,1:T(8,128)(2,1)S(1)}, u32[]{:S(2)}, u32[]{:S(2)}) collective-permute-start(bf16[2,2,192,384]{3,2,0,1:T(8,128)(2,1)} %constant_dynamic-update-slice_fusion), channel_id=1, source_target_pairs={{0,48},{16,0},{32,16},{48,32},{1,49},{17,1},{33,17},{49,33},{2,50}... | collective-permute-start | bytes 1769480 | tf_op jit(solution)/shard_map/ppermute | solution.py:42
  134.4 10.5 %collective-permute-start.7 = (bf16[2,2,768,384]{3,2,0,1:T(8,128)(2,1)}, bf16[2,2,768,384]{3,2,0,1:T(8,128)(2,1)}, u32[]{:S(2)}, u32[]{:S(2)}) collective-permute-start(bf16[2,2,768,384]{3,2,0,1:T(8,128)(2,1)} %constant_dynamic-update-slice_fusion.5), channel_id=1, source_target_pairs={{0,64},{64,0},{1,65},{65,1},{2,66},{66,2},{3,67},{67,3},{4,68},{68... | collective-permute-start | bytes 7077896 | tf_op jit(solution)/shard_map/ppermute | solution.py:58
  171.6 14.2 %copy-start.7 = (f32[512,768]{1,0:T(8,128)S(1)}, f32[512,768]{1,0:T(8,128)}, u32[]{:S(2)}) copy-start(f32[512,768]{1,0:T(8,128)} %fusion.70) | copy-start | bytes 4718596
  171.6 41.9 %all-to-all-start.2 = ((bf16[64,8,768]{2,1,0:T(8,128)(2,1)}), bf16[64,8,768]{2,1,0:T(8,128)(2,1)S(1)}, u32[]{:S(2)}, u32[]{:S(2)}) async-start(bf16[64,8,768]{2,1,0:T(8,128)(2,1)} %get-tuple-element.39), calls=%async_computation.2 | async-start | bytes 1572864 | tf_op jit(solution)/shard_map/all_to_all | solution.py:35
  185.8 1.8 copy-start.8
  187.6 1.9 copy-start.6
  189.5 1.9 copy-start.5
  193.1 1.7 copy-start
  194.8 18.6 %copy-start.12 = (bf16[512,512]{1,0:T(8,128)(2,1)S(1)}, bf16[512,512]{1,0:T(8,128)(2,1)}, u32[]{:S(2)}) copy-start(bf16[512,512]{1,0:T(8,128)(2,1)} %mul.218) | copy-start | bytes 1572868
  213.5 1.5 copy-start.3
  214.9 32.3 %all-to-all-start.3 = ((bf16[64,8,768]{2,1,0:T(8,128)(2,1)}), bf16[64,8,768]{2,1,0:T(8,128)(2,1)S(1)}, u32[]{:S(2)}, u32[]{:S(2)}) async-start(bf16[64,8,768]{2,1,0:T(8,128)(2,1)} %fusion.37), calls=%async_computation.3 | async-start | bytes 1572864 | tf_op jit(solution)/shard_map/all_to_all | solution.py:35
  247.2 2.1 copy-start.1
  250.2 50.3 %all-to-all-start.4 = ((bf16[8,72,512]{2,1,0:T(8,128)(2,1)}), bf16[8,72,512]{2,1,0:T(8,128)(2,1)}, u32[]{:S(2)}, u32[]{:S(2)}) async-start(bf16[8,72,512]{2,1,0:T(8,128)(2,1)} %pad_maximum_fusion.2), calls=%async_computation.4 | async-start | bytes 1179648 | tf_op jit(solution)/shard_map/all_to_all | solution.py:114
where the time goes:
time: 305 us; the launch traced here: 303 us
  starting transfers between devices  123 us (40%)
  waiting for transfers between devices  64.8 us (21%)
  local copies, waits for them, and re-layouts  52.3 us (17%)
  matrix products  48.2 us (16%)
  other arithmetic  14.2 us (5%)
    all_to_all x4, starting transfers between devices, exchange(): lax.all_to_all(x.reshape(blocks, x.shape[0] // blocks, x.shape[1]), TO, s...  61.1 us
    all_to_all x1, starting transfers between devices, shards(): lax.all_to_all(jnp.concatenate([term_one, term_two], axis=1), ('lo', 'cor...  34.4 us
    dot_general x11, matrix products, nn(): lax.dot_general(a, b, (((1,), (0,)), ((), ())), preferred_element_type=F32)  31.5 us
    ppermute x6, waiting for transfers between devices, shift(): return lax.ppermute(x, axis, [(i, (i + step) % SIDE) for i in range(SIDE)])  29.5 us
    another operation x2, local copies, waits for them, and re-layouts, shards(): same = jnp.tile(jnp.eye(own_p, dtype=F32), (blocks, blocks))  20.4 us
    ppermute x6, starting transfers between devices, shift(): return lax.ppermute(x, axis, [(i, (i + step) % SIDE) for i in range(SIDE)])  19.6 us
    all_to_all x4, waiting for transfers between devices, exchange(): lax.all_to_all(x.reshape(blocks, x.shape[0] // blocks, x.shape[1]), TO, s...  18.5 us
    mul x1, local copies, waits for them, and re-layouts, shards(): two = (two[:, :, :, None] * eye[None, :, None, :]).reshape(block, block)  13.6 us
  transfers between devices with their start and end apart: 13, of which 7 were waited for; matrix products, arithmetic and copies ran while one was open for 24% of the time, Pallas kernels for 0%

commit v1 on v0

v1 whole, which is shorter than its diff:
```python
import functools

import jax
import jax.numpy as jnp
from jax import lax
from jax.experimental import pallas as pl
from jax.experimental.pallas import tpu as pltpu
from jax.sharding import Mesh
from jax.sharding import PartitionSpec as P


F32 = jnp.float32
BF16 = jnp.bfloat16
SIDE = 4
CORES = 2
RING = SIDE * SIDE
TO = ("x", "hi", "y")
WEIGHT_SLICES = 8
C0 = 0.7978845608028654
C1 = 0.044715


def nt(a, b):
    return lax.dot_general(a, b, (((1,), (1,)), ((), ())), preferred_element_type=F32)


def nn(a, b):
    return lax.dot_general(a, b, (((1,), (0,)), ((), ())), preferred_element_type=F32)


def tn(a, b):
    return lax.dot_general(a, b, (((0,), (0,)), ((), ())), preferred_element_type=F32)


def swap(x, axis=0):
    shape = x.shape
    rest = shape[axis] // SIDE**3
    x = x.reshape(shape[:axis] + (SIDE, SIDE, SIDE, rest) + shape[axis + 1 :])
    return jnp.swapaxes(x, axis, axis + 2).reshape(shape)


def exchange(x, blocks):
    out = lax.all_to_all(
        x.reshape(blocks, x.shape[0] // blocks, x.shape[1]), TO, split_axis=0, concat_axis=0, tiled=True
    )
    return out.reshape(x.shape)


def along_z(x, step):
    at = [(z % SIDE) * SIDE + z // SIDE for z in range(RING)]
    return lax.ppermute(x, ("lo", "hi"), [(at[z], at[(z + step) % RING]) for z in range(RING)])


def shift(x, axis, step):
    return lax.ppermute(x, axis, [(i, (i + step) % SIDE) for i in range(SIDE)])


def gate(m_ref, x_ref):
    x = x_ref[...].astype(F32)
    return (m_ref[...].astype(F32) * (x * jax.nn.sigmoid(x))).astype(BF16)


def grads_kernel(m_ref, x_ref, c_ref, own_ref, other_ref, two_ref, grad_ref, gated, total):
    half = pl.program_id(1)

    @pl.when(half == 0)
    def _():
        gated[...] = gate(m_ref, x_ref)
        total[...] = c_ref[...].astype(F32)

    def add(w_ref):
        up, down = w_ref[0, 0], w_ref[0, 1]
        pre = nt(gated[...], up)
        back = nt(c_ref[...], down)
        square = pre * pre
        t = jnp.tanh(pre * (C0 + (C0 * C1) * square))
        slope = 0.5 + 0.5 * t + (0.5 * pre) * (1.0 - t * t) * (C0 + (3.0 * C0 * C1) * square)
        total[...] += nn((back * slope).astype(BF16), up)

    @pl.when(half == 0)
    def _():
        add(own_ref)

    @pl.when(half == 1)
    def _():
        add(other_ref)
        x = x_ref[...].astype(F32)
        grad_ref[...] = total[...]
        two_ref[...] = (total[...] * (x * jax.nn.sigmoid(x))).astype(BF16)


def outputs_kernel(rows, m_ref, x_ref, own_ref, other_ref, out_ref, gated, total):
    half = pl.program_id(1)

    @pl.when(half == 0)
    def _():
        gated[...] = gate(m_ref, x_ref)
        total[...] = gated[...].astype(F32)

    def add(w_ref):
        up, down = w_ref[0, 0], w_ref[0, 1]
        for at in range(0, gated.shape[0], rows):
            part = pl.ds(at, rows)
            pre = nt(gated[part, :], up)
            t = jnp.tanh(pre * (C0 + (C0 * C1) * (pre * pre)))
            total[part, :] += nn((pre * (0.5 + 0.5 * t)).astype(BF16), down)

    @pl.when(half == 0)
    def _():
        add(own_ref)

    @pl.when(half == 1)
    def _():
        add(other_ref)
        out_ref[...] = total[...].astype(BF16)


def mlp_call(kernel, arrays, weights, out_types, dots):
    tokens, channels = arrays[0].shape
    groups, _, hid, group_ch = weights[0].shape
    cols = pl.BlockSpec((tokens, group_ch), lambda g, h: (0, g))
    whole = pl.BlockSpec((1, 2, hid, group_ch), lambda g, h: (g, 0, 0, 0))
    units = len(weights) * hid
    return pl.pallas_call(
        kernel,
        grid=(groups, len(weights)),
        in_specs=[cols] * len(arrays) + [whole] * len(weights),
        out_specs=[cols] * len(out_types),
        out_shape=[jax.ShapeDtypeStruct((tokens, channels), t) for t in out_types],
        scratch_shapes=[pltpu.VMEM((tokens, group_ch), BF16), pltpu.VMEM((tokens, group_ch), F32)],
        cost_estimate=pl.CostEstimate(
            flops=2 * dots * tokens * channels * units,
            transcendentals=tokens * units * groups,
            bytes_accessed=2 * len(arrays) * tokens * channels + 4 * channels * units,
        ),
    )(*arrays, *weights)


def weight_column(up_weight, down_weight):
    own_hid = up_weight.shape[2]
    rows = own_hid // WEIGHT_SLICES
    own = jnp.stack([jnp.swapaxes(up_weight, 1, 2), down_weight], axis=1)
    place = lax.axis_index("y") * 2 + lax.rem(lax.axis_index("x"), 2)
    piece = lax.dynamic_slice_in_dim(own, place * rows, rows, axis=2)
    column = [along_z(piece, step) for step in (1, -1, 2)]
    return own, jnp.concatenate(column, axis=2)


def weight_pair(column):
    other = lax.ppermute(column, "x", [(i, i ^ 1) for i in range(SIDE)])
    return jnp.concatenate([column, other], axis=2)


def weight_halves(own, pair):
    others = [shift(pair, "y", k) for k in (1, 2, 3)]
    half = jnp.concatenate([own, pair] + others, axis=2)
    return half, lax.ppermute(half, "core", [(0, 1), (1, 0)])


def layer(inputs, cotangent, factor_one, factor_two, up_weight, down_weight):
    block = factor_one.shape[1]
    own_p, blocks, _ = factor_two.shape
    n_dp = SIDE * CORES
    x_nat = inputs[0]

    own, column = weight_column(up_weight, down_weight)
    one = swap(factor_one[0])
    mixed_one = nn(one, x_nat).astype(BF16)
    mixed_one, column = lax.optimization_barrier((mixed_one, column))
    cols_one = exchange(mixed_one, blocks)

    at = lax.broadcasted_iota(jnp.int32, (blocks, block), 1) // own_p
    at = lax.rem(at, SIDE) * SIDE**2 + lax.rem(at // SIDE, SIDE) * SIDE + at // SIDE**2
    pick = (at == lax.broadcasted_iota(jnp.int32, (blocks, block), 0)).astype(BF16)

    def diagonal(full):
        row = lax.broadcasted_iota(jnp.int32, (block, block), 0)
        col = lax.broadcasted_iota(jnp.int32, (block, block), 1)
        return jnp.where(lax.rem(row, own_p) == lax.rem(col, own_p), full, 0.0).astype(BF16)

    by_q = swap(jnp.transpose(factor_two, (1, 0, 2))).reshape(block, blocks)
    two = diagonal(nn(by_q, pick))
    pair = weight_pair(column)
    x_all, cot_all = swap(x_nat), swap(cotangent[0])
    cols_one, _, two, x_all, cot_all = lax.optimization_barrier((cols_one, pair, two, x_all, cot_all))

    weights = weight_halves(own, pair)
    mixed_two = nn(two, cols_one).astype(BF16)
    mixed = exchange(mixed_two, blocks)

    grad_two, grad_gated = mlp_call(grads_kernel, (mixed, x_all, cot_all), weights, (BF16, F32), 3)
    grad_cols = exchange(grad_two, blocks)

    (outputs,) = mlp_call(functools.partial(outputs_kernel, 256), (mixed, x_all), weights, (BF16,), 2)
    outputs = swap(outputs)[None]
    gate_in = swap(jax.vjp(jax.nn.silu, x_all.astype(F32))[1](grad_gated * mixed.astype(F32))[0])
    grad_cols, outputs, gate_in = lax.optimization_barrier((grad_cols, outputs, gate_in))

    grad_one = exchange(tn(two, grad_cols).astype(BF16), blocks)

    term_two = nt(diagonal(nt(grad_cols, cols_one)), pick).astype(BF16)
    term_two = swap(term_two.reshape(blocks, own_p * blocks)).reshape(n_dp, -1, block)
    grad_one, term_two = lax.optimization_barrier((grad_one, term_two))

    term_one = swap(nt(grad_one, x_nat).astype(BF16)).reshape(n_dp, block // n_dp, block)
    summed = lax.all_to_all(
        jnp.concatenate([term_one, term_two], axis=1), ("lo", "core"), split_axis=0, concat_axis=0, tiled=True
    )
    summed = jnp.sum(summed.astype(F32), axis=0)
    grad_first = summed[: block // n_dp][None]
    grad_second = jnp.transpose(summed[block // n_dp :].reshape(blocks // n_dp, own_p, blocks), (1, 0, 2))

    grad_inputs = (gate_in + tn(one, grad_one)).astype(BF16)[None]
    return outputs, grad_inputs, grad_first, grad_second


def solution(mesh):
    grid = Mesh(mesh.devices.reshape(SIDE, CORES, SIDE, SIDE, SIDE), ("lo", "core", "y", "hi", "x"))
    dp, seq = ("lo", "core"), ("y", "hi", "x")
    in_specs = (P(dp, seq, None), P(dp, seq, None), P(seq, None, None), P(seq, None, None), P(None, None, dp), P(None, dp, None))
    out_specs = (P(dp, seq, None), P(dp, seq, None), P(seq, dp, None), P(seq, dp, None))
    return jax.shard_map(layer, mesh=grid, in_specs=in_specs, out_specs=out_specs, check_vma=False)
```

time: 305 us -> 274 us (0.90)
  waiting for transfers between devices: 64.8 us -> 145 us
  starting transfers between devices: 123 us -> 78 us
  matrix products: 48.2 us -> 10.7 us
  local copies, waits for them, and re-layouts: 52.3 us -> 16.2 us
  Pallas kernels: 0 us -> 18.2 us
  other arithmetic: 14.2 us -> 3.73 us
    all_to_all x4, waiting for transfers between devices: 18.5 us -> 104 us  [exchange(): lax.all_to_all(x.reshape(blocks, x.shape[0] // blocks, x.shape[1]), TO, s...]
    all_to_all x1, starting transfers between devices: 34.4 us -> 4.67 us  [layer(): lax.all_to_all(jnp.concatenate([term_one, term_two], axis=1), ('lo', 'cor...]
    dot_general x11 -> x3, matrix products: 31.5 us -> 3.28 us  [nn(): lax.dot_general(a, b, (((1,), (0,)), ((), ())), preferred_element_type=F32)]
    another operation x3 -> x1, local copies, waits for them, and re-layouts: 20.5 us -> 0.02 us  [layer(): swap(term_two.reshape(blocks, own_p * blocks)).reshape(n_dp, -1, block)]
    all_to_all x4, starting transfers between devices: 61.1 us -> 41.9 us  [exchange(): lax.all_to_all(x.reshape(blocks, x.shape[0] // blocks, x.shape[1]), TO, s...]
    pallas_call x0 -> x2, Pallas kernels: none -> 18.2 us  [mlp_call(): pl.pallas_call(kernel, grid=(groups, len(weights)), in_specs=[cols] * len...]
    ppermute x2 -> x5, starting transfers between devices: 7.38 us -> 22.1 us  [the longest x3 15.8 us: along_z(): lax.ppermute(x, ('lo', 'hi'), [(at[z], at[(z + step) % RING]) for z in ra...]
    mul x1 -> x0, local copies, waits for them, and re-layouts: 13.6 us -> none  [shards(): two = (two[:, :, :, None] * eye[None, :, None, :]).reshape(block, block)]
  transfers between devices with their start and end apart: 13 -> 13, of which waited for: 7 -> 10; matrix products, arithmetic and copies ran while one was open for 24% -> 7% of each run, Pallas kernels for 0% -> 3%
where the time goes in v1:
time: 274 us; the launch traced here: 273 us
  waiting for transfers between devices  145 us (53%)
  starting transfers between devices  78 us (28%)
  Pallas kernels  18.2 us (7%)
  local copies, waits for them, and re-layouts  16.2 us (6%)
  matrix products  10.7 us (4%)
  other arithmetic  3.73 us (1%)
    all_to_all x4, waiting for transfers between devices, exchange(): lax.all_to_all(x.reshape(blocks, x.shape[0] // blocks, x.shape[1]), TO, s...  104 us
    all_to_all x4, starting transfers between devices, exchange(): lax.all_to_all(x.reshape(blocks, x.shape[0] // blocks, x.shape[1]), TO, s...  41.9 us
    ppermute x3, waiting for transfers between devices, shift(): return lax.ppermute(x, axis, [(i, (i + step) % SIDE) for i in range(SIDE)])  18.5 us
    pallas_call x2, Pallas kernels, mlp_call(): pl.pallas_call(kernel, grid=(groups, len(weights)), in_specs=[cols] * len...  18.2 us
    ppermute x3, starting transfers between devices, along_z(): lax.ppermute(x, ('lo', 'hi'), [(at[z], at[(z + step) % RING]) for z in ra...  15.8 us
    all_to_all x1, waiting for transfers between devices, layer(): lax.all_to_all(jnp.concatenate([term_one, term_two], axis=1), ('lo', 'cor...  12.4 us
    ppermute x3, starting transfers between devices, shift(): return lax.ppermute(x, axis, [(i, (i + step) % SIDE) for i in range(SIDE)])  9.3 us
    unnamed x36, local copies, waits for them, and re-layouts  8.3 us
  transfers between devices with their start and end apart: 13, of which 10 were waited for; matrix products, arithmetic and copies ran while one was open for 7% of the time, Pallas kernels for 3%

profile of v1, /device:TPU:1, one launch (start us, length us, event | category | flops | bytes accessed | tf_op | source)
XLA Modules:
  0.0 272.5 jit_solution(17813009381794506261)
XLA Ops:
  0.7 0.9 fusion.32
  1.5 5.7 %collective-permute-start.2 = (bf16[2,2,24,384]{3,2,1,0:T(8,128)(2,1)S(1)}, bf16[2,2,24,384]{3,2,1,0:T(8,128)(2,1)S(1)}, u32[]{:S(2)}, u32[]{:S(2)}) collective-permute-start(bf16[2,2,24,384]{3,2,1,0:T(8,128)(2,1)S(1)} %fusion.32), channel_id=1, source_target_pairs={{0,256},{128,384},{256,4},{384,132},{4,260},{132,388},{260,8},{388... | collective-permute-start | bytes 221192 | tf_op jit(solution)/shard_map/ppermute | solution.py:51
  7.2 8.1 %collective-permute-start.1 = (bf16[2,2,24,384]{3,2,1,0:T(8,128)(2,1)S(1)}, bf16[2,2,24,384]{3,2,1,0:T(8,128)(2,1)S(1)}, u32[]{:S(2)}, u32[]{:S(2)}) collective-permute-start(bf16[2,2,24,384]{3,2,1,0:T(8,128)(2,1)S(1)} %fusion.32), channel_id=1, source_target_pairs={{0,396},{128,0},{256,128},{384,256},{4,384},{132,4},{260,132},{388... | collective-permute-start | bytes 221192 | tf_op jit(solution)/shard_map/ppermute | solution.py:51
  15.4 1.9 collective-permute-start
  17.3 1.1 copy.26
  18.4 0.8 copy-done.4
  19.2 1.5 convolution_convert_fusion.2
  20.7 1.0 collective-permute-done
  21.7 15.0 %all-to-all-start = ((bf16[64,8,768]{2,1,0:T(8,128)(2,1)}), bf16[64,8,768]{2,1,0:T(8,128)(2,1)S(1)}, u32[]{:S(2)}, u32[]{:S(2)}) async-start(bf16[64,8,768]{2,1,0:T(8,128)(2,1)} %bitcast.103), calls=%async_computation | async-start | bytes 1572864 | tf_op jit(solution)/shard_map/all_to_all | solution.py:43
  36.8 1.0 copy.28
  37.8 1.0 copy.29
  39.2 2.9 %collective-permute-start.3 = (bf16[2,2,72,384]{3,2,1,0:T(8,128)(2,1)S(1)}, bf16[2,2,72,384]{3,2,1,0:T(8,128)(2,1)S(1)}, u32[]{:S(2)}, u32[]{:S(2)}) collective-permute-start(bf16[2,2,72,384]{3,2,1,0:T(8,128)(2,1)S(1)} %pad_maximum_fusion.2), channel_id=1, source_target_pairs={{0,1},{1,0},{2,3},{3,2},{4,5},{5,4},{6,7},{7,6},{8,9},{9,8},{10,11... | collective-permute-start | bytes 663560 | tf_op jit(solution)/shard_map/ppermute | solution.py:150
  42.2 0.8 constant_dynamic-update-slice_fusion.6
  43.0 4.7 %collective-permute-done.3 = bf16[2,2,72,384]{3,2,1,0:T(8,128)(2,1)S(1)} collective-permute-done((bf16[2,2,72,384]{3,2,1,0:T(8,128)(2,1)S(1)}, bf16[2,2,72,384]{3,2,1,0:T(8,128)(2,1)S(1)}, u32[]{:S(2)}, u32[]{:S(2)}) %collective-permute-start.3) | collective-permute-done | bytes 221216 | tf_op jit(solution)/shard_map/ppermute | solution.py:150
  47.7 0.8 constant_dynamic-update-slice_fusion.5
  48.4 1.4 copy-done.12
  49.9 2.1 collective-permute-start.4
  52.0 25.4 %all-to-all-done = bf16[64,8,768]{2,1,0:T(8,128)(2,1)S(1)} async-done(((bf16[64,8,768]{2,1,0:T(8,128)(2,1)}), bf16[64,8,768]{2,1,0:T(8,128)(2,1)S(1)}, u32[]{:S(2)}, u32[]{:S(2)}) %all-to-all-start) | async-done | bytes 786464 | tf_op jit(solution)/shard_map/all_to_all | solution.py:43
  77.4 1.5 fusion.8
  78.9 11.0 %all-to-all-start.1 = ((bf16[64,8,768]{2,1,0:T(8,128)(2,1)}), bf16[64,8,768]{2,1,0:T(8,128)(2,1)S(1)}, u32[]{:S(2)}, u32[]{:S(2)}) async-start(bf16[64,8,768]{2,1,0:T(8,128)(2,1)} %fusion.8), calls=%async_computation.1 | async-start | bytes 1572864 | tf_op jit(solution)/shard_map/all_to_all | solution.py:43
  89.9 4.4 %collective-permute-start.5 = (bf16[2,2,144,384]{3,2,1,0:T(8,128)(2,1)}, bf16[2,2,144,384]{3,2,1,0:T(8,128)(2,1)S(1)}, u32[]{:S(2)}, u32[]{:S(2)}) collective-permute-start(bf16[2,2,144,384]{3,2,1,0:T(8,128)(2,1)} %get-tuple-element.43), channel_id=1, source_target_pairs={{0,32},{16,48},{32,0},{48,16},{1,33},{17,49},{33,1},{49,17},{2,34}... | collective-permute-start | bytes 1327112 | tf_op jit(solution)/shard_map/ppermute | solution.py:55
  94.3 2.8 %collective-permute-start.6 = (bf16[2,2,144,384]{3,2,1,0:T(8,128)(2,1)}, bf16[2,2,144,384]{3,2,1,0:T(8,128)(2,1)S(1)}, u32[]{:S(2)}, u32[]{:S(2)}) collective-permute-start(bf16[2,2,144,384]{3,2,1,0:T(8,128)(2,1)} %get-tuple-element.43), channel_id=1, source_target_pairs={{0,48},{16,0},{32,16},{48,32},{1,49},{17,1},{33,17},{49,33},{2,50}... | collective-permute-start | bytes 1327112 | tf_op jit(solution)/shard_map/ppermute | solution.py:55
  97.1 0.8 constant_dynamic-update-slice_fusion.4
  98.0 8.7 %collective-permute-done.5 = bf16[2,2,144,384]{3,2,1,0:T(8,128)(2,1)S(1)} collective-permute-done((bf16[2,2,144,384]{3,2,1,0:T(8,128)(2,1)}, bf16[2,2,144,384]{3,2,1,0:T(8,128)(2,1)S(1)}, u32[]{:S(2)}, u32[]{:S(2)}) %collective-permute-start.5) | collective-permute-done | bytes 442400 | tf_op jit(solution)/shard_map/ppermute | solution.py:55
  106.7 0.8 constant_dynamic-update-slice_fusion.3
  107.5 9.8 %collective-permute-done.6 = bf16[2,2,144,384]{3,2,1,0:T(8,128)(2,1)S(1)} collective-permute-done((bf16[2,2,144,384]{3,2,1,0:T(8,128)(2,1)}, bf16[2,2,144,384]{3,2,1,0:T(8,128)(2,1)S(1)}, u32[]{:S(2)}, u32[]{:S(2)}) %collective-permute-start.6) | collective-permute-done | bytes 442400 | tf_op jit(solution)/shard_map/ppermute | solution.py:55
  117.3 0.8 constant_dynamic-update-slice_fusion.2.own_ref
  118.1 3.4 %collective-permute-start.7 = (bf16[2,2,768,384]{3,2,1,0:T(8,128)(2,1)}, bf16[2,2,768,384]{3,2,1,0:T(8,128)(2,1)}, u32[]{:S(2)}, u32[]{:S(2)}) collective-permute-start(bf16[2,2,768,384]{3,2,1,0:T(8,128)(2,1)} %constant_dynamic-update-slice_fusion.2.own_ref), channel_id=1, source_target_pairs={{0,64},{64,0},{1,65},{65,1},{2,66},{66,2},{3,67},{67,3},{4,68},{68... | collective-permute-start | bytes 7077896 | tf_op jit(solution)/shard_map/ppermute | solution.py:157
  121.5 4.5 %collective-permute-done.7.other_ref = bf16[2,2,768,384]{3,2,1,0:T(8,128)(2,1)} collective-permute-done((bf16[2,2,768,384]{3,2,1,0:T(8,128)(2,1)}, bf16[2,2,768,384]{3,2,1,0:T(8,128)(2,1)}, u32[]{:S(2)}, u32[]{:S(2)}) %collective-permute-start.7) | collective-permute-done | bytes 2359328 | tf_op jit(solution)/shard_map/ppermute | solution.py:157
  126.0 7.8 %all-to-all-done.1 = bf16[64,8,768]{2,1,0:T(8,128)(2,1)S(1)} async-done(((bf16[64,8,768]{2,1,0:T(8,128)(2,1)}), bf16[64,8,768]{2,1,0:T(8,128)(2,1)S(1)}, u32[]{:S(2)}, u32[]{:S(2)}) %all-to-all-start.1) | async-done | bytes 786464 | tf_op jit(solution)/shard_map/all_to_all | solution.py:43
  133.8 0.9 copy-done.1
  134.6 10.1 %shard_map.93 = (bf16[512,768]{1,0:T(8,128)(2,1)}, f32[512,768]{1,0:T(8,128)}) custom-call(bf16[512,768]{1,0:T(8,128)(2,1)} %bitcast.86, bf16[512,768]{1,0:T(8,128)(2,1)} %bitcast.83, bf16[512,768]{1,0:T(8,128)(2,1)} %bitcast.101, bf16[2,2,768,384]{3,2,1,0:T(8,128)(2,1)} %constant_dynamic-update-slice_fusion.2.own_ref, ...), custom_call_target="tpu_custom_call" | custom-call | flops 3623878656 | bytes 7077888 | tf_op jit(solution)/shard_map/pallas_call | solution.py:124
  144.7 10.7 %all-to-all-start.2 = ((bf16[64,8,768]{2,1,0:T(8,128)(2,1)}), bf16[64,8,768]{2,1,0:T(8,128)(2,1)S(1)}, u32[]{:S(2)}, u32[]{:S(2)}) async-start(bf16[64,8,768]{2,1,0:T(8,128)(2,1)} %bitcast.106), calls=%async_computation.2 | async-start | bytes 1572864 | tf_op jit(solution)/shard_map/all_to_all | solution.py:43
  155.5 8.1 %shard_map.94 = bf16[512,768]{1,0:T(8,128)(2,1)} custom-call(bf16[512,768]{1,0:T(8,128)(2,1)} %bitcast.87, bf16[512,768]{1,0:T(8,128)(2,1)} %bitcast.84, bf16[2,2,768,384]{3,2,1,0:T(8,128)(2,1)} %constant_dynamic-update-slice_fusion.2.own_ref, bf16[2,2,768,384]{3,2,1,0:T(8,128)(2,1)} %collective-permute-done.7.other_ref), custom_call_target="tpu_custom_call" | custom-call | flops 2415919104 | bytes 6291456 | tf_op jit(solution)/shard_map/pallas_call | solution.py:124
  163.6 2.2 copy.30
  165.8 0.7 fusion.4
  166.6 32.4 %all-to-all-done.2 = bf16[64,8,768]{2,1,0:T(8,128)(2,1)S(1)} async-done(((bf16[64,8,768]{2,1,0:T(8,128)(2,1)}), bf16[64,8,768]{2,1,0:T(8,128)(2,1)S(1)}, u32[]{:S(2)}, u32[]{:S(2)}) %all-to-all-start.2) | async-done | bytes 786464 | tf_op jit(solution)/shard_map/all_to_all | solution.py:43
  199.0 2.8 %fusion.9 = bf16[64,8,768]{2,1,0:T(8,128)(2,1)} fusion(bf16[512,512]{0,1:T(8,128)(2,1)} %copy-done.14, bf16[512,768]{1,0:T(8,128)(2,1)S(1)} %bitcast.104), kind=kOutput, calls=%fused_computation.18 | convolution fusion | flops 403046400 | bytes 2097152 | tf_op jit(solution)/shard_map/dot_general | solution.py:32
  201.8 5.2 %all-to-all-start.3 = ((bf16[64,8,768]{2,1,0:T(8,128)(2,1)}), bf16[64,8,768]{2,1,0:T(8,128)(2,1)S(1)}, u32[]{:S(2)}, u32[]{:S(2)}) async-start(bf16[64,8,768]{2,1,0:T(8,128)(2,1)} %fusion.9), calls=%async_computation.3 | async-start | bytes 1572864 | tf_op jit(solution)/shard_map/all_to_all | solution.py:43
  207.1 2.1 fusion.13
  209.5 38.1 %all-to-all-done.3 = bf16[64,8,768]{2,1,0:T(8,128)(2,1)S(1)} async-done(((bf16[64,8,768]{2,1,0:T(8,128)(2,1)}), bf16[64,8,768]{2,1,0:T(8,128)(2,1)S(1)}, u32[]{:S(2)}, u32[]{:S(2)}) %all-to-all-start.3) | async-done | bytes 786464 | tf_op jit(solution)/shard_map/all_to_all | solution.py:43
  248.5 0.9 pad_maximum_fusion.1
  249.4 4.7 %all-to-all-start.4 = ((bf16[8,72,512]{2,1,0:T(8,128)(2,1)}), bf16[8,72,512]{2,1,0:T(8,128)(2,1)}, u32[]{:S(2)}, u32[]{:S(2)}) async-start(bf16[8,72,512]{2,1,0:T(8,128)(2,1)} %pad_maximum_fusion.1), calls=%async_computation.4 | async-start | bytes 1179648 | tf_op jit(solution)/shard_map/all_to_all | solution.py:206
  254.5 1.9 fusion.10
  256.4 1.2 copy.37
  257.6 12.4 %all-to-all-done.4 = bf16[8,72,512]{2,1,0:T(8,128)(2,1)} async-done(((bf16[8,72,512]{2,1,0:T(8,128)(2,1)}), bf16[8,72,512]{2,1,0:T(8,128)(2,1)}, u32[]{:S(2)}, u32[]{:S(2)}) %all-to-all-start.4) | async-done | bytes 589856 | tf_op jit(solution)/shard_map/all_to_all | solution.py:206
  270.0 1.2 convert_reduce_fusion
  271.1 0.7 slice_bitcast_fusion
  (48 shorter events, 3.1 us)
Async XLA Ops:
  0.6 18.6 %copy-start.9 = (bf16[1,512,768]{2,1,0:T(8,128)(2,1)S(1)}, bf16[1,512,768]{2,1,0:T(8,128)(2,1)}, u32[]{:S(2)}) copy-start(bf16[1,512,768]{2,1,0:T(8,128)(2,1)} %param.6) | copy-start | bytes 2359300
  1.5 19.1 %collective-permute-start.2 = (bf16[2,2,24,384]{3,2,1,0:T(8,128)(2,1)S(1)}, bf16[2,2,24,384]{3,2,1,0:T(8,128)(2,1)S(1)}, u32[]{:S(2)}, u32[]{:S(2)}) collective-permute-start(bf16[2,2,24,384]{3,2,1,0:T(8,128)(2,1)S(1)} %fusion.32), channel_id=1, source_target_pairs={{0,256},{128,384},{256,4},{384,132},{4,260},{132,388},{260,8},{388... | collective-permute-start | bytes 221192 | tf_op jit(solution)/shard_map/ppermute | solution.py:51
  7.2 13.4 %collective-permute-start.1 = (bf16[2,2,24,384]{3,2,1,0:T(8,128)(2,1)S(1)}, bf16[2,2,24,384]{3,2,1,0:T(8,128)(2,1)S(1)}, u32[]{:S(2)}, u32[]{:S(2)}) collective-permute-start(bf16[2,2,24,384]{3,2,1,0:T(8,128)(2,1)S(1)} %fusion.32), channel_id=1, source_target_pairs={{0,396},{128,0},{256,128},{384,256},{4,384},{132,4},{260,132},{388... | collective-permute-start | bytes 221192 | tf_op jit(solution)/shard_map/ppermute | solution.py:51
  15.4 6.3 %collective-permute-start = (bf16[2,2,24,384]{3,2,1,0:T(8,128)(2,1)S(1)}, bf16[2,2,24,384]{3,2,1,0:T(8,128)(2,1)S(1)}, u32[]{:S(2)}, u32[]{:S(2)}) collective-permute-start(bf16[2,2,24,384]{3,2,1,0:T(8,128)(2,1)S(1)} %fusion.32), channel_id=1, source_target_pairs={{0,128},{128,256},{256,384},{384,4},{4,132},{132,260},{260,388},{3... | collective-permute-start | bytes 221192 | tf_op jit(solution)/shard_map/ppermute | solution.py:51
  18.4 0.8 copy-start.4
  19.2 17.5 %copy-start.13 = (bf16[8,64,64]{2,1,0:T(8,128)(2,1)S(1)}, bf16[8,64,64]{2,1,0:T(8,128)(2,1)}, u32[]{:S(2)}) copy-start(bf16[8,64,64]{2,1,0:T(8,128)(2,1)} %param.9) | copy-start | bytes 196612
  21.7 16.1 %copy-start.8 = (bf16[1,512,768]{2,1,0:T(8,128)(2,1)S(1)}, bf16[1,512,768]{2,1,0:T(8,128)(2,1)}, u32[]{:S(2)}) copy-start(bf16[1,512,768]{2,1,0:T(8,128)(2,1)} %param.7) | copy-start | bytes 2359300
  21.7 55.6 %all-to-all-start = ((bf16[64,8,768]{2,1,0:T(8,128)(2,1)}), bf16[64,8,768]{2,1,0:T(8,128)(2,1)S(1)}, u32[]{:S(2)}, u32[]{:S(2)}) async-start(bf16[64,8,768]{2,1,0:T(8,128)(2,1)} %bitcast.103), calls=%async_computation | async-start | bytes 1572864 | tf_op jit(solution)/shard_map/all_to_all | solution.py:43
  38.8 3.3 %copy-start.6 = (bf16[2,192,384]{2,1,0:T(8,128)(2,1)S(1)}, bf16[2,192,384]{2,1,0:T(8,128)(2,1)}, u32[]{:S(2)}) copy-start(bf16[2,192,384]{2,1,0:T(8,128)(2,1)} %param.11) | copy-start | bytes 884740
  38.8 3.4 %copy-start.7 = (bf16[2,384,192]{1,2,0:T(8,128)(2,1)S(1)}, bf16[2,384,192]{1,2,0:T(8,128)(2,1)}, u32[]{:S(2)}) copy-start(bf16[2,384,192]{1,2,0:T(8,128)(2,1)} %param.10) | copy-start | bytes 884740
  39.2 39.7 %copy-start.14 = (bf16[512,512]{0,1:T(8,128)(2,1)}, bf16[512,512]{0,1:T(8,128)(2,1)S(1)}, u32[]{:S(2)}) copy-start(bf16[512,512]{0,1:T(8,128)(2,1)S(1)} %fusion.11) | copy-start | bytes 1572868
  39.2 8.5 %collective-permute-start.3 = (bf16[2,2,72,384]{3,2,1,0:T(8,128)(2,1)S(1)}, bf16[2,2,72,384]{3,2,1,0:T(8,128)(2,1)S(1)}, u32[]{:S(2)}, u32[]{:S(2)}) collective-permute-start(bf16[2,2,72,384]{3,2,1,0:T(8,128)(2,1)S(1)} %pad_maximum_fusion.2), channel_id=1, source_target_pairs={{0,1},{1,0},{2,3},{3,2},{4,5},{5,4},{6,7},{7,6},{8,9},{9,8},{10,11... | collective-permute-start | bytes 663560 | tf_op jit(solution)/shard_map/ppermute | solution.py:150
  48.4 1.4 copy-start.12
  49.9 47.3 %collective-permute-start.4 = (bf16[2,2,144,384]{3,2,1,0:T(8,128)(2,1)}, bf16[2,2,144,384]{3,2,1,0:T(8,128)(2,1)S(1)}, u32[]{:S(2)}, u32[]{:S(2)}) collective-permute-start(bf16[2,2,144,384]{3,2,1,0:T(8,128)(2,1)} %get-tuple-element.43), channel_id=1, source_target_pairs={{0,16},{16,32},{32,48},{48,0},{1,17},{17,33},{33,49},{49,1},{2,18}... | collective-permute-start | bytes 1327112 | tf_op jit(solution)/shard_map/ppermute | solution.py:55
  77.4 67.3 %copy-start.10 = (bf16[64,8,768]{2,1,0:T(8,128)(2,1)}, bf16[64,8,768]{2,1,0:T(8,128)(2,1)S(1)}, u32[]{:S(2)}) copy-start(bf16[64,8,768]{2,1,0:T(8,128)(2,1)S(1)} %all-to-all-done) | copy-start | bytes 2359300
  78.9 54.9 %all-to-all-start.1 = ((bf16[64,8,768]{2,1,0:T(8,128)(2,1)}), bf16[64,8,768]{2,1,0:T(8,128)(2,1)S(1)}, u32[]{:S(2)}, u32[]{:S(2)}) async-start(bf16[64,8,768]{2,1,0:T(8,128)(2,1)} %fusion.8), calls=%async_computation.1 | async-start | bytes 1572864 | tf_op jit(solution)/shard_map/all_to_all | solution.py:43
  89.9 16.8 %collective-permute-start.5 = (bf16[2,2,144,384]{3,2,1,0:T(8,128)(2,1)}, bf16[2,2,144,384]{3,2,1,0:T(8,128)(2,1)S(1)}, u32[]{:S(2)}, u32[]{:S(2)}) collective-permute-start(bf16[2,2,144,384]{3,2,1,0:T(8,128)(2,1)} %get-tuple-element.43), channel_id=1, source_target_pairs={{0,32},{16,48},{32,0},{48,16},{1,33},{17,49},{33,1},{49,17},{2,34}... | collective-permute-start | bytes 1327112 | tf_op jit(solution)/shard_map/ppermute | solution.py:55
  94.3 22.9 %collective-permute-start.6 = (bf16[2,2,144,384]{3,2,1,0:T(8,128)(2,1)}, bf16[2,2,144,384]{3,2,1,0:T(8,128)(2,1)S(1)}, u32[]{:S(2)}, u32[]{:S(2)}) collective-permute-start(bf16[2,2,144,384]{3,2,1,0:T(8,128)(2,1)} %get-tuple-element.43), channel_id=1, source_target_pairs={{0,48},{16,0},{32,16},{48,32},{1,49},{17,1},{33,17},{49,33},{2,50}... | collective-permute-start | bytes 1327112 | tf_op jit(solution)/shard_map/ppermute | solution.py:55
  118.1 7.9 %collective-permute-start.7 = (bf16[2,2,768,384]{3,2,1,0:T(8,128)(2,1)}, bf16[2,2,768,384]{3,2,1,0:T(8,128)(2,1)}, u32[]{:S(2)}, u32[]{:S(2)}) collective-permute-start(bf16[2,2,768,384]{3,2,1,0:T(8,128)(2,1)} %constant_dynamic-update-slice_fusion.2.own_ref), channel_id=1, source_target_pairs={{0,64},{64,0},{1,65},{65,1},{2,66},{66,2},{3,67},{67,3},{4,68},{68... | collective-permute-start | bytes 7077896 | tf_op jit(solution)/shard_map/ppermute | solution.py:157
  133.8 0.9 copy-start.1
  144.7 54.3 %all-to-all-start.2 = ((bf16[64,8,768]{2,1,0:T(8,128)(2,1)}), bf16[64,8,768]{2,1,0:T(8,128)(2,1)S(1)}, u32[]{:S(2)}, u32[]{:S(2)}) async-start(bf16[64,8,768]{2,1,0:T(8,128)(2,1)} %bitcast.106), calls=%async_computation.2 | async-start | bytes 1572864 | tf_op jit(solution)/shard_map/all_to_all | solution.py:43
  155.5 10.3 %copy-start.5 = (f32[512,768]{1,0:T(8,128)S(1)}, f32[512,768]{1,0:T(8,128)}, u32[]{:S(2)}) copy-start(f32[512,768]{1,0:T(8,128)} %get-tuple-element.24) | copy-start | bytes 4718596
  163.6 2.2 copy-start
  163.6 2.2 copy-start.2
  199.0 2.8 %copy-start.11 = (bf16[64,8,768]{2,1,0:T(8,128)(2,1)}, bf16[64,8,768]{2,1,0:T(8,128)(2,1)S(1)}, u32[]{:S(2)}) copy-start(bf16[64,8,768]{2,1,0:T(8,128)(2,1)S(1)} %all-to-all-done.2) | copy-start | bytes 2359300
  201.8 45.8 %all-to-all-start.3 = ((bf16[64,8,768]{2,1,0:T(8,128)(2,1)}), bf16[64,8,768]{2,1,0:T(8,128)(2,1)S(1)}, u32[]{:S(2)}, u32[]{:S(2)}) async-start(bf16[64,8,768]{2,1,0:T(8,128)(2,1)} %fusion.9), calls=%async_computation.3 | async-start | bytes 1572864 | tf_op jit(solution)/shard_map/all_to_all | solution.py:43
  247.6 0.9 copy-start.3
  249.4 20.6 %all-to-all-start.4 = ((bf16[8,72,512]{2,1,0:T(8,128)(2,1)}), bf16[8,72,512]{2,1,0:T(8,128)(2,1)}, u32[]{:S(2)}, u32[]{:S(2)}) async-start(bf16[8,72,512]{2,1,0:T(8,128)(2,1)} %pad_maximum_fusion.1), calls=%async_computation.4 | async-start | bytes 1179648 | tf_op jit(solution)/shard_map/all_to_all | solution.py:206

commit v2 on v1

--- a/solution.py
+++ b/solution.py
@@ -13,7 +13,6 @@
 BF16 = jnp.bfloat16
 SIDE = 4
 CORES = 2
-RING = SIDE * SIDE
 TO = ("x", "hi", "y")
 WEIGHT_SLICES = 8
 C0 = 0.7978845608028654
@@ -46,11 +45,6 @@
     return out.reshape(x.shape)
 
 
-def along_z(x, step):
-    at = [(z % SIDE) * SIDE + z // SIDE for z in range(RING)]
-    return lax.ppermute(x, ("lo", "hi"), [(at[z], at[(z + step) % RING]) for z in range(RING)])
-
-
 def shift(x, axis, step):
     return lax.ppermute(x, axis, [(i, (i + step) % SIDE) for i in range(SIDE)])
 
@@ -69,7 +63,7 @@
         total[...] = c_ref[...].astype(F32)
 
     def add(w_ref):
-        up, down = w_ref[0, 0], w_ref[0, 1]
+        up, down = w_ref[0, 0], w_ref[1, 0]
         pre = nt(gated[...], up)
         back = nt(c_ref[...], down)
         square = pre * pre
@@ -98,7 +92,7 @@
         total[...] = gated[...].astype(F32)
 
     def add(w_ref):
-        up, down = w_ref[0, 0], w_ref[0, 1]
+        up, down = w_ref[0, 0], w_ref[1, 0]
         for at in range(0, gated.shape[0], rows):
             part = pl.ds(at, rows)
             pre = nt(gated[part, :], up)
@@ -117,9 +111,9 @@
 
 def mlp_call(kernel, arrays, weights, out_types, dots):
     tokens, channels = arrays[0].shape
-    groups, _, hid, group_ch = weights[0].shape
+    _, groups, hid, group_ch = weights[0].shape
     cols = pl.BlockSpec((tokens, group_ch), lambda g, h: (0, g))
-    whole = pl.BlockSpec((1, 2, hid, group_ch), lambda g, h: (g, 0, 0, 0))
+    whole = pl.BlockSpec((2, 1, hid, group_ch), lambda g, h: (0, g, 0, 0))
     units = len(weights) * hid
     return pl.pallas_call(
         kernel,
@@ -137,24 +131,74 @@
 
 
 def weight_column(up_weight, down_weight):
-    own_hid = up_weight.shape[2]
-    rows = own_hid // WEIGHT_SLICES
-    own = jnp.stack([jnp.swapaxes(up_weight, 1, 2), down_weight], axis=1)
-    place = lax.axis_index("y") * 2 + lax.rem(lax.axis_index("x"), 2)
-    piece = lax.dynamic_slice_in_dim(own, place * rows, rows, axis=2)
-    column = [along_z(piece, step) for step in (1, -1, 2)]
-    return own, jnp.concatenate(column, axis=2)
-
-
-def weight_pair(column):
-    other = lax.ppermute(column, "x", [(i, i ^ 1) for i in range(SIDE)])
-    return jnp.concatenate([column, other], axis=2)
-
-
-def weight_halves(own, pair):
-    others = [shift(pair, "y", k) for k in (1, 2, 3)]
-    half = jnp.concatenate([own, pair] + others, axis=2)
+    slabs = jnp.stack([jnp.swapaxes(up_weight, 1, 2), down_weight])
+    slabs = slabs.reshape(slabs.shape[:2] + (WEIGHT_SLICES, -1, slabs.shape[-1]))
+    y, x = lax.axis_index("y"), lax.axis_index("x")
+    place = (y * 2 + lax.rem(x, 2), x * 2 + lax.rem(y, 2))
+    piece = jnp.stack([lax.dynamic_index_in_dim(slabs[i], place[i], axis=1, keepdims=False) for i in (0, 1)])
+    column = lax.all_to_all(
+        jnp.broadcast_to(piece[None], (SIDE, *piece.shape)), "lo", split_axis=0, concat_axis=0, tiled=True
+    )
+    return slabs, column
+
+
+def assemble_kernel(at_ref, slabs_ref, *refs):
+    out_ref = refs[-1]
+    own = slabs_ref.shape[2]
+    out_ref[:, :, :own] = slabs_ref[...]
+    for i, pieces in ((0, refs[:SIDE]), (1, refs[SIDE : 2 * SIDE])):
+        along, across = at_ref[i], lax.rem(at_ref[1 - i], 2)
+        for step, piece_ref in enumerate(pieces):
+            source = lax.rem(along + SIDE - step, SIDE)
+            twin = source + 1 - 2 * lax.rem(source, 2)
+            first, second = own + 3 * (source * 2 + across), own + 3 * (twin * 2 + 1 - across)
+            out_ref[i, :, pl.ds(first, 3)] = piece_ref[0]
+            out_ref[i, :, pl.ds(second, 3)] = piece_ref[1]
+
+
+def weight_pairs(column):
+    lo = lax.axis_index("lo")
+    others = lax.dynamic_slice_in_dim(jnp.concatenate([column, column]), lo + 1, SIDE - 1, axis=0)
+    others = jnp.moveaxis(others, 0, 2)
+    diagonal = [((y * SIDE + x), ((y ^ 1) * SIDE + (x ^ 1))) for y in range(SIDE) for x in range(SIDE)]
+    twin = lax.ppermute(others, ("y", "x"), diagonal)
+    return jnp.stack([others, twin], axis=1)
+
+
+def weight_halves(slabs, pairs):
+    ups = [pairs[0]] + [shift(pairs[0], "y", k) for k in (1, 2, 3)]
+    downs = [pairs[1]] + [shift(pairs[1], "x", k) for k in (1, 2, 3)]
+    at = jnp.stack([lax.axis_index("y"), lax.axis_index("x")]).astype(jnp.int32)
+    _, groups, own, rows, group_ch = slabs.shape
+    half = pl.pallas_call(
+        assemble_kernel,
+        in_specs=[pl.BlockSpec(memory_space=pltpu.SMEM)] + [pl.BlockSpec(memory_space=pltpu.VMEM)] * 9,
+        out_specs=pl.BlockSpec(memory_space=pltpu.VMEM),
+        out_shape=jax.ShapeDtypeStruct((2, groups, 4 * own, rows, group_ch), BF16),
+        cost_estimate=pl.CostEstimate(flops=0, transcendentals=0, bytes_accessed=16 * slabs.size),
+        name="assemble",
+    )(at, slabs, *ups, *downs)
+    half = half.reshape(2, groups, 4 * own * rows, group_ch)
     return half, lax.ppermute(half, "core", [(0, 1), (1, 0)])
+
+
+def mix_kernel(two_ref, x_ref, out_ref):
+    out_ref[...] = nn(two_ref[...], x_ref[...]).astype(BF16)
+
+
+def mix(two, x):
+    rows, channels = x.shape
+    cols = pl.BlockSpec((rows, channels // 2), lambda i: (0, i))
+    return pl.pallas_call(
+        mix_kernel,
+        grid=(2,),
+        in_specs=[pl.BlockSpec(two.shape, lambda i: (0, 0)), cols],
+        out_specs=cols,
+        out_shape=jax.ShapeDtypeStruct(x.shape, BF16),
+        cost_estimate=pl.CostEstimate(
+            flops=2 * rows * rows * channels, transcendentals=0, bytes_accessed=4 * rows * channels + 2 * rows * rows
+        ),
+    )(two, x)
 
 
 def layer(inputs, cotangent, factor_one, factor_two, up_weight, down_weight):
@@ -163,7 +207,7 @@
     n_dp = SIDE * CORES
     x_nat = inputs[0]
 
-    own, column = weight_column(up_weight, down_weight)
+    slabs, column = weight_column(up_weight, down_weight)
     one = swap(factor_one[0])
     mixed_one = nn(one, x_nat).astype(BF16)
     mixed_one, column = lax.optimization_barrier((mixed_one, column))
@@ -180,12 +224,13 @@
 
     by_q = swap(jnp.transpose(factor_two, (1, 0, 2))).reshape(block, blocks)
     two = diagonal(nn(by_q, pick))
-    pair = weight_pair(column)
+    two_t = two.T
+    pairs = weight_pairs(column)
     x_all, cot_all = swap(x_nat), swap(cotangent[0])
-    cols_one, _, two, x_all, cot_all = lax.optimization_barrier((cols_one, pair, two, x_all, cot_all))
-
-    weights = weight_halves(own, pair)
-    mixed_two = nn(two, cols_one).astype(BF16)
+    cols_one, _, two, two_t, x_all, cot_all = lax.optimization_barrier((cols_one, pairs, two, two_t, x_all, cot_all))
+
+    weights = weight_halves(slabs, pairs)
+    mixed_two = mix(two, cols_one)
     mixed = exchange(mixed_two, blocks)
 
     grad_two, grad_gated = mlp_call(grads_kernel, (mixed, x_all, cot_all), weights, (BF16, F32), 3)
@@ -196,19 +241,24 @@
     gate_in = swap(jax.vjp(jax.nn.silu, x_all.astype(F32))[1](grad_gated * mixed.astype(F32))[0])
     grad_cols, outputs, gate_in = lax.optimization_barrier((grad_cols, outputs, gate_in))
 
-    grad_one = exchange(tn(two, grad_cols).astype(BF16), blocks)
+    grad_one = exchange(mix(two_t, grad_cols), blocks)
 
     term_two = nt(diagonal(nt(grad_cols, cols_one)), pick).astype(BF16)
     term_two = swap(term_two.reshape(blocks, own_p * blocks)).reshape(n_dp, -1, block)
     grad_one, term_two = lax.optimization_barrier((grad_one, term_two))
 
     term_one = swap(nt(grad_one, x_nat).astype(BF16)).reshape(n_dp, block // n_dp, block)
-    summed = lax.all_to_all(
-        jnp.concatenate([term_one, term_two], axis=1), ("lo", "core"), split_axis=0, concat_axis=0, tiled=True
-    )
-    summed = jnp.sum(summed.astype(F32), axis=0)
-    grad_first = summed[: block // n_dp][None]
-    grad_second = jnp.transpose(summed[block // n_dp :].reshape(blocks // n_dp, own_p, blocks), (1, 0, 2))
+    terms = jnp.concatenate([term_one, term_two], axis=1)
+    terms = terms.reshape(SIDE, CORES, *terms.shape[1:])
+    core = lax.axis_index("core")
+    kept = lax.dynamic_index_in_dim(terms, core, axis=1, keepdims=False)
+    other = lax.ppermute(lax.dynamic_index_in_dim(terms, 1 - core, axis=1, keepdims=False), "core", [(0, 1), (1, 0)])
+    terms = (kept.astype(F32) + other.astype(F32)).astype(BF16)
+    terms = lax.all_to_all(terms, "lo", split_axis=0, concat_axis=0, tiled=True)
+    chunk = block // n_dp
+    grad_first = jnp.sum(terms[:, :chunk].astype(F32), axis=0)[None]
+    grad_second = jnp.sum(terms[:, chunk:].astype(F32), axis=0).reshape(blocks // n_dp, own_p, blocks)
+    grad_second = jnp.transpose(grad_second, (1, 0, 2))
 
     grad_inputs = (gate_in + tn(one, grad_one)).astype(BF16)[None]
     return outputs, grad_inputs, grad_first, grad_second

time: 274 us -> 275 us (level)
  waiting for transfers between devices: 145 us -> 122 us
  starting transfers between devices: 78 us -> 95.7 us
  Pallas kernels: 18.2 us -> 27.3 us
  matrix products: 10.7 us -> 7.65 us
    all_to_all x4, starting transfers between devices: 41.9 us -> 55 us  [exchange(): lax.all_to_all(x.reshape(blocks, x.shape[0] // blocks, x.shape[1]), TO, s...]
    ppermute x4 -> x2, starting transfers between devices: 18.7 us -> 6.45 us  [the longest x1 3.96 us: weight_pairs(): twin = lax.ppermute(others, ('y', 'x'), diagonal)]
    ppermute x3 -> x6, starting transfers between devices: 9.3 us -> 20.9 us  [shift(): return lax.ppermute(x, axis, [(i, (i + step) % SIDE) for i in range(SIDE)])]
    ppermute x3 -> x6, waiting for transfers between devices: 18.5 us -> 6.89 us  [shift(): return lax.ppermute(x, axis, [(i, (i + step) % SIDE) for i in range(SIDE)])]
    pallas_call x0 -> x3, Pallas kernels: none -> 9.09 us  [the longest x2 5.71 us: mix(): pl.pallas_call(mix_kernel, grid=(2,), in_specs=[pl.BlockSpec(two.shape, l...]
    all_to_all x1 -> x2, starting transfers between devices: 4.67 us -> 9.88 us  [the longest x1 6.43 us: weight_column(): lax.all_to_all(jnp.broadcast_to(piece[None], (SIDE, *piece.shape)), 'lo',...]
    ppermute x4 -> x2, waiting for transfers between devices: 5.78 us -> 1.19 us  [the longest x1 1.19 us: layer(): lax.ppermute(lax.dynamic_index_in_dim(terms, 1 - core, axis=1, keepdims=F...]
    all_to_all x1 -> x2, waiting for transfers between devices: 12.4 us -> 8.11 us  [the longest x1 4.55 us: layer(): terms = lax.all_to_all(terms, 'lo', split_axis=0, concat_axis=0, tiled=True)]
  transfers between devices with their start and end apart: 13 -> 15, of which waited for: 10 -> 8; matrix products, arithmetic and copies ran while one was open for 7% -> 6% of each run, Pallas kernels for 3% -> 5%
where the time goes in v2:
time: 275 us; the launch traced here: 274 us
  waiting for transfers between devices  122 us (44%)
  starting transfers between devices  95.7 us (35%)
  Pallas kernels  27.3 us (10%)
  local copies, waits for them, and re-layouts  14.8 us (5%)
  matrix products  7.65 us (3%)
  other arithmetic  5.26 us (2%)
    all_to_all x4, waiting for transfers between devices, exchange(): lax.all_to_all(x.reshape(blocks, x.shape[0] // blocks, x.shape[1]), TO, s...  102 us
    all_to_all x4, starting transfers between devices, exchange(): lax.all_to_all(x.reshape(blocks, x.shape[0] // blocks, x.shape[1]), TO, s...  55 us
    ppermute x6, starting transfers between devices, shift(): return lax.ppermute(x, axis, [(i, (i + step) % SIDE) for i in range(SIDE)])  20.9 us
    pallas_call x2, Pallas kernels, mlp_call(): pl.pallas_call(kernel, grid=(groups, len(weights)), in_specs=[cols] * len...  18.2 us
    unnamed x50, local copies, waits for them, and re-layouts  7.54 us
    ppermute x6, waiting for transfers between devices, shift(): return lax.ppermute(x, axis, [(i, (i + step) % SIDE) for i in range(SIDE)])  6.89 us
    all_to_all x1, starting transfers between devices, weight_column(): lax.all_to_all(jnp.broadcast_to(piece[None], (SIDE, *piece.shape)), 'lo',...  6.43 us
    pallas_call x2, Pallas kernels, mix(): pl.pallas_call(mix_kernel, grid=(2,), in_specs=[pl.BlockSpec(two.shape, l...  5.71 us
  transfers between devices with their start and end apart: 15, of which 8 were waited for; matrix products, arithmetic and copies ran while one was open for 6% of the time, Pallas kernels for 5%

profile of v2, /device:TPU:1, one launch (start us, length us, event | category | flops | bytes accessed | tf_op | source)
XLA Modules:
  0.0 273.9 jit_solution(11871716558032499421)
XLA Ops:
  0.7 0.9 dynamic-slice_bitcast_fusion
  1.6 0.7 broadcast_in_dim.17
  2.3 6.4 %all-to-all-start = ((bf16[4,2,2,24,384]{4,3,2,1,0:T(8,128)(2,1)}), bf16[4,2,2,24,384]{4,3,2,1,0:T(8,128)(2,1)S(1)}, u32[]{:S(2)}, u32[]{:S(2)}) async-start(bf16[4,2,2,24,384]{4,3,2,1,0:T(8,128)(2,1)} %broadcast_in_dim.17), calls=%async_computation | async-start | bytes 589824 | tf_op jit(solution)/shard_map/all_to_all | solution.py:139
  8.8 0.8 copy-done.7
  9.6 1.5 convolution_convert_fusion
  11.1 3.6 %all-to-all-done = bf16[4,2,2,24,384]{4,3,2,1,0:T(8,128)(2,1)S(1)} async-done(((bf16[4,2,2,24,384]{4,3,2,1,0:T(8,128)(2,1)}), bf16[4,2,2,24,384]{4,3,2,1,0:T(8,128)(2,1)S(1)}, u32[]{:S(2)}, u32[]{:S(2)}) %all-to-all-start) | async-done | bytes 294944 | tf_op jit(solution)/shard_map/all_to_all | solution.py:139
  14.7 20.9 %all-to-all-start.1 = ((bf16[64,8,768]{2,1,0:T(8,128)(2,1)}), bf16[64,8,768]{2,1,0:T(8,128)(2,1)S(1)}, u32[]{:S(2)}, u32[]{:S(2)}) async-start(bf16[64,8,768]{2,1,0:T(8,128)(2,1)} %bitcast.9), calls=%async_computation.1 | async-start | bytes 1572864 | tf_op jit(solution)/shard_map/all_to_all | solution.py:42
  36.4 4.0 %collective-permute-start = (bf16[2,2,3,24,384]{4,3,2,1,0:T(8,128)(2,1)S(1)}, bf16[2,2,3,24,384]{4,3,2,1,0:T(8,128)(2,1)S(1)}, u32[]{:S(2)}, u32[]{:S(2)}) collective-permute-start(bf16[2,2,3,24,384]{4,3,2,1,0:T(8,128)(2,1)S(1)} %get-tuple-element.50), channel_id=1, source_target_pairs={{0,17},{1,16},{2,19},{3,18},{16,1},{17,0},{18,3},{19,2},{32,49},{3... | collective-permute-start | bytes 663560 | tf_op jit(solution)/shard_map/ppermute | solution.py:164
  40.4 1.3 select_convert_fusion
  41.7 1.0 copy.50
  42.7 1.0 copy.51
  43.7 32.9 %all-to-all-done.1 = bf16[64,8,768]{2,1,0:T(8,128)(2,1)S(1)} async-done(((bf16[64,8,768]{2,1,0:T(8,128)(2,1)}), bf16[64,8,768]{2,1,0:T(8,128)(2,1)S(1)}, u32[]{:S(2)}, u32[]{:S(2)}) %all-to-all-start.1) | async-done | bytes 786464 | tf_op jit(solution)/shard_map/all_to_all | solution.py:42
  76.6 0.9 copy-done.4
  77.4 2.8 %shard_map.93 = bf16[512,768]{1,0:T(8,128)(2,1)} custom-call(bf16[512,512]{1,0:T(8,128)(2,1)} %get-tuple-element.20.two_ref, bf16[512,768]{1,0:T(8,128)(2,1)} %bitcast.111), custom_call_target="tpu_custom_call" | custom-call | flops 402653184 | bytes 2097152 | tf_op jit(solution)/shard_map/pallas_call | solution.py:192
  80.2 10.9 %all-to-all-start.2 = ((bf16[64,8,768]{2,1,0:T(8,128)(2,1)}), bf16[64,8,768]{2,1,0:T(8,128)(2,1)S(1)}, u32[]{:S(2)}, u32[]{:S(2)}) async-start(bf16[64,8,768]{2,1,0:T(8,128)(2,1)} %bitcast.113), calls=%async_computation.2 | async-start | bytes 1572864 | tf_op jit(solution)/shard_map/all_to_all | solution.py:42
  91.2 2.9 %collective-permute-start.1 = (bf16[2,2,3,24,384]{4,3,2,1,0:T(8,128)(2,1)S(1)}, bf16[2,2,3,24,384]{4,3,2,1,0:T(8,128)(2,1)S(1)}, u32[]{:S(2)}, u32[]{:S(2)}) collective-permute-start(bf16[2,2,3,24,384]{4,3,2,1,0:T(8,128)(2,1)S(1)} %get-tuple-element.49.refs_0_), channel_id=1, source_target_pairs={{0,16},{16,32},{32,48},{48,0},{1,17},{17,33},{33,49},{49,1},{2,18}... | collective-permute-start | bytes 663560 | tf_op jit(solution)/shard_map/ppermute | solution.py:49
  94.2 4.3 %collective-permute-start.2 = (bf16[2,2,3,24,384]{4,3,2,1,0:T(8,128)(2,1)S(1)}, bf16[2,2,3,24,384]{4,3,2,1,0:T(8,128)(2,1)S(1)}, u32[]{:S(2)}, u32[]{:S(2)}) collective-permute-start(bf16[2,2,3,24,384]{4,3,2,1,0:T(8,128)(2,1)S(1)} %get-tuple-element.49.refs_0_), channel_id=1, source_target_pairs={{0,32},{16,48},{32,0},{48,16},{1,33},{17,49},{33,1},{49,17},{2,34}... | collective-permute-start | bytes 663560 | tf_op jit(solution)/shard_map/ppermute | solution.py:49
  98.5 3.1 %collective-permute-start.3 = (bf16[2,2,3,24,384]{4,3,2,1,0:T(8,128)(2,1)S(1)}, bf16[2,2,3,24,384]{4,3,2,1,0:T(8,128)(2,1)S(1)}, u32[]{:S(2)}, u32[]{:S(2)}) collective-permute-start(bf16[2,2,3,24,384]{4,3,2,1,0:T(8,128)(2,1)S(1)} %get-tuple-element.49.refs_0_), channel_id=1, source_target_pairs={{0,48},{16,0},{32,16},{48,32},{1,49},{17,1},{33,17},{49,33},{2,50}... | collective-permute-start | bytes 663560 | tf_op jit(solution)/shard_map/ppermute | solution.py:49
  101.6 3.1 %collective-permute-start.4 = (bf16[2,2,3,24,384]{4,3,2,1,0:T(8,128)(2,1)S(1)}, bf16[2,2,3,24,384]{4,3,2,1,0:T(8,128)(2,1)S(1)}, u32[]{:S(2)}, u32[]{:S(2)}) collective-permute-start(bf16[2,2,3,24,384]{4,3,2,1,0:T(8,128)(2,1)S(1)} %get-tuple-element.48.refs_4_), channel_id=1, source_target_pairs={{0,1},{1,2},{2,3},{3,0},{4,5},{5,6},{6,7},{7,4},{8,9},{9,10},{10,1... | collective-permute-start | bytes 663560 | tf_op jit(solution)/shard_map/ppermute | solution.py:49
  104.7 4.5 %collective-permute-start.5 = (bf16[2,2,3,24,384]{4,3,2,1,0:T(8,128)(2,1)S(1)}, bf16[2,2,3,24,384]{4,3,2,1,0:T(8,128)(2,1)S(1)}, u32[]{:S(2)}, u32[]{:S(2)}) collective-permute-start(bf16[2,2,3,24,384]{4,3,2,1,0:T(8,128)(2,1)S(1)} %get-tuple-element.48.refs_4_), channel_id=1, source_target_pairs={{0,2},{1,3},{2,0},{3,1},{4,6},{5,7},{6,4},{7,5},{8,10},{9,11},{10,... | collective-permute-start | bytes 663560 | tf_op jit(solution)/shard_map/ppermute | solution.py:49
  109.2 3.0 %collective-permute-start.6 = (bf16[2,2,3,24,384]{4,3,2,1,0:T(8,128)(2,1)S(1)}, bf16[2,2,3,24,384]{4,3,2,1,0:T(8,128)(2,1)S(1)}, u32[]{:S(2)}, u32[]{:S(2)}) collective-permute-start(bf16[2,2,3,24,384]{4,3,2,1,0:T(8,128)(2,1)S(1)} %get-tuple-element.48.refs_4_), channel_id=1, source_target_pairs={{0,3},{1,0},{2,1},{3,2},{4,7},{5,4},{6,5},{7,6},{8,11},{9,8},{10,9... | collective-permute-start | bytes 663560 | tf_op jit(solution)/shard_map/ppermute | solution.py:49
  112.9 0.9 pad_maximum_fusion.slabs_ref
  113.8 6.9 %collective-permute-done.5.refs_6_ = bf16[2,2,3,24,384]{4,3,2,1,0:T(8,128)(2,1)S(1)} collective-permute-done((bf16[2,2,3,24,384]{4,3,2,1,0:T(8,128)(2,1)S(1)}, bf16[2,2,3,24,384]{4,3,2,1,0:T(8,128)(2,1)S(1)}, u32[]{:S(2)}, u32[]{:S(2)}) %collective-permute-start.5) | collective-permute-done | bytes 221216 | tf_op jit(solution)/shard_map/ppermute | solution.py:49
  121.4 0.7 copy-done.21
  122.1 3.4 %assemble.1 = bf16[2,2,32,24,384]{4,3,2,1,0:T(8,128)(2,1)} custom-call(s32[2]{0:T(128)} %pad_add_fusion.at_ref, bf16[2,2,8,24,384]{4,3,2,1,0:T(8,128)(2,1)} %pad_maximum_fusion.slabs_ref, bf16[2,2,3,24,384]{4,3,2,1,0:T(8,128)(2,1)} %copy-done.10, bf16[2,2,3,24,384]{4,3,2,1,0:T(8,128)(2,1)} %copy-done.16, bf16[2,2,3,24,384]{4,3,2,1,0:T(8,128)(2,1)} %copy-done.17, ...), custom_call_target="tpu_custom_call" | custom-call | bytes 4718592 | tf_op jit(solution)/shard_map/assemble/pallas_call | solution.py:173
  125.4 3.5 %collective-permute-start.7 = (bf16[2,2,768,384]{3,2,1,0:T(8,128)(2,1)}, bf16[2,2,768,384]{3,2,1,0:T(8,128)(2,1)S(1)}, u32[]{:S(2)}, u32[]{:S(2)}) collective-permute-start(bf16[2,2,768,384]{3,2,1,0:T(8,128)(2,1)} %bitcast.117), channel_id=1, source_target_pairs={{0,64},{64,0},{1,65},{65,1},{2,66},{66,2},{3,67},{67,3},{4,68},{68... | collective-permute-start | bytes 7077896 | tf_op jit(solution)/shard_map/ppermute | solution.py:182
  128.9 4.3 %collective-permute-done.7.other_ref = bf16[2,2,768,384]{3,2,1,0:T(8,128)(2,1)S(1)} collective-permute-done((bf16[2,2,768,384]{3,2,1,0:T(8,128)(2,1)}, bf16[2,2,768,384]{3,2,1,0:T(8,128)(2,1)S(1)}, u32[]{:S(2)}, u32[]{:S(2)}) %collective-permute-start.7) | collective-permute-done | bytes 2359328 | tf_op jit(solution)/shard_map/ppermute | solution.py:182
  133.3 1.4 copy-done.23
  135.1 10.1 %shard_map.94 = (bf16[512,768]{1,0:T(8,128)(2,1)}, f32[512,768]{1,0:T(8,128)}) custom-call(bf16[512,768]{1,0:T(8,128)(2,1)} %bitcast.107, bf16[512,768]{1,0:T(8,128)(2,1)} %bitcast.104, bf16[512,768]{1,0:T(8,128)(2,1)} %bitcast.125, bf16[2,2,768,384]{3,2,1,0:T(8,128)(2,1)} %bitcast.118, bf16[2,2,768,384]{3,2,1,0:T(8,128)(2,1)} %copy-done.23), custom_call_target="tpu_custom_call" | custom-call | flops 3623878656 | bytes 7077888 | tf_op jit(solution)/shard_map/pallas_call | solution.py:118
  145.2 15.3 %all-to-all-start.3 = ((bf16[64,8,768]{2,1,0:T(8,128)(2,1)}), bf16[64,8,768]{2,1,0:T(8,128)(2,1)S(1)}, u32[]{:S(2)}, u32[]{:S(2)}) async-start(bf16[64,8,768]{2,1,0:T(8,128)(2,1)} %bitcast.126), calls=%async_computation.3 | async-start | bytes 1572864 | tf_op jit(solution)/shard_map/all_to_all | solution.py:42
  160.5 8.1 %shard_map.95 = bf16[512,768]{1,0:T(8,128)(2,1)} custom-call(bf16[512,768]{1,0:T(8,128)(2,1)} %bitcast.108, bf16[512,768]{1,0:T(8,128)(2,1)} %bitcast.105, bf16[2,2,768,384]{3,2,1,0:T(8,128)(2,1)} %bitcast.119, bf16[2,2,768,384]{3,2,1,0:T(8,128)(2,1)} %copy-done.23), custom_call_target="tpu_custom_call" | custom-call | flops 2415919104 | bytes 6291456 | tf_op jit(solution)/shard_map/pallas_call | solution.py:118
  168.6 2.2 copy.52
  170.8 0.7 fusion.4
  171.7 30.5 %all-to-all-done.3 = bf16[64,8,768]{2,1,0:T(8,128)(2,1)S(1)} async-done(((bf16[64,8,768]{2,1,0:T(8,128)(2,1)}), bf16[64,8,768]{2,1,0:T(8,128)(2,1)S(1)}, u32[]{:S(2)}, u32[]{:S(2)}) %all-to-all-start.3) | async-done | bytes 786464 | tf_op jit(solution)/shard_map/all_to_all | solution.py:42
  202.1 0.9 copy-done.6
  203.0 2.9 %shard_map.96 = bf16[512,768]{1,0:T(8,128)(2,1)} custom-call(bf16[512,512]{1,0:T(8,128)(2,1)} %get-tuple-element.28.two_ref, bf16[512,768]{1,0:T(8,128)(2,1)} %bitcast.114), custom_call_target="tpu_custom_call" | custom-call | flops 402653184 | bytes 2097152 | tf_op jit(solution)/shard_map/pallas_call | solution.py:192
  205.9 7.9 %all-to-all-start.4 = ((bf16[64,8,768]{2,1,0:T(8,128)(2,1)}), bf16[64,8,768]{2,1,0:T(8,128)(2,1)S(1)}, u32[]{:S(2)}, u32[]{:S(2)}) async-start(bf16[64,8,768]{2,1,0:T(8,128)(2,1)} %bitcast.116), calls=%async_computation.4 | async-start | bytes 1572864 | tf_op jit(solution)/shard_map/all_to_all | solution.py:42
  213.8 1.9 fusion.9
  216.1 38.3 %all-to-all-done.4 = bf16[64,8,768]{2,1,0:T(8,128)(2,1)S(1)} async-done(((bf16[64,8,768]{2,1,0:T(8,128)(2,1)}), bf16[64,8,768]{2,1,0:T(8,128)(2,1)S(1)}, u32[]{:S(2)}, u32[]{:S(2)}) %all-to-all-start.4) | async-done | bytes 786464 | tf_op jit(solution)/shard_map/all_to_all | solution.py:42
  254.4 2.0 convolution_convert_fusion.1
  256.5 2.5 collective-permute-start.8
  259.0 1.2 collective-permute-done.8
  260.2 0.8 fusion.13
  261.0 3.5 %all-to-all-start.5 = ((bf16[4,72,512]{2,1,0:T(8,128)(2,1)}), bf16[4,72,512]{2,1,0:T(8,128)(2,1)S(1)}, u32[]{:S(2)}, u32[]{:S(2)}) async-start(bf16[4,72,512]{2,1,0:T(8,128)(2,1)} %fusion.13), calls=%async_computation.5 | async-start | bytes 589824 | tf_op jit(solution)/shard_map/all_to_all | solution.py:257
  265.0 1.9 fusion.7
  266.8 1.2 copy.58
  268.0 4.5 %all-to-all-done.5 = bf16[4,72,512]{2,1,0:T(8,128)(2,1)S(1)} async-done(((bf16[4,72,512]{2,1,0:T(8,128)(2,1)}), bf16[4,72,512]{2,1,0:T(8,128)(2,1)S(1)}, u32[]{:S(2)}, u32[]{:S(2)}) %all-to-all-start.5) | async-done | bytes 294944 | tf_op jit(solution)/shard_map/all_to_all | solution.py:257
  273.2 0.7 convert_reduce_fusion
  (72 shorter events, 4.4 us)
Async XLA Ops:
  0.6 8.1 %copy-start.13 = (bf16[1,512,512]{2,1,0:T(8,128)(2,1)S(1)}, bf16[1,512,512]{2,1,0:T(8,128)(2,1)}, u32[]{:S(2)}) copy-start(bf16[1,512,512]{2,1,0:T(8,128)(2,1)} %param.8) | copy-start | bytes 1572868
  0.6 9.0 %copy-start.12 = (bf16[1,512,768]{2,1,0:T(8,128)(2,1)S(1)}, bf16[1,512,768]{2,1,0:T(8,128)(2,1)}, u32[]{:S(2)}) copy-start(bf16[1,512,768]{2,1,0:T(8,128)(2,1)} %param.6) | copy-start | bytes 2359300
  2.3 12.3 %all-to-all-start = ((bf16[4,2,2,24,384]{4,3,2,1,0:T(8,128)(2,1)}), bf16[4,2,2,24,384]{4,3,2,1,0:T(8,128)(2,1)S(1)}, u32[]{:S(2)}, u32[]{:S(2)}) async-start(bf16[4,2,2,24,384]{4,3,2,1,0:T(8,128)(2,1)} %broadcast_in_dim.17), calls=%async_computation | async-start | bytes 589824 | tf_op jit(solution)/shard_map/all_to_all | solution.py:139
  8.8 0.8 copy-start.7
  9.6 26.0 %copy-start.22 = (bf16[8,64,64]{2,1,0:T(8,128)(2,1)S(1)}, bf16[8,64,64]{2,1,0:T(8,128)(2,1)}, u32[]{:S(2)}) copy-start(bf16[8,64,64]{2,1,0:T(8,128)(2,1)} %param.9) | copy-start | bytes 196612
  14.7 61.9 %all-to-all-start.1 = ((bf16[64,8,768]{2,1,0:T(8,128)(2,1)}), bf16[64,8,768]{2,1,0:T(8,128)(2,1)S(1)}, u32[]{:S(2)}, u32[]{:S(2)}) async-start(bf16[64,8,768]{2,1,0:T(8,128)(2,1)} %bitcast.9), calls=%async_computation.1 | async-start | bytes 1572864 | tf_op jit(solution)/shard_map/all_to_all | solution.py:42
  36.4 6.2 %copy-start.11 = (bf16[1,512,768]{2,1,0:T(8,128)(2,1)S(1)}, bf16[1,512,768]{2,1,0:T(8,128)(2,1)}, u32[]{:S(2)}) copy-start(bf16[1,512,768]{2,1,0:T(8,128)(2,1)} %param.7) | copy-start | bytes 2359300
  36.4 54.7 %collective-permute-start = (bf16[2,2,3,24,384]{4,3,2,1,0:T(8,128)(2,1)S(1)}, bf16[2,2,3,24,384]{4,3,2,1,0:T(8,128)(2,1)S(1)}, u32[]{:S(2)}, u32[]{:S(2)}) collective-permute-start(bf16[2,2,3,24,384]{4,3,2,1,0:T(8,128)(2,1)S(1)} %get-tuple-element.50), channel_id=1, source_target_pairs={{0,17},{1,16},{2,19},{3,18},{16,1},{17,0},{18,3},{19,2},{32,49},{3... | collective-permute-start | bytes 663560 | tf_op jit(solution)/shard_map/ppermute | solution.py:164
  76.6 0.9 copy-start.4
  80.2 32.6 %copy-start.14 = (bf16[2,192,384]{2,1,0:T(8,128)(2,1)S(1)}, bf16[2,192,384]{2,1,0:T(8,128)(2,1)}, u32[]{:S(2)}) copy-start(bf16[2,192,384]{2,1,0:T(8,128)(2,1)} %param.11) | copy-start | bytes 884740
  80.2 32.6 %copy-start.15 = (bf16[2,384,192]{1,2,0:T(8,128)(2,1)S(1)}, bf16[2,384,192]{1,2,0:T(8,128)(2,1)}, u32[]{:S(2)}) copy-start(bf16[2,384,192]{1,2,0:T(8,128)(2,1)} %param.10) | copy-start | bytes 884740
  80.2 53.0 %all-to-all-start.2 = ((bf16[64,8,768]{2,1,0:T(8,128)(2,1)}), bf16[64,8,768]{2,1,0:T(8,128)(2,1)S(1)}, u32[]{:S(2)}, u32[]{:S(2)}) async-start(bf16[64,8,768]{2,1,0:T(8,128)(2,1)} %bitcast.113), calls=%async_computation.2 | async-start | bytes 1572864 | tf_op jit(solution)/shard_map/all_to_all | solution.py:42
  91.2 29.5 %copy-start.9 = (bf16[2,2,3,24,384]{4,3,2,1,0:T(8,128)(2,1)}, bf16[2,2,3,24,384]{4,3,2,1,0:T(8,128)(2,1)S(1)}, u32[]{:S(2)}) copy-start(bf16[2,2,3,24,384]{4,3,2,1,0:T(8,128)(2,1)S(1)} %get-tuple-element.48.refs_4_) | copy-start | bytes 663556
  91.2 29.5 %copy-start.10 = (bf16[2,2,3,24,384]{4,3,2,1,0:T(8,128)(2,1)}, bf16[2,2,3,24,384]{4,3,2,1,0:T(8,128)(2,1)S(1)}, u32[]{:S(2)}) copy-start(bf16[2,2,3,24,384]{4,3,2,1,0:T(8,128)(2,1)S(1)} %get-tuple-element.49.refs_0_) | copy-start | bytes 663556
  91.2 18.0 %collective-permute-start.1 = (bf16[2,2,3,24,384]{4,3,2,1,0:T(8,128)(2,1)S(1)}, bf16[2,2,3,24,384]{4,3,2,1,0:T(8,128)(2,1)S(1)}, u32[]{:S(2)}, u32[]{:S(2)}) collective-permute-start(bf16[2,2,3,24,384]{4,3,2,1,0:T(8,128)(2,1)S(1)} %get-tuple-element.49.refs_0_), channel_id=1, source_target_pairs={{0,16},{16,32},{32,48},{48,0},{1,17},{17,33},{33,49},{49,1},{2,18}... | collective-permute-start | bytes 663560 | tf_op jit(solution)/shard_map/ppermute | solution.py:49
  94.2 19.6 %collective-permute-start.2 = (bf16[2,2,3,24,384]{4,3,2,1,0:T(8,128)(2,1)S(1)}, bf16[2,2,3,24,384]{4,3,2,1,0:T(8,128)(2,1)S(1)}, u32[]{:S(2)}, u32[]{:S(2)}) collective-permute-start(bf16[2,2,3,24,384]{4,3,2,1,0:T(8,128)(2,1)S(1)} %get-tuple-element.49.refs_0_), channel_id=1, source_target_pairs={{0,32},{16,48},{32,0},{48,16},{1,33},{17,49},{33,1},{49,17},{2,34}... | collective-permute-start | bytes 663560 | tf_op jit(solution)/shard_map/ppermute | solution.py:49
  98.5 15.3 %collective-permute-start.3 = (bf16[2,2,3,24,384]{4,3,2,1,0:T(8,128)(2,1)S(1)}, bf16[2,2,3,24,384]{4,3,2,1,0:T(8,128)(2,1)S(1)}, u32[]{:S(2)}, u32[]{:S(2)}) collective-permute-start(bf16[2,2,3,24,384]{4,3,2,1,0:T(8,128)(2,1)S(1)} %get-tuple-element.49.refs_0_), channel_id=1, source_target_pairs={{0,48},{16,0},{32,16},{48,32},{1,49},{17,1},{33,17},{49,33},{2,50}... | collective-permute-start | bytes 663560 | tf_op jit(solution)/shard_map/ppermute | solution.py:49
  101.6 12.2 %collective-permute-start.4 = (bf16[2,2,3,24,384]{4,3,2,1,0:T(8,128)(2,1)S(1)}, bf16[2,2,3,24,384]{4,3,2,1,0:T(8,128)(2,1)S(1)}, u32[]{:S(2)}, u32[]{:S(2)}) collective-permute-start(bf16[2,2,3,24,384]{4,3,2,1,0:T(8,128)(2,1)S(1)} %get-tuple-element.48.refs_4_), channel_id=1, source_target_pairs={{0,1},{1,2},{2,3},{3,0},{4,5},{5,6},{6,7},{7,4},{8,9},{9,10},{10,1... | collective-permute-start | bytes 663560 | tf_op jit(solution)/shard_map/ppermute | solution.py:49
  104.7 16.0 %collective-permute-start.5 = (bf16[2,2,3,24,384]{4,3,2,1,0:T(8,128)(2,1)S(1)}, bf16[2,2,3,24,384]{4,3,2,1,0:T(8,128)(2,1)S(1)}, u32[]{:S(2)}, u32[]{:S(2)}) collective-permute-start(bf16[2,2,3,24,384]{4,3,2,1,0:T(8,128)(2,1)S(1)} %get-tuple-element.48.refs_4_), channel_id=1, source_target_pairs={{0,2},{1,3},{2,0},{3,1},{4,6},{5,7},{6,4},{7,5},{8,10},{9,11},{10,... | collective-permute-start | bytes 663560 | tf_op jit(solution)/shard_map/ppermute | solution.py:49
  109.2 11.5 %copy-start.16 = (bf16[2,2,3,24,384]{4,3,2,1,0:T(8,128)(2,1)}, bf16[2,2,3,24,384]{4,3,2,1,0:T(8,128)(2,1)S(1)}, u32[]{:S(2)}) copy-start(bf16[2,2,3,24,384]{4,3,2,1,0:T(8,128)(2,1)S(1)} %collective-permute-done.1.refs_1_) | copy-start | bytes 663556
  109.2 11.5 %collective-permute-start.6 = (bf16[2,2,3,24,384]{4,3,2,1,0:T(8,128)(2,1)S(1)}, bf16[2,2,3,24,384]{4,3,2,1,0:T(8,128)(2,1)S(1)}, u32[]{:S(2)}, u32[]{:S(2)}) collective-permute-start(bf16[2,2,3,24,384]{4,3,2,1,0:T(8,128)(2,1)S(1)} %get-tuple-element.48.refs_4_), channel_id=1, source_target_pairs={{0,3},{1,0},{2,1},{3,2},{4,7},{5,4},{6,5},{7,6},{8,11},{9,8},{10,9... | collective-permute-start | bytes 663560 | tf_op jit(solution)/shard_map/ppermute | solution.py:49
  113.8 6.9 %copy-start.17 = (bf16[2,2,3,24,384]{4,3,2,1,0:T(8,128)(2,1)}, bf16[2,2,3,24,384]{4,3,2,1,0:T(8,128)(2,1)S(1)}, u32[]{:S(2)}) copy-start(bf16[2,2,3,24,384]{4,3,2,1,0:T(8,128)(2,1)S(1)} %collective-permute-done.2.refs_2_) | copy-start | bytes 663556
  113.8 6.9 %copy-start.18 = (bf16[2,2,3,24,384]{4,3,2,1,0:T(8,128)(2,1)}, bf16[2,2,3,24,384]{4,3,2,1,0:T(8,128)(2,1)S(1)}, u32[]{:S(2)}) copy-start(bf16[2,2,3,24,384]{4,3,2,1,0:T(8,128)(2,1)S(1)} %collective-permute-done.3.refs_3_) | copy-start | bytes 663556
  113.8 6.9 %copy-start.19 = (bf16[2,2,3,24,384]{4,3,2,1,0:T(8,128)(2,1)}, bf16[2,2,3,24,384]{4,3,2,1,0:T(8,128)(2,1)S(1)}, u32[]{:S(2)}) copy-start(bf16[2,2,3,24,384]{4,3,2,1,0:T(8,128)(2,1)S(1)} %collective-permute-done.4.refs_5_) | copy-start | bytes 663556
  120.7 0.7 copy-start.20
  121.4 0.7 copy-start.21
  125.4 7.8 %collective-permute-start.7 = (bf16[2,2,768,384]{3,2,1,0:T(8,128)(2,1)}, bf16[2,2,768,384]{3,2,1,0:T(8,128)(2,1)S(1)}, u32[]{:S(2)}, u32[]{:S(2)}) collective-permute-start(bf16[2,2,768,384]{3,2,1,0:T(8,128)(2,1)} %bitcast.117), channel_id=1, source_target_pairs={{0,64},{64,0},{1,65},{65,1},{2,66},{66,2},{3,67},{67,3},{4,68},{68... | collective-permute-start | bytes 7077896 | tf_op jit(solution)/shard_map/ppermute | solution.py:182
  133.3 1.4 copy-start.23
  133.3 1.8 copy-start.1
  145.2 57.0 %all-to-all-start.3 = ((bf16[64,8,768]{2,1,0:T(8,128)(2,1)}), bf16[64,8,768]{2,1,0:T(8,128)(2,1)S(1)}, u32[]{:S(2)}, u32[]{:S(2)}) async-start(bf16[64,8,768]{2,1,0:T(8,128)(2,1)} %bitcast.126), calls=%async_computation.3 | async-start | bytes 1572864 | tf_op jit(solution)/shard_map/all_to_all | solution.py:42
  160.5 10.3 %copy-start.8 = (f32[512,768]{1,0:T(8,128)S(1)}, f32[512,768]{1,0:T(8,128)}, u32[]{:S(2)}) copy-start(f32[512,768]{1,0:T(8,128)} %get-tuple-element.25) | copy-start | bytes 4718596
  168.6 2.2 copy-start
  168.6 2.2 copy-start.2
  202.1 0.9 copy-start.6
  203.0 10.8 %copy-start.5 = (bf16[64,8,768]{2,1,0:T(8,128)(2,1)S(1)}, bf16[64,8,768]{2,1,0:T(8,128)(2,1)}, u32[]{:S(2)}) copy-start(bf16[64,8,768]{2,1,0:T(8,128)(2,1)} %copy-done.4) | copy-start | bytes 2359300
  205.9 48.4 %all-to-all-start.4 = ((bf16[64,8,768]{2,1,0:T(8,128)(2,1)}), bf16[64,8,768]{2,1,0:T(8,128)(2,1)S(1)}, u32[]{:S(2)}, u32[]{:S(2)}) async-start(bf16[64,8,768]{2,1,0:T(8,128)(2,1)} %bitcast.116), calls=%async_computation.4 | async-start | bytes 1572864 | tf_op jit(solution)/shard_map/all_to_all | solution.py:42
  254.4 2.0 copy-start.3
  256.5 3.7 %collective-permute-start.8 = (bf16[4,72,512]{2,1,0:T(8,128)(2,1)S(1)}, bf16[4,72,512]{2,1,0:T(8,128)(2,1)S(1)}, u32[]{:S(2)}, u32[]{:S(2)}) collective-permute-start(bf16[4,72,512]{2,1,0:T(8,128)(2,1)S(1)} %fusion.18), channel_id=1, source_target_pairs={{0,64},{64,0},{1,65},{65,1},{2,66},{66,2},{3,67},{67,3},{4,68},{68... | collective-permute-start | bytes 884744 | tf_op jit(solution)/shard_map/ppermute | solution.py:255
  261.0 11.5 %all-to-all-start.5 = ((bf16[4,72,512]{2,1,0:T(8,128)(2,1)}), bf16[4,72,512]{2,1,0:T(8,128)(2,1)S(1)}, u32[]{:S(2)}, u32[]{:S(2)}) async-start(bf16[4,72,512]{2,1,0:T(8,128)(2,1)} %fusion.13), calls=%async_computation.5 | async-start | bytes 589824 | tf_op jit(solution)/shard_map/all_to_all | solution.py:257

commit v3 on v2

--- a/solution.py
+++ b/solution.py
@@ -4,6 +4,7 @@
 import jax.numpy as jnp
 from jax import lax
 from jax.experimental import pallas as pl
+from jax.experimental.layout import Layout, with_layout_constraint
 from jax.experimental.pallas import tpu as pltpu
 from jax.sharding import Mesh
 from jax.sharding import PartitionSpec as P
@@ -13,7 +14,22 @@
 BF16 = jnp.bfloat16
 SIDE = 4
 CORES = 2
-TO = ("x", "hi", "y")
+CHIPS = SIDE**3
+OTHER_WAY = (0, 3, 2, 1)
+
+
+def exchange_groups():
+    return [
+        [
+            core * CHIPS + (y * SIDE + (OTHER_WAY[hi] if core else hi)) * SIDE + x
+            for x in range(SIDE)
+            for hi in range(SIDE)
+            for y in range(SIDE)
+        ]
+        for core in range(CORES)
+    ]
+
+
 WEIGHT_SLICES = 8
 C0 = 0.7978845608028654
 C1 = 0.044715
@@ -29,6 +45,10 @@
 
 def tn(a, b):
     return lax.dot_general(a, b, (((0,), (0,)), ((), ())), preferred_element_type=F32)
+
+
+def row_major(x):
+    return with_layout_constraint(x, Layout(major_to_minor=tuple(range(x.ndim))))
 
 
 def swap(x, axis=0):
@@ -40,9 +60,27 @@
 
 def exchange(x, blocks):
     out = lax.all_to_all(
-        x.reshape(blocks, x.shape[0] // blocks, x.shape[1]), TO, split_axis=0, concat_axis=0, tiled=True
+        x.reshape(blocks, x.shape[0] // blocks, x.shape[1]),
+        ("core", "y", "hi", "x"),
+        split_axis=0,
+        concat_axis=0,
+        tiled=True,
+        axis_index_groups=exchange_groups(),
     )
     return out.reshape(x.shape)
+
+
+def other_way(x):
+    parts = x.reshape(SIDE, SIDE, -1, *x.shape[1:])
+    turned = jnp.stack([parts[:, hi] for hi in OTHER_WAY], axis=1).reshape(x.shape)
+    return jnp.where(lax.axis_index("core") == 1, turned, x)
+
+
+def turn(x):
+    pairs = [(SIDE + hi, SIDE + OTHER_WAY[hi]) for hi in (1, 3)]
+    moved = lax.ppermute(x, ("core", "hi"), pairs)
+    here = (lax.axis_index("core") == 1) & (lax.rem(lax.axis_index("hi"), 2) == 1)
+    return jnp.where(here, moved, x)
 
 
 def shift(x, axis, step):
@@ -182,25 +220,6 @@
     return half, lax.ppermute(half, "core", [(0, 1), (1, 0)])
 
 
-def mix_kernel(two_ref, x_ref, out_ref):
-    out_ref[...] = nn(two_ref[...], x_ref[...]).astype(BF16)
-
-
-def mix(two, x):
-    rows, channels = x.shape
-    cols = pl.BlockSpec((rows, channels // 2), lambda i: (0, i))
-    return pl.pallas_call(
-        mix_kernel,
-        grid=(2,),
-        in_specs=[pl.BlockSpec(two.shape, lambda i: (0, 0)), cols],
-        out_specs=cols,
-        out_shape=jax.ShapeDtypeStruct(x.shape, BF16),
-        cost_estimate=pl.CostEstimate(
-            flops=2 * rows * rows * channels, transcendentals=0, bytes_accessed=4 * rows * channels + 2 * rows * rows
-        ),
-    )(two, x)
-
-
 def layer(inputs, cotangent, factor_one, factor_two, up_weight, down_weight):
     block = factor_one.shape[1]
     own_p, blocks, _ = factor_two.shape
@@ -214,7 +233,9 @@
     cols_one = exchange(mixed_one, blocks)
 
     at = lax.broadcasted_iota(jnp.int32, (blocks, block), 1) // own_p
-    at = lax.rem(at, SIDE) * SIDE**2 + lax.rem(at // SIDE, SIDE) * SIDE + at // SIDE**2
+    hi = lax.rem(at // SIDE, SIDE)
+    hi = jnp.where(lax.axis_index("core") == 1, lax.rem(SIDE - hi, SIDE), hi)
+    at = lax.rem(at, SIDE) * SIDE**2 + hi * SIDE + at // SIDE**2
     pick = (at == lax.broadcasted_iota(jnp.int32, (blocks, block), 0)).astype(BF16)
 
     def diagonal(full):
@@ -222,15 +243,15 @@
         col = lax.broadcasted_iota(jnp.int32, (block, block), 1)
         return jnp.where(lax.rem(row, own_p) == lax.rem(col, own_p), full, 0.0).astype(BF16)
 
-    by_q = swap(jnp.transpose(factor_two, (1, 0, 2))).reshape(block, blocks)
-    two = diagonal(nn(by_q, pick))
-    two_t = two.T
+    by_q = other_way(swap(jnp.transpose(turn(factor_two), (1, 0, 2)))).reshape(block, blocks)
+    two = row_major(diagonal(nn(by_q, pick)))
+    two_t = row_major(two.T)
     pairs = weight_pairs(column)
     x_all, cot_all = swap(x_nat), swap(cotangent[0])
     cols_one, _, two, two_t, x_all, cot_all = lax.optimization_barrier((cols_one, pairs, two, two_t, x_all, cot_all))
 
     weights = weight_halves(slabs, pairs)
-    mixed_two = mix(two, cols_one)
+    mixed_two = nn(two, cols_one).astype(BF16)
     mixed = exchange(mixed_two, blocks)
 
     grad_two, grad_gated = mlp_call(grads_kernel, (mixed, x_all, cot_all), weights, (BF16, F32), 3)
@@ -241,10 +262,11 @@
     gate_in = swap(jax.vjp(jax.nn.silu, x_all.astype(F32))[1](grad_gated * mixed.astype(F32))[0])
     grad_cols, outputs, gate_in = lax.optimization_barrier((grad_cols, outputs, gate_in))
 
-    grad_one = exchange(mix(two_t, grad_cols), blocks)
+    grad_one = exchange(nn(two_t, grad_cols).astype(BF16), blocks)
 
     term_two = nt(diagonal(nt(grad_cols, cols_one)), pick).astype(BF16)
-    term_two = swap(term_two.reshape(blocks, own_p * blocks)).reshape(n_dp, -1, block)
+    term_two = swap(other_way(term_two.reshape(blocks, own_p * blocks))).reshape(n_dp, -1, block)
+    term_two = turn(term_two)
     grad_one, term_two = lax.optimization_barrier((grad_one, term_two))
 
     term_one = swap(nt(grad_one, x_nat).astype(BF16)).reshape(n_dp, block // n_dp, block)

time: 275 us -> 279 us (1.015)
  Pallas kernels: 27.3 us -> 21.6 us
  starting transfers between devices: 95.7 us -> 101 us
  matrix products: 7.65 us -> 10.7 us
    all_to_all x1, starting transfers between devices: 3.45 us -> 9.39 us  [layer(): terms = lax.all_to_all(terms, 'lo', split_axis=0, concat_axis=0, tiled=True)]
    pallas_call x2 -> x0, Pallas kernels: 5.71 us -> none  [mix(): pl.pallas_call(mix_kernel, grid=(2,), in_specs=[pl.BlockSpec(two.shape, l...]
    dot_general x2 -> x4, matrix products: 1.8 us -> 6.01 us  [nn(): lax.dot_general(a, b, (((1,), (0,)), ((), ())), preferred_element_type=F32)]
    unnamed x50 -> x44, local copies, waits for them, and re-layouts: 7.54 us -> 4.48 us
  transfers between devices with their start and end apart: 15 -> 17, of which waited for: 8 -> 10; matrix products, arithmetic and copies ran while one was open for 6% -> 7% of each run, Pallas kernels for 5% -> 4%
where the time goes in v3:
time: 279 us; the launch traced here: 276 us
  waiting for transfers between devices  124 us (44%)
  starting transfers between devices  101 us (36%)
  Pallas kernels  21.6 us (8%)
  local copies, waits for them, and re-layouts  12.7 us (5%)
  matrix products  10.7 us (4%)
  other arithmetic  4.81 us (2%)
    all_to_all x4, waiting for transfers between devices, exchange(): lax.all_to_all(x.reshape(blocks, x.shape[0] // blocks, x.shape[1]), ('cor...  104 us
    all_to_all x4, starting transfers between devices, exchange(): lax.all_to_all(x.reshape(blocks, x.shape[0] // blocks, x.shape[1]), ('cor...  55.2 us
    ppermute x6, starting transfers between devices, shift(): return lax.ppermute(x, axis, [(i, (i + step) % SIDE) for i in range(SIDE)])  20.9 us
    pallas_call x2, Pallas kernels, mlp_call(): pl.pallas_call(kernel, grid=(groups, len(weights)), in_specs=[cols] * len...  18.2 us
    all_to_all x1, starting transfers between devices, layer(): terms = lax.all_to_all(terms, 'lo', split_axis=0, concat_axis=0, tiled=True)  9.39 us
    all_to_all x1, starting transfers between devices, weight_column(): lax.all_to_all(jnp.broadcast_to(piece[None], (SIDE, *piece.shape)), 'lo',...  6.43 us
    dot_general x4, matrix products, nn(): lax.dot_general(a, b, (((1,), (0,)), ((), ())), preferred_element_type=F32)  6.01 us
    ppermute x6, waiting for transfers between devices, shift(): return lax.ppermute(x, axis, [(i, (i + step) % SIDE) for i in range(SIDE)])  5.82 us
  transfers between devices with their start and end apart: 17, of which 10 were waited for; matrix products, arithmetic and copies ran while one was open for 7% of the time, Pallas kernels for 4%

profile of v3, /device:TPU:1, one launch (start us, length us, event | category | flops | bytes accessed | tf_op | source)
XLA Modules:
  0.0 275.9 jit_solution(8267532461617963489)
XLA Ops:
  0.7 0.9 dynamic-slice_bitcast_fusion
  1.6 0.7 broadcast_in_dim.17
  2.3 6.4 %all-to-all-start = ((bf16[4,2,2,24,384]{4,3,2,1,0:T(8,128)(2,1)}), bf16[4,2,2,24,384]{4,3,2,1,0:T(8,128)(2,1)S(1)}, u32[]{:S(2)}, u32[]{:S(2)}) async-start(bf16[4,2,2,24,384]{4,3,2,1,0:T(8,128)(2,1)} %broadcast_in_dim.17), calls=%async_computation | async-start | bytes 589824 | tf_op jit(solution)/shard_map/all_to_all | solution.py:177
  8.8 0.8 copy-done.4
  9.6 1.5 convolution_convert_fusion.2
  11.1 3.6 %all-to-all-done = bf16[4,2,2,24,384]{4,3,2,1,0:T(8,128)(2,1)S(1)} async-done(((bf16[4,2,2,24,384]{4,3,2,1,0:T(8,128)(2,1)}), bf16[4,2,2,24,384]{4,3,2,1,0:T(8,128)(2,1)S(1)}, u32[]{:S(2)}, u32[]{:S(2)}) %all-to-all-start) | async-done | bytes 294944 | tf_op jit(solution)/shard_map/all_to_all | solution.py:177
  14.7 21.1 %all-to-all-start.1 = ((bf16[64,8,768]{2,1,0:T(8,128)(2,1)}), bf16[64,8,768]{2,1,0:T(8,128)(2,1)S(1)}, u32[]{:S(2)}, u32[]{:S(2)}) async-start(bf16[64,8,768]{2,1,0:T(8,128)(2,1)} %bitcast.150), calls=%async_computation.1 | async-start | bytes 1572864 | tf_op jit(solution)/shard_map/all_to_all | solution.py:62
  35.7 0.7 collective-permute-start.1
  36.4 1.0 copy.62
  37.4 1.0 copy.63
  39.0 1.0 copy.61
  40.0 0.8 copy_bitcast_fusion.1
  40.8 3.8 %collective-permute-start = (bf16[2,2,3,24,384]{4,3,2,1,0:T(8,128)(2,1)}, bf16[2,2,3,24,384]{4,3,2,1,0:T(8,128)(2,1)S(1)}, u32[]{:S(2)}, u32[]{:S(2)}) collective-permute-start(bf16[2,2,3,24,384]{4,3,2,1,0:T(8,128)(2,1)} %get-tuple-element.50), channel_id=1, source_target_pairs={{0,17},{1,16},{2,19},{3,18},{16,1},{17,0},{18,3},{19,2},{32,49},{3... | collective-permute-start | bytes 663560 | tf_op jit(solution)/shard_map/ppermute | solution.py:202
  44.6 36.8 %all-to-all-done.1 = bf16[64,8,768]{2,1,0:T(8,128)(2,1)S(1)} async-done(((bf16[64,8,768]{2,1,0:T(8,128)(2,1)}), bf16[64,8,768]{2,1,0:T(8,128)(2,1)S(1)}, u32[]{:S(2)}, u32[]{:S(2)}) %all-to-all-start.1) | async-done | bytes 786464 | tf_op jit(solution)/shard_map/all_to_all | solution.py:62
  81.5 1.5 fusion.7
  82.9 12.1 %all-to-all-start.2 = ((bf16[64,8,768]{2,1,0:T(8,128)(2,1)}), bf16[64,8,768]{2,1,0:T(8,128)(2,1)S(1)}, u32[]{:S(2)}, u32[]{:S(2)}) async-start(bf16[64,8,768]{2,1,0:T(8,128)(2,1)} %fusion.7), calls=%async_computation.2 | async-start | bytes 1572864 | tf_op jit(solution)/shard_map/all_to_all | solution.py:62
  95.1 2.9 %collective-permute-start.2 = (bf16[2,2,3,24,384]{4,3,2,1,0:T(8,128)(2,1)S(1)}, bf16[2,2,3,24,384]{4,3,2,1,0:T(8,128)(2,1)S(1)}, u32[]{:S(2)}, u32[]{:S(2)}) collective-permute-start(bf16[2,2,3,24,384]{4,3,2,1,0:T(8,128)(2,1)S(1)} %get-tuple-element.49.refs_0_), channel_id=1, source_target_pairs={{0,16},{16,32},{32,48},{48,0},{1,17},{17,33},{33,49},{49,1},{2,18}... | collective-permute-start | bytes 663560 | tf_op jit(solution)/shard_map/ppermute | solution.py:87
  98.1 4.3 %collective-permute-start.3 = (bf16[2,2,3,24,384]{4,3,2,1,0:T(8,128)(2,1)S(1)}, bf16[2,2,3,24,384]{4,3,2,1,0:T(8,128)(2,1)S(1)}, u32[]{:S(2)}, u32[]{:S(2)}) collective-permute-start(bf16[2,2,3,24,384]{4,3,2,1,0:T(8,128)(2,1)S(1)} %get-tuple-element.49.refs_0_), channel_id=1, source_target_pairs={{0,32},{16,48},{32,0},{48,16},{1,33},{17,49},{33,1},{49,17},{2,34}... | collective-permute-start | bytes 663560 | tf_op jit(solution)/shard_map/ppermute | solution.py:87
  102.4 3.1 %collective-permute-start.4 = (bf16[2,2,3,24,384]{4,3,2,1,0:T(8,128)(2,1)S(1)}, bf16[2,2,3,24,384]{4,3,2,1,0:T(8,128)(2,1)S(1)}, u32[]{:S(2)}, u32[]{:S(2)}) collective-permute-start(bf16[2,2,3,24,384]{4,3,2,1,0:T(8,128)(2,1)S(1)} %get-tuple-element.49.refs_0_), channel_id=1, source_target_pairs={{0,48},{16,0},{32,16},{48,32},{1,49},{17,1},{33,17},{49,33},{2,50}... | collective-permute-start | bytes 663560 | tf_op jit(solution)/shard_map/ppermute | solution.py:87
  105.5 3.1 %collective-permute-start.5 = (bf16[2,2,3,24,384]{4,3,2,1,0:T(8,128)(2,1)S(1)}, bf16[2,2,3,24,384]{4,3,2,1,0:T(8,128)(2,1)S(1)}, u32[]{:S(2)}, u32[]{:S(2)}) collective-permute-start(bf16[2,2,3,24,384]{4,3,2,1,0:T(8,128)(2,1)S(1)} %get-tuple-element.48.refs_4_), channel_id=1, source_target_pairs={{0,1},{1,2},{2,3},{3,0},{4,5},{5,6},{6,7},{7,4},{8,9},{9,10},{10,1... | collective-permute-start | bytes 663560 | tf_op jit(solution)/shard_map/ppermute | solution.py:87
  108.6 4.5 %collective-permute-start.6 = (bf16[2,2,3,24,384]{4,3,2,1,0:T(8,128)(2,1)S(1)}, bf16[2,2,3,24,384]{4,3,2,1,0:T(8,128)(2,1)S(1)}, u32[]{:S(2)}, u32[]{:S(2)}) collective-permute-start(bf16[2,2,3,24,384]{4,3,2,1,0:T(8,128)(2,1)S(1)} %get-tuple-element.48.refs_4_), channel_id=1, source_target_pairs={{0,2},{1,3},{2,0},{3,1},{4,6},{5,7},{6,4},{7,5},{8,10},{9,11},{10,... | collective-permute-start | bytes 663560 | tf_op jit(solution)/shard_map/ppermute | solution.py:87
  113.1 3.0 %collective-permute-start.7 = (bf16[2,2,3,24,384]{4,3,2,1,0:T(8,128)(2,1)S(1)}, bf16[2,2,3,24,384]{4,3,2,1,0:T(8,128)(2,1)}, u32[]{:S(2)}, u32[]{:S(2)}) collective-permute-start(bf16[2,2,3,24,384]{4,3,2,1,0:T(8,128)(2,1)S(1)} %get-tuple-element.48.refs_4_), channel_id=1, source_target_pairs={{0,3},{1,0},{2,1},{3,2},{4,7},{5,4},{6,5},{7,6},{8,11},{9,8},{10,9... | collective-permute-start | bytes 663560 | tf_op jit(solution)/shard_map/ppermute | solution.py:87
  116.8 0.9 pad_maximum_fusion.slabs_ref
  117.7 5.6 %collective-permute-done.6.refs_6_ = bf16[2,2,3,24,384]{4,3,2,1,0:T(8,128)(2,1)S(1)} collective-permute-done((bf16[2,2,3,24,384]{4,3,2,1,0:T(8,128)(2,1)S(1)}, bf16[2,2,3,24,384]{4,3,2,1,0:T(8,128)(2,1)S(1)}, u32[]{:S(2)}, u32[]{:S(2)}) %collective-permute-start.6) | collective-permute-done | bytes 221216 | tf_op jit(solution)/shard_map/ppermute | solution.py:87
  123.3 0.7 copy-done.19
  124.2 3.4 %assemble.1 = bf16[2,2,32,24,384]{4,3,2,1,0:T(8,128)(2,1)} custom-call(s32[2]{0:T(128)} %pad_add_fusion.at_ref, bf16[2,2,8,24,384]{4,3,2,1,0:T(8,128)(2,1)} %pad_maximum_fusion.slabs_ref, bf16[2,2,3,24,384]{4,3,2,1,0:T(8,128)(2,1)} %copy-done.7, bf16[2,2,3,24,384]{4,3,2,1,0:T(8,128)(2,1)} %copy-done.15, bf16[2,2,3,24,384]{4,3,2,1,0:T(8,128)(2,1)} %copy-done.16, ...), custom_call_target="tpu_custom_call" | custom-call | bytes 4718592 | tf_op jit(solution)/shard_map/assemble/pallas_call | solution.py:211
  127.6 1.9 collective-permute-start.8
  129.5 4.8 %collective-permute-done.8.other_ref = bf16[2,2,768,384]{3,2,1,0:T(8,128)(2,1)} collective-permute-done((bf16[2,2,768,384]{3,2,1,0:T(8,128)(2,1)}, bf16[2,2,768,384]{3,2,1,0:T(8,128)(2,1)}, u32[]{:S(2)}, u32[]{:S(2)}) %collective-permute-start.8) | collective-permute-done | bytes 2359328 | tf_op jit(solution)/shard_map/ppermute | solution.py:220
  134.4 1.5 all-to-all-done.2
  135.9 0.9 copy-done.1
  136.8 10.2 %shard_map.93 = (bf16[512,768]{1,0:T(8,128)(2,1)}, f32[512,768]{1,0:T(8,128)}) custom-call(bf16[512,768]{1,0:T(8,128)(2,1)} %bitcast.134, bf16[512,768]{1,0:T(8,128)(2,1)} %bitcast.131, bf16[512,768]{1,0:T(8,128)(2,1)} %bitcast.148, bf16[2,2,768,384]{3,2,1,0:T(8,128)(2,1)} %bitcast.139, bf16[2,2,768,384]{3,2,1,0:T(8,128)(2,1)} %collective-permute-done.8.other_ref), custom_call_target="tpu_custom_call" | custom-call | flops 3623878656 | bytes 7077888 | tf_op jit(solution)/shard_map/pallas_call | solution.py:156
  146.9 13.0 %all-to-all-start.3 = ((bf16[64,8,768]{2,1,0:T(8,128)(2,1)}), bf16[64,8,768]{2,1,0:T(8,128)(2,1)S(1)}, u32[]{:S(2)}, u32[]{:S(2)}) async-start(bf16[64,8,768]{2,1,0:T(8,128)(2,1)} %bitcast.153), calls=%async_computation.3 | async-start | bytes 1572864 | tf_op jit(solution)/shard_map/all_to_all | solution.py:62
  159.9 8.1 %shard_map.94 = bf16[512,768]{1,0:T(8,128)(2,1)} custom-call(bf16[512,768]{1,0:T(8,128)(2,1)} %bitcast.135, bf16[512,768]{1,0:T(8,128)(2,1)} %bitcast.132, bf16[2,2,768,384]{3,2,1,0:T(8,128)(2,1)} %bitcast.140, bf16[2,2,768,384]{3,2,1,0:T(8,128)(2,1)} %collective-permute-done.8.other_ref), custom_call_target="tpu_custom_call" | custom-call | flops 2415919104 | bytes 6291456 | tf_op jit(solution)/shard_map/pallas_call | solution.py:156
  168.0 2.2 copy.64
  170.2 0.7 fusion.4
  171.1 31.7 %all-to-all-done.3 = bf16[64,8,768]{2,1,0:T(8,128)(2,1)S(1)} async-done(((bf16[64,8,768]{2,1,0:T(8,128)(2,1)}), bf16[64,8,768]{2,1,0:T(8,128)(2,1)S(1)}, u32[]{:S(2)}, u32[]{:S(2)}) %all-to-all-start.3) | async-done | bytes 786464 | tf_op jit(solution)/shard_map/all_to_all | solution.py:62
  202.7 2.8 %fusion.8 = bf16[64,8,768]{2,1,0:T(8,128)(2,1)} fusion(bf16[512,512]{1,0:T(8,128)(2,1)} %bitcast.158, bf16[512,768]{1,0:T(8,128)(2,1)S(1)} %bitcast.151), kind=kOutput, calls=%fused_computation.17 | convolution fusion | flops 403046400 | bytes 2097152 | tf_op jit(solution)/shard_map/dot_general | solution.py:43
  205.5 9.0 %all-to-all-start.4 = ((bf16[64,8,768]{2,1,0:T(8,128)(2,1)}), bf16[64,8,768]{2,1,0:T(8,128)(2,1)S(1)}, u32[]{:S(2)}, u32[]{:S(2)}) async-start(bf16[64,8,768]{2,1,0:T(8,128)(2,1)} %fusion.8), calls=%async_computation.4 | async-start | bytes 1572864 | tf_op jit(solution)/shard_map/all_to_all | solution.py:62
  214.6 2.2 fusion.12
  218.0 33.7 %all-to-all-done.4 = bf16[64,8,768]{2,1,0:T(8,128)(2,1)S(1)} async-done(((bf16[64,8,768]{2,1,0:T(8,128)(2,1)}), bf16[64,8,768]{2,1,0:T(8,128)(2,1)S(1)}, u32[]{:S(2)}, u32[]{:S(2)}) %all-to-all-start.4) | async-done | bytes 786464 | tf_op jit(solution)/shard_map/all_to_all | solution.py:62
  252.7 2.3 collective-permute-start.10
  255.1 1.2 collective-permute-done.10
  256.2 0.8 fusion.15
  257.0 9.4 %all-to-all-start.5 = ((bf16[4,72,512]{2,1,0:T(8,128)(2,1)}), bf16[4,72,512]{2,1,0:T(8,128)(2,1)S(1)}, u32[]{:S(2)}, u32[]{:S(2)}) async-start(bf16[4,72,512]{2,1,0:T(8,128)(2,1)} %fusion.15), calls=%async_computation.5 | async-start | bytes 589824 | tf_op jit(solution)/shard_map/all_to_all | solution.py:279
  266.9 1.9 fusion.9
  268.8 1.2 copy.75
  269.9 4.6 %all-to-all-done.5 = bf16[4,72,512]{2,1,0:T(8,128)(2,1)S(1)} async-done(((bf16[4,72,512]{2,1,0:T(8,128)(2,1)}), bf16[4,72,512]{2,1,0:T(8,128)(2,1)S(1)}, u32[]{:S(2)}, u32[]{:S(2)}) %all-to-all-start.5) | async-done | bytes 294944 | tf_op jit(solution)/shard_map/all_to_all | solution.py:279
  275.2 0.7 convert_reduce_fusion
  (77 shorter events, 5.1 us)
Async XLA Ops:
  0.6 8.1 %copy-start.12 = (bf16[1,512,512]{2,1,0:T(8,128)(2,1)S(1)}, bf16[1,512,512]{2,1,0:T(8,128)(2,1)}, u32[]{:S(2)}) copy-start(bf16[1,512,512]{2,1,0:T(8,128)(2,1)} %param.8) | copy-start | bytes 1572868
  0.6 9.0 %copy-start.9 = (bf16[1,512,768]{2,1,0:T(8,128)(2,1)S(1)}, bf16[1,512,768]{2,1,0:T(8,128)(2,1)}, u32[]{:S(2)}) copy-start(bf16[1,512,768]{2,1,0:T(8,128)(2,1)} %param.6) | copy-start | bytes 2359300
  2.3 12.3 %all-to-all-start = ((bf16[4,2,2,24,384]{4,3,2,1,0:T(8,128)(2,1)}), bf16[4,2,2,24,384]{4,3,2,1,0:T(8,128)(2,1)S(1)}, u32[]{:S(2)}, u32[]{:S(2)}) async-start(bf16[4,2,2,24,384]{4,3,2,1,0:T(8,128)(2,1)} %broadcast_in_dim.17), calls=%async_computation | async-start | bytes 589824 | tf_op jit(solution)/shard_map/all_to_all | solution.py:177
  8.8 0.8 copy-start.4
  9.6 26.1 %copy-start.20 = (bf16[8,64,64]{2,1,0:T(8,128)(2,1)S(1)}, bf16[8,64,64]{2,1,0:T(8,128)(2,1)}, u32[]{:S(2)}) copy-start(bf16[8,64,64]{2,1,0:T(8,128)(2,1)} %param.9) | copy-start | bytes 196612
  14.6 22.8 %copy-start.8 = (bf16[1,512,768]{2,1,0:T(8,128)(2,1)S(1)}, bf16[1,512,768]{2,1,0:T(8,128)(2,1)}, u32[]{:S(2)}) copy-start(bf16[1,512,768]{2,1,0:T(8,128)(2,1)} %param.7) | copy-start | bytes 2359300
  14.7 66.8 %all-to-all-start.1 = ((bf16[64,8,768]{2,1,0:T(8,128)(2,1)}), bf16[64,8,768]{2,1,0:T(8,128)(2,1)S(1)}, u32[]{:S(2)}, u32[]{:S(2)}) async-start(bf16[64,8,768]{2,1,0:T(8,128)(2,1)} %bitcast.150), calls=%async_computation.1 | async-start | bytes 1572864 | tf_op jit(solution)/shard_map/all_to_all | solution.py:62
  35.7 2.7 collective-permute-start.1
  40.8 54.2 %collective-permute-start = (bf16[2,2,3,24,384]{4,3,2,1,0:T(8,128)(2,1)}, bf16[2,2,3,24,384]{4,3,2,1,0:T(8,128)(2,1)S(1)}, u32[]{:S(2)}, u32[]{:S(2)}) collective-permute-start(bf16[2,2,3,24,384]{4,3,2,1,0:T(8,128)(2,1)} %get-tuple-element.50), channel_id=1, source_target_pairs={{0,17},{1,16},{2,19},{3,18},{16,1},{17,0},{18,3},{19,2},{32,49},{3... | collective-permute-start | bytes 663560 | tf_op jit(solution)/shard_map/ppermute | solution.py:202
  81.4 13.6 %copy-start.10 = (bf16[64,8,768]{2,1,0:T(8,128)(2,1)}, bf16[64,8,768]{2,1,0:T(8,128)(2,1)S(1)}, u32[]{:S(2)}) copy-start(bf16[64,8,768]{2,1,0:T(8,128)(2,1)S(1)} %all-to-all-done.1) | copy-start | bytes 2359300
  82.9 33.9 %copy-start.13 = (bf16[2,192,384]{2,1,0:T(8,128)(2,1)S(1)}, bf16[2,192,384]{2,1,0:T(8,128)(2,1)}, u32[]{:S(2)}) copy-start(bf16[2,192,384]{2,1,0:T(8,128)(2,1)} %param.11) | copy-start | bytes 884740
  82.9 33.9 %copy-start.14 = (bf16[2,384,192]{1,2,0:T(8,128)(2,1)S(1)}, bf16[2,384,192]{1,2,0:T(8,128)(2,1)}, u32[]{:S(2)}) copy-start(bf16[2,384,192]{1,2,0:T(8,128)(2,1)} %param.10) | copy-start | bytes 884740
  82.9 53.0 %all-to-all-start.2 = ((bf16[64,8,768]{2,1,0:T(8,128)(2,1)}), bf16[64,8,768]{2,1,0:T(8,128)(2,1)S(1)}, u32[]{:S(2)}, u32[]{:S(2)}) async-start(bf16[64,8,768]{2,1,0:T(8,128)(2,1)} %fusion.7), calls=%async_computation.2 | async-start | bytes 1572864 | tf_op jit(solution)/shard_map/all_to_all | solution.py:62
  95.1 29.1 %copy-start.6 = (bf16[2,2,3,24,384]{4,3,2,1,0:T(8,128)(2,1)}, bf16[2,2,3,24,384]{4,3,2,1,0:T(8,128)(2,1)S(1)}, u32[]{:S(2)}) copy-start(bf16[2,2,3,24,384]{4,3,2,1,0:T(8,128)(2,1)S(1)} %get-tuple-element.48.refs_4_) | copy-start | bytes 663556
  95.1 29.1 %copy-start.7 = (bf16[2,2,3,24,384]{4,3,2,1,0:T(8,128)(2,1)}, bf16[2,2,3,24,384]{4,3,2,1,0:T(8,128)(2,1)S(1)}, u32[]{:S(2)}) copy-start(bf16[2,2,3,24,384]{4,3,2,1,0:T(8,128)(2,1)S(1)} %get-tuple-element.49.refs_0_) | copy-start | bytes 663556
  95.1 18.0 %collective-permute-start.2 = (bf16[2,2,3,24,384]{4,3,2,1,0:T(8,128)(2,1)S(1)}, bf16[2,2,3,24,384]{4,3,2,1,0:T(8,128)(2,1)S(1)}, u32[]{:S(2)}, u32[]{:S(2)}) collective-permute-start(bf16[2,2,3,24,384]{4,3,2,1,0:T(8,128)(2,1)S(1)} %get-tuple-element.49.refs_0_), channel_id=1, source_target_pairs={{0,16},{16,32},{32,48},{48,0},{1,17},{17,33},{33,49},{49,1},{2,18}... | collective-permute-start | bytes 663560 | tf_op jit(solution)/shard_map/ppermute | solution.py:87
  98.1 19.6 %collective-permute-start.3 = (bf16[2,2,3,24,384]{4,3,2,1,0:T(8,128)(2,1)S(1)}, bf16[2,2,3,24,384]{4,3,2,1,0:T(8,128)(2,1)S(1)}, u32[]{:S(2)}, u32[]{:S(2)}) collective-permute-start(bf16[2,2,3,24,384]{4,3,2,1,0:T(8,128)(2,1)S(1)} %get-tuple-element.49.refs_0_), channel_id=1, source_target_pairs={{0,32},{16,48},{32,0},{48,16},{1,33},{17,49},{33,1},{49,17},{2,34}... | collective-permute-start | bytes 663560 | tf_op jit(solution)/shard_map/ppermute | solution.py:87
  102.4 15.3 %collective-permute-start.4 = (bf16[2,2,3,24,384]{4,3,2,1,0:T(8,128)(2,1)S(1)}, bf16[2,2,3,24,384]{4,3,2,1,0:T(8,128)(2,1)S(1)}, u32[]{:S(2)}, u32[]{:S(2)}) collective-permute-start(bf16[2,2,3,24,384]{4,3,2,1,0:T(8,128)(2,1)S(1)} %get-tuple-element.49.refs_0_), channel_id=1, source_target_pairs={{0,48},{16,0},{32,16},{48,32},{1,49},{17,1},{33,17},{49,33},{2,50}... | collective-permute-start | bytes 663560 | tf_op jit(solution)/shard_map/ppermute | solution.py:87
  105.5 12.2 %collective-permute-start.5 = (bf16[2,2,3,24,384]{4,3,2,1,0:T(8,128)(2,1)S(1)}, bf16[2,2,3,24,384]{4,3,2,1,0:T(8,128)(2,1)S(1)}, u32[]{:S(2)}, u32[]{:S(2)}) collective-permute-start(bf16[2,2,3,24,384]{4,3,2,1,0:T(8,128)(2,1)S(1)} %get-tuple-element.48.refs_4_), channel_id=1, source_target_pairs={{0,1},{1,2},{2,3},{3,0},{4,5},{5,6},{6,7},{7,4},{8,9},{9,10},{10,1... | collective-permute-start | bytes 663560 | tf_op jit(solution)/shard_map/ppermute | solution.py:87
  108.6 14.7 %collective-permute-start.6 = (bf16[2,2,3,24,384]{4,3,2,1,0:T(8,128)(2,1)S(1)}, bf16[2,2,3,24,384]{4,3,2,1,0:T(8,128)(2,1)S(1)}, u32[]{:S(2)}, u32[]{:S(2)}) collective-permute-start(bf16[2,2,3,24,384]{4,3,2,1,0:T(8,128)(2,1)S(1)} %get-tuple-element.48.refs_4_), channel_id=1, source_target_pairs={{0,2},{1,3},{2,0},{3,1},{4,6},{5,7},{6,4},{7,5},{8,10},{9,11},{10,... | collective-permute-start | bytes 663560 | tf_op jit(solution)/shard_map/ppermute | solution.py:87
  113.1 11.1 %copy-start.15 = (bf16[2,2,3,24,384]{4,3,2,1,0:T(8,128)(2,1)}, bf16[2,2,3,24,384]{4,3,2,1,0:T(8,128)(2,1)S(1)}, u32[]{:S(2)}) copy-start(bf16[2,2,3,24,384]{4,3,2,1,0:T(8,128)(2,1)S(1)} %collective-permute-done.2.refs_1_) | copy-start | bytes 663556
  113.1 11.1 %collective-permute-start.7 = (bf16[2,2,3,24,384]{4,3,2,1,0:T(8,128)(2,1)S(1)}, bf16[2,2,3,24,384]{4,3,2,1,0:T(8,128)(2,1)}, u32[]{:S(2)}, u32[]{:S(2)}) collective-permute-start(bf16[2,2,3,24,384]{4,3,2,1,0:T(8,128)(2,1)S(1)} %get-tuple-element.48.refs_4_), channel_id=1, source_target_pairs={{0,3},{1,0},{2,1},{3,2},{4,7},{5,4},{6,5},{7,6},{8,11},{9,8},{10,9... | collective-permute-start | bytes 663560 | tf_op jit(solution)/shard_map/ppermute | solution.py:87
  117.7 6.6 %copy-start.16 = (bf16[2,2,3,24,384]{4,3,2,1,0:T(8,128)(2,1)}, bf16[2,2,3,24,384]{4,3,2,1,0:T(8,128)(2,1)S(1)}, u32[]{:S(2)}) copy-start(bf16[2,2,3,24,384]{4,3,2,1,0:T(8,128)(2,1)S(1)} %collective-permute-done.3.refs_2_) | copy-start | bytes 663556
  117.7 6.6 %copy-start.17 = (bf16[2,2,3,24,384]{4,3,2,1,0:T(8,128)(2,1)}, bf16[2,2,3,24,384]{4,3,2,1,0:T(8,128)(2,1)S(1)}, u32[]{:S(2)}) copy-start(bf16[2,2,3,24,384]{4,3,2,1,0:T(8,128)(2,1)S(1)} %collective-permute-done.4.refs_3_) | copy-start | bytes 663556
  117.7 5.6 %copy-start.18 = (bf16[2,2,3,24,384]{4,3,2,1,0:T(8,128)(2,1)}, bf16[2,2,3,24,384]{4,3,2,1,0:T(8,128)(2,1)S(1)}, u32[]{:S(2)}) copy-start(bf16[2,2,3,24,384]{4,3,2,1,0:T(8,128)(2,1)S(1)} %collective-permute-done.5.refs_5_) | copy-start | bytes 663556
  123.3 0.7 copy-start.19
  127.6 6.8 %collective-permute-start.8 = (bf16[2,2,768,384]{3,2,1,0:T(8,128)(2,1)}, bf16[2,2,768,384]{3,2,1,0:T(8,128)(2,1)}, u32[]{:S(2)}, u32[]{:S(2)}) collective-permute-start(bf16[2,2,768,384]{3,2,1,0:T(8,128)(2,1)} %bitcast.138), channel_id=1, source_target_pairs={{0,64},{64,0},{1,65},{65,1},{2,66},{66,2},{3,67},{67,3},{4,68},{68... | collective-permute-start | bytes 7077896 | tf_op jit(solution)/shard_map/ppermute | solution.py:220
  135.9 0.9 copy-start.1
  146.9 55.8 %all-to-all-start.3 = ((bf16[64,8,768]{2,1,0:T(8,128)(2,1)}), bf16[64,8,768]{2,1,0:T(8,128)(2,1)S(1)}, u32[]{:S(2)}, u32[]{:S(2)}) async-start(bf16[64,8,768]{2,1,0:T(8,128)(2,1)} %bitcast.153), calls=%async_computation.3 | async-start | bytes 1572864 | tf_op jit(solution)/shard_map/all_to_all | solution.py:62
  159.9 10.3 %copy-start.5 = (f32[512,768]{1,0:T(8,128)S(1)}, f32[512,768]{1,0:T(8,128)}, u32[]{:S(2)}) copy-start(f32[512,768]{1,0:T(8,128)} %get-tuple-element.25) | copy-start | bytes 4718596
  168.0 2.2 copy-start
  168.0 2.2 copy-start.2
  202.7 2.8 %copy-start.11 = (bf16[64,8,768]{2,1,0:T(8,128)(2,1)}, bf16[64,8,768]{2,1,0:T(8,128)(2,1)S(1)}, u32[]{:S(2)}) copy-start(bf16[64,8,768]{2,1,0:T(8,128)(2,1)S(1)} %all-to-all-done.3) | copy-start | bytes 2359300
  205.5 46.2 %all-to-all-start.4 = ((bf16[64,8,768]{2,1,0:T(8,128)(2,1)}), bf16[64,8,768]{2,1,0:T(8,128)(2,1)S(1)}, u32[]{:S(2)}, u32[]{:S(2)}) async-start(bf16[64,8,768]{2,1,0:T(8,128)(2,1)} %fusion.8), calls=%async_computation.4 | async-start | bytes 1572864 | tf_op jit(solution)/shard_map/all_to_all | solution.py:62
  217.3 0.7 collective-permute-start.9
  251.7 0.9 copy-start.3
  252.7 3.5 %collective-permute-start.10 = (bf16[4,72,512]{2,1,0:T(8,128)(2,1)S(1)}, bf16[4,72,512]{2,1,0:T(8,128)(2,1)S(1)}, u32[]{:S(2)}, u32[]{:S(2)}) collective-permute-start(bf16[4,72,512]{2,1,0:T(8,128)(2,1)S(1)} %fusion.20), channel_id=1, source_target_pairs={{0,64},{64,0},{1,65},{65,1},{2,66},{66,2},{3,67},{67,3},{4,68},{68... | collective-permute-start | bytes 884744 | tf_op jit(solution)/shard_map/ppermute | solution.py:277
  257.0 17.5 %all-to-all-start.5 = ((bf16[4,72,512]{2,1,0:T(8,128)(2,1)}), bf16[4,72,512]{2,1,0:T(8,128)(2,1)S(1)}, u32[]{:S(2)}, u32[]{:S(2)}) async-start(bf16[4,72,512]{2,1,0:T(8,128)(2,1)} %fusion.15), calls=%async_computation.5 | async-start | bytes 589824 | tf_op jit(solution)/shard_map/all_to_all | solution.py:279

commit v4 on v2

--- a/solution.py
+++ b/solution.py
@@ -4,6 +4,7 @@
 import jax.numpy as jnp
 from jax import lax
 from jax.experimental import pallas as pl
+from jax.experimental.layout import Layout, with_layout_constraint
 from jax.experimental.pallas import tpu as pltpu
 from jax.sharding import Mesh
 from jax.sharding import PartitionSpec as P
@@ -13,6 +14,7 @@
 BF16 = jnp.bfloat16
 SIDE = 4
 CORES = 2
+RING = SIDE * SIDE
 TO = ("x", "hi", "y")
 WEIGHT_SLICES = 8
 C0 = 0.7978845608028654
@@ -29,6 +31,10 @@
 
 def tn(a, b):
     return lax.dot_general(a, b, (((0,), (0,)), ((), ())), preferred_element_type=F32)
+
+
+def row_major(x):
+    return with_layout_constraint(x, Layout(major_to_minor=tuple(range(x.ndim))))
 
 
 def swap(x, axis=0):
@@ -43,6 +49,11 @@
         x.reshape(blocks, x.shape[0] // blocks, x.shape[1]), TO, split_axis=0, concat_axis=0, tiled=True
     )
     return out.reshape(x.shape)
+
+
+def along_z(x, step):
+    at = [(z % SIDE) * SIDE + z // SIDE for z in range(RING)]
+    return lax.ppermute(x, ("lo", "hi"), [(at[z], at[(z + step) % RING]) for z in range(RING)])
 
 
 def shift(x, axis, step):
@@ -136,9 +147,7 @@
     y, x = lax.axis_index("y"), lax.axis_index("x")
     place = (y * 2 + lax.rem(x, 2), x * 2 + lax.rem(y, 2))
     piece = jnp.stack([lax.dynamic_index_in_dim(slabs[i], place[i], axis=1, keepdims=False) for i in (0, 1)])
-    column = lax.all_to_all(
-        jnp.broadcast_to(piece[None], (SIDE, *piece.shape)), "lo", split_axis=0, concat_axis=0, tiled=True
-    )
+    column = jnp.stack([along_z(piece, step) for step in (1, -1, 2)], axis=2)
     return slabs, column
 
 
@@ -156,10 +165,7 @@
             out_ref[i, :, pl.ds(second, 3)] = piece_ref[1]
 
 
-def weight_pairs(column):
-    lo = lax.axis_index("lo")
-    others = lax.dynamic_slice_in_dim(jnp.concatenate([column, column]), lo + 1, SIDE - 1, axis=0)
-    others = jnp.moveaxis(others, 0, 2)
+def weight_pairs(others):
     diagonal = [((y * SIDE + x), ((y ^ 1) * SIDE + (x ^ 1))) for y in range(SIDE) for x in range(SIDE)]
     twin = lax.ppermute(others, ("y", "x"), diagonal)
     return jnp.stack([others, twin], axis=1)
@@ -182,36 +188,16 @@
     return half, lax.ppermute(half, "core", [(0, 1), (1, 0)])
 
 
-def mix_kernel(two_ref, x_ref, out_ref):
-    out_ref[...] = nn(two_ref[...], x_ref[...]).astype(BF16)
-
-
-def mix(two, x):
-    rows, channels = x.shape
-    cols = pl.BlockSpec((rows, channels // 2), lambda i: (0, i))
-    return pl.pallas_call(
-        mix_kernel,
-        grid=(2,),
-        in_specs=[pl.BlockSpec(two.shape, lambda i: (0, 0)), cols],
-        out_specs=cols,
-        out_shape=jax.ShapeDtypeStruct(x.shape, BF16),
-        cost_estimate=pl.CostEstimate(
-            flops=2 * rows * rows * channels, transcendentals=0, bytes_accessed=4 * rows * channels + 2 * rows * rows
-        ),
-    )(two, x)
-
-
 def layer(inputs, cotangent, factor_one, factor_two, up_weight, down_weight):
     block = factor_one.shape[1]
     own_p, blocks, _ = factor_two.shape
     n_dp = SIDE * CORES
     x_nat = inputs[0]
 
-    slabs, column = weight_column(up_weight, down_weight)
     one = swap(factor_one[0])
     mixed_one = nn(one, x_nat).astype(BF16)
-    mixed_one, column = lax.optimization_barrier((mixed_one, column))
     cols_one = exchange(mixed_one, blocks)
+    slabs, column = weight_column(up_weight, down_weight)
 
     at = lax.broadcasted_iota(jnp.int32, (blocks, block), 1) // own_p
     at = lax.rem(at, SIDE) * SIDE**2 + lax.rem(at // SIDE, SIDE) * SIDE + at // SIDE**2
@@ -223,14 +209,12 @@
         return jnp.where(lax.rem(row, own_p) == lax.rem(col, own_p), full, 0.0).astype(BF16)
 
     by_q = swap(jnp.transpose(factor_two, (1, 0, 2))).reshape(block, blocks)
-    two = diagonal(nn(by_q, pick))
-    two_t = two.T
-    pairs = weight_pairs(column)
+    two = row_major(diagonal(nn(by_q, pick)))
     x_all, cot_all = swap(x_nat), swap(cotangent[0])
-    cols_one, _, two, two_t, x_all, cot_all = lax.optimization_barrier((cols_one, pairs, two, two_t, x_all, cot_all))
-
-    weights = weight_halves(slabs, pairs)
-    mixed_two = mix(two, cols_one)
+    cols_one, two, x_all, cot_all = lax.optimization_barrier((cols_one, two, x_all, cot_all))
+
+    weights = weight_halves(slabs, weight_pairs(column))
+    mixed_two = nn(two, cols_one).astype(BF16)
     mixed = exchange(mixed_two, blocks)
 
     grad_two, grad_gated = mlp_call(grads_kernel, (mixed, x_all, cot_all), weights, (BF16, F32), 3)
@@ -241,7 +225,7 @@
     gate_in = swap(jax.vjp(jax.nn.silu, x_all.astype(F32))[1](grad_gated * mixed.astype(F32))[0])
     grad_cols, outputs, gate_in = lax.optimization_barrier((grad_cols, outputs, gate_in))
 
-    grad_one = exchange(mix(two_t, grad_cols), blocks)
+    grad_one = exchange(tn(two, grad_cols).astype(BF16), blocks)
 
     term_two = nt(diagonal(nt(grad_cols, cols_one)), pick).astype(BF16)
     term_two = swap(term_two.reshape(blocks, own_p * blocks)).reshape(n_dp, -1, block)

time: 275 us -> 273 us (level)
  starting transfers between devices: 95.7 us -> 141 us
  waiting for transfers between devices: 122 us -> 77.5 us
  matrix products: 7.65 us -> 14 us
  Pallas kernels: 27.3 us -> 21.5 us
  local copies, waits for them, and re-layouts: 14.8 us -> 10.9 us
    all_to_all x4, waiting for transfers between devices: 102 us -> 33.4 us  [exchange(): lax.all_to_all(x.reshape(blocks, x.shape[0] // blocks, x.shape[1]), TO, s...]
    ppermute x1, starting transfers between devices: 2.5 us -> 40.7 us  [layer(): lax.ppermute(lax.dynamic_index_in_dim(terms, 1 - core, axis=1, keepdims=F...]
    ppermute x0 -> x3, waiting for transfers between devices: none -> 29 us  [along_z(): lax.ppermute(x, ('lo', 'hi'), [(at[z], at[(z + step) % RING]) for z in ra...]
    ppermute x0 -> x3, starting transfers between devices: none -> 9.47 us  [along_z(): lax.ppermute(x, ('lo', 'hi'), [(at[z], at[(z + step) % RING]) for z in ra...]
    all_to_all x1 -> x0, starting transfers between devices: 6.43 us -> none  [weight_column(): lax.all_to_all(jnp.broadcast_to(piece[None], (SIDE, *piece.shape)), 'lo',...]
    pallas_call x2 -> x0, Pallas kernels: 5.71 us -> none  [mix(): pl.pallas_call(mix_kernel, grid=(2,), in_specs=[pl.BlockSpec(two.shape, l...]
    dot_general x2 -> x3, matrix products: 1.8 us -> 6.57 us  [nn(): lax.dot_general(a, b, (((1,), (0,)), ((), ())), preferred_element_type=F32)]
    all_to_all x1 -> x0, waiting for transfers between devices: 3.57 us -> none  [weight_column(): lax.all_to_all(jnp.broadcast_to(piece[None], (SIDE, *piece.shape)), 'lo',...]
  transfers between devices with their start and end apart: 15 -> 17, of which waited for: 8 -> 9; matrix products, arithmetic and copies ran while one was open for 6% -> 6% of each run, Pallas kernels for 5% -> 4%
where the time goes in v4:
time: 273 us; the launch traced here: 270 us
  starting transfers between devices  141 us (52%)
  waiting for transfers between devices  77.5 us (28%)
  Pallas kernels  21.5 us (8%)
  matrix products  14 us (5%)
  local copies, waits for them, and re-layouts  10.9 us (4%)
  other arithmetic  3.87 us (1%)
    all_to_all x4, starting transfers between devices, exchange(): lax.all_to_all(x.reshape(blocks, x.shape[0] // blocks, x.shape[1]), TO, s...  55.2 us
    ppermute x1, starting transfers between devices, layer(): lax.ppermute(lax.dynamic_index_in_dim(terms, 1 - core, axis=1, keepdims=F...  40.7 us
    all_to_all x4, waiting for transfers between devices, exchange(): lax.all_to_all(x.reshape(blocks, x.shape[0] // blocks, x.shape[1]), TO, s...  33.4 us
    ppermute x3, waiting for transfers between devices, along_z(): lax.ppermute(x, ('lo', 'hi'), [(at[z], at[(z + step) % RING]) for z in ra...  29 us
    ppermute x6, starting transfers between devices, shift(): return lax.ppermute(x, axis, [(i, (i + step) % SIDE) for i in range(SIDE)])  20.9 us
    pallas_call x2, Pallas kernels, mlp_call(): pl.pallas_call(kernel, grid=(groups, len(weights)), in_specs=[cols] * len...  18.1 us
    ppermute x3, starting transfers between devices, along_z(): lax.ppermute(x, ('lo', 'hi'), [(at[z], at[(z + step) % RING]) for z in ra...  9.47 us
    dot_general x3, matrix products, nn(): lax.dot_general(a, b, (((1,), (0,)), ((), ())), preferred_element_type=F32)  6.57 us
  transfers between devices with their start and end apart: 17, of which 9 were waited for; matrix products, arithmetic and copies ran while one was open for 6% of the time, Pallas kernels for 4%

profile of v4, /device:TPU:1, one launch (start us, length us, event | category | flops | bytes accessed | tf_op | source)
XLA Modules:
  0.0 269.7 jit_solution(13247302872465312185)
XLA Ops:
  0.6 1.1 copy.36
  1.7 0.8 copy-done.4
  2.5 2.7 fusion.8
  5.2 21.7 %all-to-all-start = ((bf16[64,8,768]{2,1,0:T(8,128)(2,1)}), bf16[64,8,768]{2,1,0:T(8,128)(2,1)S(1)}, u32[]{:S(2)}, u32[]{:S(2)}) async-start(bf16[64,8,768]{2,1,0:T(8,128)(2,1)} %fusion.8), calls=%async_computation | async-start | bytes 1572864 | tf_op jit(solution)/shard_map/all_to_all | solution.py:48
  27.0 3.2 %collective-permute-start.2 = (bf16[2,2,24,384]{3,2,1,0:T(8,128)(2,1)S(1)}, bf16[2,2,24,384]{3,2,1,0:T(8,128)(2,1)S(1)}, u32[]{:S(2)}, u32[]{:S(2)}) collective-permute-start(bf16[2,2,24,384]{3,2,1,0:T(8,128)(2,1)S(1)} %pad_maximum_fusion.3), channel_id=1, source_target_pairs={{0,256},{128,384},{256,4},{384,132},{4,260},{132,388},{260,8},{388... | collective-permute-start | bytes 221192 | tf_op jit(solution)/shard_map/ppermute | solution.py:56
  30.3 4.3 %collective-permute-start.1 = (bf16[2,2,24,384]{3,2,1,0:T(8,128)(2,1)S(1)}, bf16[2,2,24,384]{3,2,1,0:T(8,128)(2,1)S(1)}, u32[]{:S(2)}, u32[]{:S(2)}) collective-permute-start(bf16[2,2,24,384]{3,2,1,0:T(8,128)(2,1)S(1)} %pad_maximum_fusion.3), channel_id=1, source_target_pairs={{0,396},{128,0},{256,128},{384,256},{4,384},{132,4},{260,132},{388... | collective-permute-start | bytes 221192 | tf_op jit(solution)/shard_map/ppermute | solution.py:56
  34.6 1.9 collective-permute-start
  36.7 1.1 fusion.12
  37.8 1.0 copy.38
  38.8 1.0 copy.39
  39.8 27.2 %collective-permute-done.2 = bf16[2,2,24,384]{3,2,1,0:T(8,128)(2,1)S(1)} collective-permute-done((bf16[2,2,24,384]{3,2,1,0:T(8,128)(2,1)S(1)}, bf16[2,2,24,384]{3,2,1,0:T(8,128)(2,1)S(1)}, u32[]{:S(2)}, u32[]{:S(2)}) %collective-permute-start.2) | collective-permute-done | bytes 73760 | tf_op jit(solution)/shard_map/ppermute | solution.py:56
  67.0 1.8 collective-permute-done
  68.8 4.2 %collective-permute-start.3 = (bf16[2,2,3,24,384]{4,3,2,1,0:T(8,128)(2,1)S(1)}, bf16[2,2,3,24,384]{4,3,2,1,0:T(8,128)(2,1)S(1)}, u32[]{:S(2)}, u32[]{:S(2)}) collective-permute-start(bf16[2,2,3,24,384]{4,3,2,1,0:T(8,128)(2,1)S(1)} %get-tuple-element.40), channel_id=1, source_target_pairs={{0,17},{1,16},{2,19},{3,18},{16,1},{17,0},{18,3},{19,2},{32,49},{3... | collective-permute-start | bytes 663560 | tf_op jit(solution)/shard_map/ppermute | solution.py:170
  73.1 2.8 %fusion.9 = bf16[64,8,768]{2,1,0:T(8,128)(2,1)} fusion(bf16[512,512]{1,0:T(8,128)(2,1)} %fusion.12, bf16[512,768]{1,0:T(8,128)(2,1)S(1)} %bitcast.137), kind=kOutput, calls=%fused_computation.18 | convolution fusion | flops 403046400 | bytes 2097152 | tf_op jit(solution)/shard_map/dot_general | solution.py:29
  75.8 12.4 %all-to-all-start.1 = ((bf16[64,8,768]{2,1,0:T(8,128)(2,1)}), bf16[64,8,768]{2,1,0:T(8,128)(2,1)S(1)}, u32[]{:S(2)}, u32[]{:S(2)}) async-start(bf16[64,8,768]{2,1,0:T(8,128)(2,1)} %fusion.9), calls=%async_computation.1 | async-start | bytes 1572864 | tf_op jit(solution)/shard_map/all_to_all | solution.py:48
  88.3 2.9 %collective-permute-start.4 = (bf16[2,2,3,24,384]{4,3,2,1,0:T(8,128)(2,1)S(1)}, bf16[2,2,3,24,384]{4,3,2,1,0:T(8,128)(2,1)S(1)}, u32[]{:S(2)}, u32[]{:S(2)}) collective-permute-start(bf16[2,2,3,24,384]{4,3,2,1,0:T(8,128)(2,1)S(1)} %get-tuple-element.39.refs_0_), channel_id=1, source_target_pairs={{0,16},{16,32},{32,48},{48,0},{1,17},{17,33},{33,49},{49,1},{2,18}... | collective-permute-start | bytes 663560 | tf_op jit(solution)/shard_map/ppermute | solution.py:60
  91.2 4.3 %collective-permute-start.5 = (bf16[2,2,3,24,384]{4,3,2,1,0:T(8,128)(2,1)S(1)}, bf16[2,2,3,24,384]{4,3,2,1,0:T(8,128)(2,1)S(1)}, u32[]{:S(2)}, u32[]{:S(2)}) collective-permute-start(bf16[2,2,3,24,384]{4,3,2,1,0:T(8,128)(2,1)S(1)} %get-tuple-element.39.refs_0_), channel_id=1, source_target_pairs={{0,32},{16,48},{32,0},{48,16},{1,33},{17,49},{33,1},{49,17},{2,34}... | collective-permute-start | bytes 663560 | tf_op jit(solution)/shard_map/ppermute | solution.py:60
  95.6 3.1 %collective-permute-start.6 = (bf16[2,2,3,24,384]{4,3,2,1,0:T(8,128)(2,1)S(1)}, bf16[2,2,3,24,384]{4,3,2,1,0:T(8,128)(2,1)S(1)}, u32[]{:S(2)}, u32[]{:S(2)}) collective-permute-start(bf16[2,2,3,24,384]{4,3,2,1,0:T(8,128)(2,1)S(1)} %get-tuple-element.39.refs_0_), channel_id=1, source_target_pairs={{0,48},{16,0},{32,16},{48,32},{1,49},{17,1},{33,17},{49,33},{2,50}... | collective-permute-start | bytes 663560 | tf_op jit(solution)/shard_map/ppermute | solution.py:60
  98.7 3.1 %collective-permute-start.7 = (bf16[2,2,3,24,384]{4,3,2,1,0:T(8,128)(2,1)S(1)}, bf16[2,2,3,24,384]{4,3,2,1,0:T(8,128)(2,1)S(1)}, u32[]{:S(2)}, u32[]{:S(2)}) collective-permute-start(bf16[2,2,3,24,384]{4,3,2,1,0:T(8,128)(2,1)S(1)} %get-tuple-element.38.refs_4_), channel_id=1, source_target_pairs={{0,1},{1,2},{2,3},{3,0},{4,5},{5,6},{6,7},{7,4},{8,9},{9,10},{10,1... | collective-permute-start | bytes 663560 | tf_op jit(solution)/shard_map/ppermute | solution.py:60
  101.8 4.5 %collective-permute-start.8 = (bf16[2,2,3,24,384]{4,3,2,1,0:T(8,128)(2,1)S(1)}, bf16[2,2,3,24,384]{4,3,2,1,0:T(8,128)(2,1)S(1)}, u32[]{:S(2)}, u32[]{:S(2)}) collective-permute-start(bf16[2,2,3,24,384]{4,3,2,1,0:T(8,128)(2,1)S(1)} %get-tuple-element.38.refs_4_), channel_id=1, source_target_pairs={{0,2},{1,3},{2,0},{3,1},{4,6},{5,7},{6,4},{7,5},{8,10},{9,11},{10,... | collective-permute-start | bytes 663560 | tf_op jit(solution)/shard_map/ppermute | solution.py:60
  106.3 3.0 %collective-permute-start.9 = (bf16[2,2,3,24,384]{4,3,2,1,0:T(8,128)(2,1)S(1)}, bf16[2,2,3,24,384]{4,3,2,1,0:T(8,128)(2,1)}, u32[]{:S(2)}, u32[]{:S(2)}) collective-permute-start(bf16[2,2,3,24,384]{4,3,2,1,0:T(8,128)(2,1)S(1)} %get-tuple-element.38.refs_4_), channel_id=1, source_target_pairs={{0,3},{1,0},{2,1},{3,2},{4,7},{5,4},{6,5},{7,6},{8,11},{9,8},{10,9... | collective-permute-start | bytes 663560 | tf_op jit(solution)/shard_map/ppermute | solution.py:60
  109.3 0.7 pad_add_fusion.at_ref
  109.9 0.9 pad_maximum_fusion.slabs_ref
  110.9 3.7 %collective-permute-done.8.refs_6_ = bf16[2,2,3,24,384]{4,3,2,1,0:T(8,128)(2,1)S(1)} collective-permute-done((bf16[2,2,3,24,384]{4,3,2,1,0:T(8,128)(2,1)S(1)}, bf16[2,2,3,24,384]{4,3,2,1,0:T(8,128)(2,1)S(1)}, u32[]{:S(2)}, u32[]{:S(2)}) %collective-permute-start.8) | collective-permute-done | bytes 221216 | tf_op jit(solution)/shard_map/ppermute | solution.py:60
  114.6 0.7 copy-done.18
  115.3 1.2 collective-permute-done.9.refs_7_
  116.5 3.4 %assemble.1 = bf16[2,2,32,24,384]{4,3,2,1,0:T(8,128)(2,1)} custom-call(s32[2]{0:T(128)} %pad_add_fusion.at_ref, bf16[2,2,8,24,384]{4,3,2,1,0:T(8,128)(2,1)} %pad_maximum_fusion.slabs_ref, bf16[2,2,3,24,384]{4,3,2,1,0:T(8,128)(2,1)} %copy-done.7, bf16[2,2,3,24,384]{4,3,2,1,0:T(8,128)(2,1)} %copy-done.14, bf16[2,2,3,24,384]{4,3,2,1,0:T(8,128)(2,1)} %copy-done.15, ...), custom_call_target="tpu_custom_call" | custom-call | bytes 4718592 | tf_op jit(solution)/shard_map/assemble/pallas_call | solution.py:179
  119.9 4.2 %collective-permute-start.10 = (bf16[2,2,768,384]{3,2,1,0:T(8,128)(2,1)}, bf16[2,2,768,384]{3,2,1,0:T(8,128)(2,1)}, u32[]{:S(2)}, u32[]{:S(2)}) collective-permute-start(bf16[2,2,768,384]{3,2,1,0:T(8,128)(2,1)} %bitcast.130), channel_id=1, source_target_pairs={{0,64},{64,0},{1,65},{65,1},{2,66},{66,2},{3,67},{67,3},{4,68},{68... | collective-permute-start | bytes 7077896 | tf_op jit(solution)/shard_map/ppermute | solution.py:188
  124.1 4.5 %collective-permute-done.10.other_ref = bf16[2,2,768,384]{3,2,1,0:T(8,128)(2,1)} collective-permute-done((bf16[2,2,768,384]{3,2,1,0:T(8,128)(2,1)}, bf16[2,2,768,384]{3,2,1,0:T(8,128)(2,1)}, u32[]{:S(2)}, u32[]{:S(2)}) %collective-permute-start.10) | collective-permute-done | bytes 2359328 | tf_op jit(solution)/shard_map/ppermute | solution.py:188
  128.5 0.9 copy-done.1
  129.4 10.1 %shard_map.93 = (bf16[512,768]{1,0:T(8,128)(2,1)}, f32[512,768]{1,0:T(8,128)}) custom-call(bf16[512,768]{1,0:T(8,128)(2,1)} %bitcast.126, bf16[512,768]{1,0:T(8,128)(2,1)} %bitcast.123, bf16[512,768]{1,0:T(8,128)(2,1)} %bitcast.140, bf16[2,2,768,384]{3,2,1,0:T(8,128)(2,1)} %bitcast.131, bf16[2,2,768,384]{3,2,1,0:T(8,128)(2,1)} %collective-permute-done.10.other_ref), custom_call_target="tpu_custom_call" | custom-call | flops 3623878656 | bytes 7077888 | tf_op jit(solution)/shard_map/pallas_call | solution.py:129
  139.5 13.7 %all-to-all-start.2 = ((bf16[64,8,768]{2,1,0:T(8,128)(2,1)}), bf16[64,8,768]{2,1,0:T(8,128)(2,1)S(1)}, u32[]{:S(2)}, u32[]{:S(2)}) async-start(bf16[64,8,768]{2,1,0:T(8,128)(2,1)} %bitcast.143), calls=%async_computation.2 | async-start | bytes 1572864 | tf_op jit(solution)/shard_map/all_to_all | solution.py:48
  153.2 8.1 %shard_map.94 = bf16[512,768]{1,0:T(8,128)(2,1)} custom-call(bf16[512,768]{1,0:T(8,128)(2,1)} %bitcast.127, bf16[512,768]{1,0:T(8,128)(2,1)} %bitcast.124, bf16[2,2,768,384]{3,2,1,0:T(8,128)(2,1)} %bitcast.132, bf16[2,2,768,384]{3,2,1,0:T(8,128)(2,1)} %collective-permute-done.10.other_ref), custom_call_target="tpu_custom_call" | custom-call | flops 2415919104 | bytes 6291456 | tf_op jit(solution)/shard_map/pallas_call | solution.py:129
  161.2 2.2 copy.45
  163.5 0.7 fusion.4
  164.3 14.6 %all-to-all-done.2 = bf16[64,8,768]{2,1,0:T(8,128)(2,1)S(1)} async-done(((bf16[64,8,768]{2,1,0:T(8,128)(2,1)}), bf16[64,8,768]{2,1,0:T(8,128)(2,1)S(1)}, u32[]{:S(2)}, u32[]{:S(2)}) %all-to-all-start.2) | async-done | bytes 786464 | tf_op jit(solution)/shard_map/all_to_all | solution.py:48
  178.9 2.8 %fusion.10 = bf16[64,8,768]{2,1,0:T(8,128)(2,1)} fusion(bf16[512,512]{1,0:T(8,128)(2,1)} %fusion.12, bf16[512,768]{1,0:T(8,128)(2,1)S(1)} %bitcast.141), kind=kOutput, calls=%fused_computation.19 | convolution fusion | flops 403046400 | bytes 2097152 | tf_op jit(solution)/shard_map/dot_general | solution.py:33
  181.7 7.4 %all-to-all-start.3 = ((bf16[64,8,768]{2,1,0:T(8,128)(2,1)}), bf16[64,8,768]{2,1,0:T(8,128)(2,1)S(1)}, u32[]{:S(2)}, u32[]{:S(2)}) async-start(bf16[64,8,768]{2,1,0:T(8,128)(2,1)} %fusion.10), calls=%async_computation.3 | async-start | bytes 1572864 | tf_op jit(solution)/shard_map/all_to_all | solution.py:48
  189.1 2.2 fusion.14
  191.7 18.8 %all-to-all-done.3 = bf16[64,8,768]{2,1,0:T(8,128)(2,1)S(1)} async-done(((bf16[64,8,768]{2,1,0:T(8,128)(2,1)}), bf16[64,8,768]{2,1,0:T(8,128)(2,1)S(1)}, u32[]{:S(2)}, u32[]{:S(2)}) %all-to-all-start.3) | async-done | bytes 786464 | tf_op jit(solution)/shard_map/all_to_all | solution.py:48
  211.4 40.7 %collective-permute-start.11 = (bf16[4,72,512]{2,1,0:T(8,128)(2,1)S(1)}, bf16[4,72,512]{2,1,0:T(8,128)(2,1)S(1)}, u32[]{:S(2)}, u32[]{:S(2)}) collective-permute-start(bf16[4,72,512]{2,1,0:T(8,128)(2,1)S(1)} %fusion.22), channel_id=1, source_target_pairs={{0,64},{64,0},{1,65},{65,1},{2,66},{66,2},{3,67},{67,3},{4,68},{68... | collective-permute-start | bytes 884744 | tf_op jit(solution)/shard_map/ppermute | solution.py:239
  252.2 1.2 collective-permute-done.11
  253.4 0.8 fusion.17
  254.2 6.0 %all-to-all-start.4 = ((bf16[4,72,512]{2,1,0:T(8,128)(2,1)}), bf16[4,72,512]{2,1,0:T(8,128)(2,1)S(1)}, u32[]{:S(2)}, u32[]{:S(2)}) async-start(bf16[4,72,512]{2,1,0:T(8,128)(2,1)} %fusion.17), calls=%async_computation.4 | async-start | bytes 589824 | tf_op jit(solution)/shard_map/all_to_all | solution.py:241
  260.7 1.9 fusion.11
  262.6 1.2 copy.51
  263.7 4.6 %all-to-all-done.4 = bf16[4,72,512]{2,1,0:T(8,128)(2,1)S(1)} async-done(((bf16[4,72,512]{2,1,0:T(8,128)(2,1)}), bf16[4,72,512]{2,1,0:T(8,128)(2,1)S(1)}, u32[]{:S(2)}, u32[]{:S(2)}) %all-to-all-start.4) | async-done | bytes 294944 | tf_op jit(solution)/shard_map/all_to_all | solution.py:241
  269.0 0.7 convert_reduce_fusion
  (65 shorter events, 2.9 us)
Async XLA Ops:
  1.7 0.8 copy-start.4
  2.5 24.4 %copy-start.12 = (bf16[2,192,384]{2,1,0:T(8,128)(2,1)S(1)}, bf16[2,192,384]{2,1,0:T(8,128)(2,1)}, u32[]{:S(2)}) copy-start(bf16[2,192,384]{2,1,0:T(8,128)(2,1)} %param.11) | copy-start | bytes 884740
  2.5 24.4 %copy-start.13 = (bf16[2,384,192]{1,2,0:T(8,128)(2,1)S(1)}, bf16[2,384,192]{1,2,0:T(8,128)(2,1)}, u32[]{:S(2)}) copy-start(bf16[2,384,192]{1,2,0:T(8,128)(2,1)} %param.10) | copy-start | bytes 884740
  2.5 34.0 %copy-start.19 = (bf16[8,64,64]{2,1,0:T(8,128)(2,1)S(1)}, bf16[8,64,64]{2,1,0:T(8,128)(2,1)}, u32[]{:S(2)}) copy-start(bf16[8,64,64]{2,1,0:T(8,128)(2,1)} %param.9) | copy-start | bytes 196612
  5.2 67.9 %all-to-all-start = ((bf16[64,8,768]{2,1,0:T(8,128)(2,1)}), bf16[64,8,768]{2,1,0:T(8,128)(2,1)S(1)}, u32[]{:S(2)}, u32[]{:S(2)}) async-start(bf16[64,8,768]{2,1,0:T(8,128)(2,1)} %fusion.8), calls=%async_computation | async-start | bytes 1572864 | tf_op jit(solution)/shard_map/all_to_all | solution.py:48
  26.9 10.9 %copy-start.9 = (bf16[1,512,768]{2,1,0:T(8,128)(2,1)S(1)}, bf16[1,512,768]{2,1,0:T(8,128)(2,1)}, u32[]{:S(2)}) copy-start(bf16[1,512,768]{2,1,0:T(8,128)(2,1)} %param.6) | copy-start | bytes 2359300
  27.0 40.0 %collective-permute-start.2 = (bf16[2,2,24,384]{3,2,1,0:T(8,128)(2,1)S(1)}, bf16[2,2,24,384]{3,2,1,0:T(8,128)(2,1)S(1)}, u32[]{:S(2)}, u32[]{:S(2)}) collective-permute-start(bf16[2,2,24,384]{3,2,1,0:T(8,128)(2,1)S(1)} %pad_maximum_fusion.3), channel_id=1, source_target_pairs={{0,256},{128,384},{256,4},{384,132},{4,260},{132,388},{260,8},{388... | collective-permute-start | bytes 221192 | tf_op jit(solution)/shard_map/ppermute | solution.py:56
  30.3 36.7 %collective-permute-start.1 = (bf16[2,2,24,384]{3,2,1,0:T(8,128)(2,1)S(1)}, bf16[2,2,24,384]{3,2,1,0:T(8,128)(2,1)S(1)}, u32[]{:S(2)}, u32[]{:S(2)}) collective-permute-start(bf16[2,2,24,384]{3,2,1,0:T(8,128)(2,1)S(1)} %pad_maximum_fusion.3), channel_id=1, source_target_pairs={{0,396},{128,0},{256,128},{384,256},{4,384},{132,4},{260,132},{388... | collective-permute-start | bytes 221192 | tf_op jit(solution)/shard_map/ppermute | solution.py:56
  34.6 34.2 %collective-permute-start = (bf16[2,2,24,384]{3,2,1,0:T(8,128)(2,1)S(1)}, bf16[2,2,24,384]{3,2,1,0:T(8,128)(2,1)S(1)}, u32[]{:S(2)}, u32[]{:S(2)}) collective-permute-start(bf16[2,2,24,384]{3,2,1,0:T(8,128)(2,1)S(1)} %pad_maximum_fusion.3), channel_id=1, source_target_pairs={{0,128},{128,256},{256,384},{384,4},{4,132},{132,260},{260,388},{3... | collective-permute-start | bytes 221192 | tf_op jit(solution)/shard_map/ppermute | solution.py:56
  36.6 2.2 copy-start.8
  68.8 19.4 %collective-permute-start.3 = (bf16[2,2,3,24,384]{4,3,2,1,0:T(8,128)(2,1)S(1)}, bf16[2,2,3,24,384]{4,3,2,1,0:T(8,128)(2,1)S(1)}, u32[]{:S(2)}, u32[]{:S(2)}) collective-permute-start(bf16[2,2,3,24,384]{4,3,2,1,0:T(8,128)(2,1)S(1)} %get-tuple-element.40), channel_id=1, source_target_pairs={{0,17},{1,16},{2,19},{3,18},{16,1},{17,0},{18,3},{19,2},{32,49},{3... | collective-permute-start | bytes 663560 | tf_op jit(solution)/shard_map/ppermute | solution.py:170
  73.1 2.8 %copy-start.10 = (bf16[64,8,768]{2,1,0:T(8,128)(2,1)}, bf16[64,8,768]{2,1,0:T(8,128)(2,1)S(1)}, u32[]{:S(2)}) copy-start(bf16[64,8,768]{2,1,0:T(8,128)(2,1)S(1)} %all-to-all-done) | copy-start | bytes 2359300
  75.8 52.7 %all-to-all-start.1 = ((bf16[64,8,768]{2,1,0:T(8,128)(2,1)}), bf16[64,8,768]{2,1,0:T(8,128)(2,1)S(1)}, u32[]{:S(2)}, u32[]{:S(2)}) async-start(bf16[64,8,768]{2,1,0:T(8,128)(2,1)} %fusion.9), calls=%async_computation.1 | async-start | bytes 1572864 | tf_op jit(solution)/shard_map/all_to_all | solution.py:48
  88.3 28.2 %copy-start.6 = (bf16[2,2,3,24,384]{4,3,2,1,0:T(8,128)(2,1)}, bf16[2,2,3,24,384]{4,3,2,1,0:T(8,128)(2,1)S(1)}, u32[]{:S(2)}) copy-start(bf16[2,2,3,24,384]{4,3,2,1,0:T(8,128)(2,1)S(1)} %get-tuple-element.38.refs_4_) | copy-start | bytes 663556
  88.3 28.2 %copy-start.7 = (bf16[2,2,3,24,384]{4,3,2,1,0:T(8,128)(2,1)}, bf16[2,2,3,24,384]{4,3,2,1,0:T(8,128)(2,1)S(1)}, u32[]{:S(2)}) copy-start(bf16[2,2,3,24,384]{4,3,2,1,0:T(8,128)(2,1)S(1)} %get-tuple-element.39.refs_0_) | copy-start | bytes 663556
  88.3 18.0 %collective-permute-start.4 = (bf16[2,2,3,24,384]{4,3,2,1,0:T(8,128)(2,1)S(1)}, bf16[2,2,3,24,384]{4,3,2,1,0:T(8,128)(2,1)S(1)}, u32[]{:S(2)}, u32[]{:S(2)}) collective-permute-start(bf16[2,2,3,24,384]{4,3,2,1,0:T(8,128)(2,1)S(1)} %get-tuple-element.39.refs_0_), channel_id=1, source_target_pairs={{0,16},{16,32},{32,48},{48,0},{1,17},{17,33},{33,49},{49,1},{2,18}... | collective-permute-start | bytes 663560 | tf_op jit(solution)/shard_map/ppermute | solution.py:60
  91.2 19.6 %collective-permute-start.5 = (bf16[2,2,3,24,384]{4,3,2,1,0:T(8,128)(2,1)S(1)}, bf16[2,2,3,24,384]{4,3,2,1,0:T(8,128)(2,1)S(1)}, u32[]{:S(2)}, u32[]{:S(2)}) collective-permute-start(bf16[2,2,3,24,384]{4,3,2,1,0:T(8,128)(2,1)S(1)} %get-tuple-element.39.refs_0_), channel_id=1, source_target_pairs={{0,32},{16,48},{32,0},{48,16},{1,33},{17,49},{33,1},{49,17},{2,34}... | collective-permute-start | bytes 663560 | tf_op jit(solution)/shard_map/ppermute | solution.py:60
  95.6 15.3 %collective-permute-start.6 = (bf16[2,2,3,24,384]{4,3,2,1,0:T(8,128)(2,1)S(1)}, bf16[2,2,3,24,384]{4,3,2,1,0:T(8,128)(2,1)S(1)}, u32[]{:S(2)}, u32[]{:S(2)}) collective-permute-start(bf16[2,2,3,24,384]{4,3,2,1,0:T(8,128)(2,1)S(1)} %get-tuple-element.39.refs_0_), channel_id=1, source_target_pairs={{0,48},{16,0},{32,16},{48,32},{1,49},{17,1},{33,17},{49,33},{2,50}... | collective-permute-start | bytes 663560 | tf_op jit(solution)/shard_map/ppermute | solution.py:60
  98.7 12.2 %collective-permute-start.7 = (bf16[2,2,3,24,384]{4,3,2,1,0:T(8,128)(2,1)S(1)}, bf16[2,2,3,24,384]{4,3,2,1,0:T(8,128)(2,1)S(1)}, u32[]{:S(2)}, u32[]{:S(2)}) collective-permute-start(bf16[2,2,3,24,384]{4,3,2,1,0:T(8,128)(2,1)S(1)} %get-tuple-element.38.refs_4_), channel_id=1, source_target_pairs={{0,1},{1,2},{2,3},{3,0},{4,5},{5,6},{6,7},{7,4},{8,9},{9,10},{10,1... | collective-permute-start | bytes 663560 | tf_op jit(solution)/shard_map/ppermute | solution.py:60
  101.8 12.8 %collective-permute-start.8 = (bf16[2,2,3,24,384]{4,3,2,1,0:T(8,128)(2,1)S(1)}, bf16[2,2,3,24,384]{4,3,2,1,0:T(8,128)(2,1)S(1)}, u32[]{:S(2)}, u32[]{:S(2)}) collective-permute-start(bf16[2,2,3,24,384]{4,3,2,1,0:T(8,128)(2,1)S(1)} %get-tuple-element.38.refs_4_), channel_id=1, source_target_pairs={{0,2},{1,3},{2,0},{3,1},{4,6},{5,7},{6,4},{7,5},{8,10},{9,11},{10,... | collective-permute-start | bytes 663560 | tf_op jit(solution)/shard_map/ppermute | solution.py:60
  106.3 10.2 %copy-start.14 = (bf16[2,2,3,24,384]{4,3,2,1,0:T(8,128)(2,1)}, bf16[2,2,3,24,384]{4,3,2,1,0:T(8,128)(2,1)S(1)}, u32[]{:S(2)}) copy-start(bf16[2,2,3,24,384]{4,3,2,1,0:T(8,128)(2,1)S(1)} %collective-permute-done.4.refs_1_) | copy-start | bytes 663556
  106.3 10.2 %collective-permute-start.9 = (bf16[2,2,3,24,384]{4,3,2,1,0:T(8,128)(2,1)S(1)}, bf16[2,2,3,24,384]{4,3,2,1,0:T(8,128)(2,1)}, u32[]{:S(2)}, u32[]{:S(2)}) collective-permute-start(bf16[2,2,3,24,384]{4,3,2,1,0:T(8,128)(2,1)S(1)} %get-tuple-element.38.refs_4_), channel_id=1, source_target_pairs={{0,3},{1,0},{2,1},{3,2},{4,7},{5,4},{6,5},{7,6},{8,11},{9,8},{10,9... | collective-permute-start | bytes 663560 | tf_op jit(solution)/shard_map/ppermute | solution.py:60
  110.8 5.7 %copy-start.15 = (bf16[2,2,3,24,384]{4,3,2,1,0:T(8,128)(2,1)}, bf16[2,2,3,24,384]{4,3,2,1,0:T(8,128)(2,1)S(1)}, u32[]{:S(2)}) copy-start(bf16[2,2,3,24,384]{4,3,2,1,0:T(8,128)(2,1)S(1)} %collective-permute-done.5.refs_2_) | copy-start | bytes 663556
  110.8 5.7 %copy-start.16 = (bf16[2,2,3,24,384]{4,3,2,1,0:T(8,128)(2,1)}, bf16[2,2,3,24,384]{4,3,2,1,0:T(8,128)(2,1)S(1)}, u32[]{:S(2)}) copy-start(bf16[2,2,3,24,384]{4,3,2,1,0:T(8,128)(2,1)S(1)} %collective-permute-done.6.refs_3_) | copy-start | bytes 663556
  110.9 3.7 %copy-start.17 = (bf16[2,2,3,24,384]{4,3,2,1,0:T(8,128)(2,1)}, bf16[2,2,3,24,384]{4,3,2,1,0:T(8,128)(2,1)S(1)}, u32[]{:S(2)}) copy-start(bf16[2,2,3,24,384]{4,3,2,1,0:T(8,128)(2,1)S(1)} %collective-permute-done.7.refs_5_) | copy-start | bytes 663556
  114.6 0.7 copy-start.18
  119.9 8.7 %collective-permute-start.10 = (bf16[2,2,768,384]{3,2,1,0:T(8,128)(2,1)}, bf16[2,2,768,384]{3,2,1,0:T(8,128)(2,1)}, u32[]{:S(2)}, u32[]{:S(2)}) collective-permute-start(bf16[2,2,768,384]{3,2,1,0:T(8,128)(2,1)} %bitcast.130), channel_id=1, source_target_pairs={{0,64},{64,0},{1,65},{65,1},{2,66},{66,2},{3,67},{67,3},{4,68},{68... | collective-permute-start | bytes 7077896 | tf_op jit(solution)/shard_map/ppermute | solution.py:188
  128.5 0.9 copy-start.1
  139.5 39.4 %all-to-all-start.2 = ((bf16[64,8,768]{2,1,0:T(8,128)(2,1)}), bf16[64,8,768]{2,1,0:T(8,128)(2,1)S(1)}, u32[]{:S(2)}, u32[]{:S(2)}) async-start(bf16[64,8,768]{2,1,0:T(8,128)(2,1)} %bitcast.143), calls=%async_computation.2 | async-start | bytes 1572864 | tf_op jit(solution)/shard_map/all_to_all | solution.py:48
  153.2 10.3 %copy-start.5 = (f32[512,768]{1,0:T(8,128)S(1)}, f32[512,768]{1,0:T(8,128)}, u32[]{:S(2)}) copy-start(f32[512,768]{1,0:T(8,128)} %get-tuple-element.20) | copy-start | bytes 4718596
  161.2 2.2 copy-start
  161.2 2.2 copy-start.2
  178.9 2.8 %copy-start.11 = (bf16[64,8,768]{2,1,0:T(8,128)(2,1)}, bf16[64,8,768]{2,1,0:T(8,128)(2,1)S(1)}, u32[]{:S(2)}) copy-start(bf16[64,8,768]{2,1,0:T(8,128)(2,1)S(1)} %all-to-all-done.2) | copy-start | bytes 2359300
  181.7 28.8 %all-to-all-start.3 = ((bf16[64,8,768]{2,1,0:T(8,128)(2,1)}), bf16[64,8,768]{2,1,0:T(8,128)(2,1)S(1)}, u32[]{:S(2)}, u32[]{:S(2)}) async-start(bf16[64,8,768]{2,1,0:T(8,128)(2,1)} %fusion.10), calls=%async_computation.3 | async-start | bytes 1572864 | tf_op jit(solution)/shard_map/all_to_all | solution.py:48
  210.5 0.9 copy-start.3
  211.4 41.9 %collective-permute-start.11 = (bf16[4,72,512]{2,1,0:T(8,128)(2,1)S(1)}, bf16[4,72,512]{2,1,0:T(8,128)(2,1)S(1)}, u32[]{:S(2)}, u32[]{:S(2)}) collective-permute-start(bf16[4,72,512]{2,1,0:T(8,128)(2,1)S(1)} %fusion.22), channel_id=1, source_target_pairs={{0,64},{64,0},{1,65},{65,1},{2,66},{66,2},{3,67},{67,3},{4,68},{68... | collective-permute-start | bytes 884744 | tf_op jit(solution)/shard_map/ppermute | solution.py:239
  254.2 14.1 %all-to-all-start.4 = ((bf16[4,72,512]{2,1,0:T(8,128)(2,1)}), bf16[4,72,512]{2,1,0:T(8,128)(2,1)S(1)}, u32[]{:S(2)}, u32[]{:S(2)}) async-start(bf16[4,72,512]{2,1,0:T(8,128)(2,1)} %fusion.17), calls=%async_computation.4 | async-start | bytes 589824 | tf_op jit(solution)/shard_map/all_to_all | solution.py:241

commit v5 on v4

--- a/solution.py
+++ b/solution.py
@@ -14,7 +14,6 @@
 BF16 = jnp.bfloat16
 SIDE = 4
 CORES = 2
-RING = SIDE * SIDE
 TO = ("x", "hi", "y")
 WEIGHT_SLICES = 8
 C0 = 0.7978845608028654
@@ -49,11 +48,6 @@
         x.reshape(blocks, x.shape[0] // blocks, x.shape[1]), TO, split_axis=0, concat_axis=0, tiled=True
     )
     return out.reshape(x.shape)
-
-
-def along_z(x, step):
-    at = [(z % SIDE) * SIDE + z // SIDE for z in range(RING)]
-    return lax.ppermute(x, ("lo", "hi"), [(at[z], at[(z + step) % RING]) for z in range(RING)])
 
 
 def shift(x, axis, step):
@@ -147,7 +141,9 @@
     y, x = lax.axis_index("y"), lax.axis_index("x")
     place = (y * 2 + lax.rem(x, 2), x * 2 + lax.rem(y, 2))
     piece = jnp.stack([lax.dynamic_index_in_dim(slabs[i], place[i], axis=1, keepdims=False) for i in (0, 1)])
-    column = jnp.stack([along_z(piece, step) for step in (1, -1, 2)], axis=2)
+    column = lax.all_to_all(
+        jnp.broadcast_to(piece[None], (SIDE, *piece.shape)), "lo", split_axis=0, concat_axis=0, tiled=True
+    )
     return slabs, column
 
 
@@ -165,7 +161,10 @@
             out_ref[i, :, pl.ds(second, 3)] = piece_ref[1]
 
 
-def weight_pairs(others):
+def weight_pairs(column):
+    lo = lax.axis_index("lo")
+    others = lax.dynamic_slice_in_dim(jnp.concatenate([column, column]), lo + 1, SIDE - 1, axis=0)
+    others = jnp.moveaxis(others, 0, 2)
     diagonal = [((y * SIDE + x), ((y ^ 1) * SIDE + (x ^ 1))) for y in range(SIDE) for x in range(SIDE)]
     twin = lax.ppermute(others, ("y", "x"), diagonal)
     return jnp.stack([others, twin], axis=1)
@@ -194,10 +193,11 @@
     n_dp = SIDE * CORES
     x_nat = inputs[0]
 
+    slabs, column = weight_column(up_weight, down_weight)
     one = swap(factor_one[0])
     mixed_one = nn(one, x_nat).astype(BF16)
+    mixed_one, column = lax.optimization_barrier((mixed_one, column))
     cols_one = exchange(mixed_one, blocks)
-    slabs, column = weight_column(up_weight, down_weight)
 
     at = lax.broadcasted_iota(jnp.int32, (blocks, block), 1) // own_p
     at = lax.rem(at, SIDE) * SIDE**2 + lax.rem(at // SIDE, SIDE) * SIDE + at // SIDE**2
@@ -210,10 +210,11 @@
 
     by_q = swap(jnp.transpose(factor_two, (1, 0, 2))).reshape(block, blocks)
     two = row_major(diagonal(nn(by_q, pick)))
+    pairs = weight_pairs(column)
     x_all, cot_all = swap(x_nat), swap(cotangent[0])
-    cols_one, two, x_all, cot_all = lax.optimization_barrier((cols_one, two, x_all, cot_all))
-
-    weights = weight_halves(slabs, weight_pairs(column))
+    cols_one, _, two, x_all, cot_all = lax.optimization_barrier((cols_one, pairs, two, x_all, cot_all))
+
+    weights = weight_halves(slabs, pairs)
     mixed_two = nn(two, cols_one).astype(BF16)
     mixed = exchange(mixed_two, blocks)
 

time: 273 us -> 270 us (0.989)
  starting transfers between devices: 141 us -> 95.7 us
  waiting for transfers between devices: 77.5 us -> 120 us
    all_to_all x4, waiting for transfers between devices: 33.4 us -> 99.9 us  [exchange(): lax.all_to_all(x.reshape(blocks, x.shape[0] // blocks, x.shape[1]), TO, s...]
    ppermute x1, starting transfers between devices: 40.7 us -> 2.54 us  [layer(): lax.ppermute(lax.dynamic_index_in_dim(terms, 1 - core, axis=1, keepdims=F...]
    ppermute x3 -> x0, waiting for transfers between devices: 29 us -> none  [along_z(): lax.ppermute(x, ('lo', 'hi'), [(at[z], at[(z + step) % RING]) for z in ra...]
    ppermute x3 -> x0, starting transfers between devices: 9.47 us -> none  [along_z(): lax.ppermute(x, ('lo', 'hi'), [(at[z], at[(z + step) % RING]) for z in ra...]
    all_to_all x0 -> x1, starting transfers between devices: none -> 6.43 us  [weight_column(): lax.all_to_all(jnp.broadcast_to(piece[None], (SIDE, *piece.shape)), 'lo',...]
    all_to_all x0 -> x1, waiting for transfers between devices: none -> 3.58 us  [weight_column(): lax.all_to_all(jnp.broadcast_to(piece[None], (SIDE, *piece.shape)), 'lo',...]
  transfers between devices with their start and end apart: 17 -> 15, of which waited for: 9 -> 9; matrix products, arithmetic and copies ran while one was open for 6% -> 7% of each run, Pallas kernels for 4% -> 4%
where the time goes in v5:
time: 270 us; the launch traced here: 269 us
  waiting for transfers between devices  120 us (44%)
  starting transfers between devices  95.7 us (35%)
  Pallas kernels  21.5 us (8%)
  matrix products  12.8 us (5%)
  local copies, waits for them, and re-layouts  11.4 us (4%)
  other arithmetic  5.56 us (2%)
    all_to_all x4, waiting for transfers between devices, exchange(): lax.all_to_all(x.reshape(blocks, x.shape[0] // blocks, x.shape[1]), TO, s...  99.9 us
    all_to_all x4, starting transfers between devices, exchange(): lax.all_to_all(x.reshape(blocks, x.shape[0] // blocks, x.shape[1]), TO, s...  54.1 us
    ppermute x6, starting transfers between devices, shift(): return lax.ppermute(x, axis, [(i, (i + step) % SIDE) for i in range(SIDE)])  20.9 us
    pallas_call x2, Pallas kernels, mlp_call(): pl.pallas_call(kernel, grid=(groups, len(weights)), in_specs=[cols] * len...  18.1 us
    ppermute x6, waiting for transfers between devices, shift(): return lax.ppermute(x, axis, [(i, (i + step) % SIDE) for i in range(SIDE)])  6.71 us
    all_to_all x1, starting transfers between devices, weight_column(): lax.all_to_all(jnp.broadcast_to(piece[None], (SIDE, *piece.shape)), 'lo',...  6.43 us
  transfers between devices with their start and end apart: 15, of which 9 were waited for; matrix products, arithmetic and copies ran while one was open for 7% of the time, Pallas kernels for 4%

profile of v5, /device:TPU:1, one launch (start us, length us, event | category | flops | bytes accessed | tf_op | source)
XLA Modules:
  0.0 268.5 jit_solution(1566642316618037308)
XLA Ops:
  0.7 0.9 dynamic-slice_bitcast_fusion
  1.6 0.7 broadcast_in_dim.17
  2.3 6.4 %all-to-all-start = ((bf16[4,2,2,24,384]{4,3,2,1,0:T(8,128)(2,1)}), bf16[4,2,2,24,384]{4,3,2,1,0:T(8,128)(2,1)S(1)}, u32[]{:S(2)}, u32[]{:S(2)}) async-start(bf16[4,2,2,24,384]{4,3,2,1,0:T(8,128)(2,1)} %broadcast_in_dim.17), calls=%async_computation | async-start | bytes 589824 | tf_op jit(solution)/shard_map/all_to_all | solution.py:144
  8.8 0.8 copy-done.4
  9.6 1.5 convolution_convert_fusion.2
  11.1 3.6 %all-to-all-done = bf16[4,2,2,24,384]{4,3,2,1,0:T(8,128)(2,1)S(1)} async-done(((bf16[4,2,2,24,384]{4,3,2,1,0:T(8,128)(2,1)}), bf16[4,2,2,24,384]{4,3,2,1,0:T(8,128)(2,1)S(1)}, u32[]{:S(2)}, u32[]{:S(2)}) %all-to-all-start) | async-done | bytes 294944 | tf_op jit(solution)/shard_map/all_to_all | solution.py:144
  14.7 21.1 %all-to-all-start.1 = ((bf16[64,8,768]{2,1,0:T(8,128)(2,1)}), bf16[64,8,768]{2,1,0:T(8,128)(2,1)S(1)}, u32[]{:S(2)}, u32[]{:S(2)}) async-start(bf16[64,8,768]{2,1,0:T(8,128)(2,1)} %bitcast.134), calls=%async_computation.1 | async-start | bytes 1572864 | tf_op jit(solution)/shard_map/all_to_all | solution.py:47
  35.8 1.0 copy.46
  36.8 1.0 copy.47
  37.8 1.1 fusion.11
  38.9 0.8 copy_bitcast_fusion.1
  39.7 3.8 %collective-permute-start = (bf16[2,2,3,24,384]{4,3,2,1,0:T(8,128)(2,1)}, bf16[2,2,3,24,384]{4,3,2,1,0:T(8,128)(2,1)}, u32[]{:S(2)}, u32[]{:S(2)}) collective-permute-start(bf16[2,2,3,24,384]{4,3,2,1,0:T(8,128)(2,1)} %get-tuple-element.48), channel_id=1, source_target_pairs={{0,17},{1,16},{2,19},{3,18},{16,1},{17,0},{18,3},{19,2},{32,49},{3... | collective-permute-start | bytes 663560 | tf_op jit(solution)/shard_map/ppermute | solution.py:169
  43.5 33.2 %all-to-all-done.1 = bf16[64,8,768]{2,1,0:T(8,128)(2,1)S(1)} async-done(((bf16[64,8,768]{2,1,0:T(8,128)(2,1)}), bf16[64,8,768]{2,1,0:T(8,128)(2,1)S(1)}, u32[]{:S(2)}, u32[]{:S(2)}) %all-to-all-start.1) | async-done | bytes 786464 | tf_op jit(solution)/shard_map/all_to_all | solution.py:47
  76.7 2.8 %fusion.8 = bf16[64,8,768]{2,1,0:T(8,128)(2,1)} fusion(bf16[512,512]{1,0:T(8,128)(2,1)} %fusion.11, bf16[512,768]{1,0:T(8,128)(2,1)S(1)} %bitcast.128), kind=kOutput, calls=%fused_computation.17 | convolution fusion | flops 403046400 | bytes 2097152 | tf_op jit(solution)/shard_map/dot_general | solution.py:28
  79.5 10.9 %all-to-all-start.2 = ((bf16[64,8,768]{2,1,0:T(8,128)(2,1)}), bf16[64,8,768]{2,1,0:T(8,128)(2,1)S(1)}, u32[]{:S(2)}, u32[]{:S(2)}) async-start(bf16[64,8,768]{2,1,0:T(8,128)(2,1)} %fusion.8), calls=%async_computation.2 | async-start | bytes 1572864 | tf_op jit(solution)/shard_map/all_to_all | solution.py:47
  90.4 1.0 fusion.27
  91.4 2.9 %collective-permute-start.1 = (bf16[2,2,3,24,384]{4,3,2,1,0:T(8,128)(2,1)S(1)}, bf16[2,2,3,24,384]{4,3,2,1,0:T(8,128)(2,1)S(1)}, u32[]{:S(2)}, u32[]{:S(2)}) collective-permute-start(bf16[2,2,3,24,384]{4,3,2,1,0:T(8,128)(2,1)S(1)} %get-tuple-element.47.refs_0_), channel_id=1, source_target_pairs={{0,16},{16,32},{32,48},{48,0},{1,17},{17,33},{33,49},{49,1},{2,18}... | collective-permute-start | bytes 663560 | tf_op jit(solution)/shard_map/ppermute | solution.py:54
  94.3 4.3 %collective-permute-start.2 = (bf16[2,2,3,24,384]{4,3,2,1,0:T(8,128)(2,1)S(1)}, bf16[2,2,3,24,384]{4,3,2,1,0:T(8,128)(2,1)S(1)}, u32[]{:S(2)}, u32[]{:S(2)}) collective-permute-start(bf16[2,2,3,24,384]{4,3,2,1,0:T(8,128)(2,1)S(1)} %get-tuple-element.47.refs_0_), channel_id=1, source_target_pairs={{0,32},{16,48},{32,0},{48,16},{1,33},{17,49},{33,1},{49,17},{2,34}... | collective-permute-start | bytes 663560 | tf_op jit(solution)/shard_map/ppermute | solution.py:54
  98.6 3.1 %collective-permute-start.3 = (bf16[2,2,3,24,384]{4,3,2,1,0:T(8,128)(2,1)S(1)}, bf16[2,2,3,24,384]{4,3,2,1,0:T(8,128)(2,1)S(1)}, u32[]{:S(2)}, u32[]{:S(2)}) collective-permute-start(bf16[2,2,3,24,384]{4,3,2,1,0:T(8,128)(2,1)S(1)} %get-tuple-element.47.refs_0_), channel_id=1, source_target_pairs={{0,48},{16,0},{32,16},{48,32},{1,49},{17,1},{33,17},{49,33},{2,50}... | collective-permute-start | bytes 663560 | tf_op jit(solution)/shard_map/ppermute | solution.py:54
  101.7 3.1 %collective-permute-start.4 = (bf16[2,2,3,24,384]{4,3,2,1,0:T(8,128)(2,1)S(1)}, bf16[2,2,3,24,384]{4,3,2,1,0:T(8,128)(2,1)S(1)}, u32[]{:S(2)}, u32[]{:S(2)}) collective-permute-start(bf16[2,2,3,24,384]{4,3,2,1,0:T(8,128)(2,1)S(1)} %get-tuple-element.46.refs_4_), channel_id=1, source_target_pairs={{0,1},{1,2},{2,3},{3,0},{4,5},{5,6},{6,7},{7,4},{8,9},{9,10},{10,1... | collective-permute-start | bytes 663560 | tf_op jit(solution)/shard_map/ppermute | solution.py:54
  104.9 4.5 %collective-permute-start.5 = (bf16[2,2,3,24,384]{4,3,2,1,0:T(8,128)(2,1)S(1)}, bf16[2,2,3,24,384]{4,3,2,1,0:T(8,128)(2,1)S(1)}, u32[]{:S(2)}, u32[]{:S(2)}) collective-permute-start(bf16[2,2,3,24,384]{4,3,2,1,0:T(8,128)(2,1)S(1)} %get-tuple-element.46.refs_4_), channel_id=1, source_target_pairs={{0,2},{1,3},{2,0},{3,1},{4,6},{5,7},{6,4},{7,5},{8,10},{9,11},{10,... | collective-permute-start | bytes 663560 | tf_op jit(solution)/shard_map/ppermute | solution.py:54
  109.4 3.0 %collective-permute-start.6 = (bf16[2,2,3,24,384]{4,3,2,1,0:T(8,128)(2,1)S(1)}, bf16[2,2,3,24,384]{4,3,2,1,0:T(8,128)(2,1)}, u32[]{:S(2)}, u32[]{:S(2)}) collective-permute-start(bf16[2,2,3,24,384]{4,3,2,1,0:T(8,128)(2,1)S(1)} %get-tuple-element.46.refs_4_), channel_id=1, source_target_pairs={{0,3},{1,0},{2,1},{3,2},{4,7},{5,4},{6,5},{7,6},{8,11},{9,8},{10,9... | collective-permute-start | bytes 663560 | tf_op jit(solution)/shard_map/ppermute | solution.py:54
  113.0 0.9 pad_maximum_fusion.slabs_ref
  114.0 5.5 %collective-permute-done.5.refs_6_ = bf16[2,2,3,24,384]{4,3,2,1,0:T(8,128)(2,1)S(1)} collective-permute-done((bf16[2,2,3,24,384]{4,3,2,1,0:T(8,128)(2,1)S(1)}, bf16[2,2,3,24,384]{4,3,2,1,0:T(8,128)(2,1)S(1)}, u32[]{:S(2)}, u32[]{:S(2)}) %collective-permute-start.5) | collective-permute-done | bytes 221216 | tf_op jit(solution)/shard_map/ppermute | solution.py:54
  119.5 0.7 copy-done.19
  120.2 1.2 collective-permute-done.6.refs_7_
  121.4 3.4 %assemble.1 = bf16[2,2,32,24,384]{4,3,2,1,0:T(8,128)(2,1)} custom-call(s32[2]{0:T(128)} %pad_add_fusion.at_ref, bf16[2,2,8,24,384]{4,3,2,1,0:T(8,128)(2,1)} %pad_maximum_fusion.slabs_ref, bf16[2,2,3,24,384]{4,3,2,1,0:T(8,128)(2,1)} %copy-done.7, bf16[2,2,3,24,384]{4,3,2,1,0:T(8,128)(2,1)} %copy-done.15, bf16[2,2,3,24,384]{4,3,2,1,0:T(8,128)(2,1)} %copy-done.16, ...), custom_call_target="tpu_custom_call" | custom-call | bytes 4718592 | tf_op jit(solution)/shard_map/assemble/pallas_call | solution.py:178
  124.7 4.4 %collective-permute-start.7 = (bf16[2,2,768,384]{3,2,1,0:T(8,128)(2,1)}, bf16[2,2,768,384]{3,2,1,0:T(8,128)(2,1)}, u32[]{:S(2)}, u32[]{:S(2)}) collective-permute-start(bf16[2,2,768,384]{3,2,1,0:T(8,128)(2,1)} %bitcast.121), channel_id=1, source_target_pairs={{0,64},{64,0},{1,65},{65,1},{2,66},{66,2},{3,67},{67,3},{4,68},{68... | collective-permute-start | bytes 7077896 | tf_op jit(solution)/shard_map/ppermute | solution.py:187
  129.2 4.5 %collective-permute-done.7.other_ref = bf16[2,2,768,384]{3,2,1,0:T(8,128)(2,1)} collective-permute-done((bf16[2,2,768,384]{3,2,1,0:T(8,128)(2,1)}, bf16[2,2,768,384]{3,2,1,0:T(8,128)(2,1)}, u32[]{:S(2)}, u32[]{:S(2)}) %collective-permute-start.7) | collective-permute-done | bytes 2359328 | tf_op jit(solution)/shard_map/ppermute | solution.py:187
  133.7 0.9 copy-done.1
  134.6 10.1 %shard_map.93 = (bf16[512,768]{1,0:T(8,128)(2,1)}, f32[512,768]{1,0:T(8,128)}) custom-call(bf16[512,768]{1,0:T(8,128)(2,1)} %bitcast.117, bf16[512,768]{1,0:T(8,128)(2,1)} %bitcast.114, bf16[512,768]{1,0:T(8,128)(2,1)} %bitcast.130, bf16[2,2,768,384]{3,2,1,0:T(8,128)(2,1)} %bitcast.122, bf16[2,2,768,384]{3,2,1,0:T(8,128)(2,1)} %collective-permute-done.7.other_ref), custom_call_target="tpu_custom_call" | custom-call | flops 3623878656 | bytes 7077888 | tf_op jit(solution)/shard_map/pallas_call | solution.py:123
  144.7 14.3 %all-to-all-start.3 = ((bf16[64,8,768]{2,1,0:T(8,128)(2,1)}), bf16[64,8,768]{2,1,0:T(8,128)(2,1)S(1)}, u32[]{:S(2)}, u32[]{:S(2)}) async-start(bf16[64,8,768]{2,1,0:T(8,128)(2,1)} %bitcast.135), calls=%async_computation.3 | async-start | bytes 1572864 | tf_op jit(solution)/shard_map/all_to_all | solution.py:47
  159.0 8.1 %shard_map.94 = bf16[512,768]{1,0:T(8,128)(2,1)} custom-call(bf16[512,768]{1,0:T(8,128)(2,1)} %bitcast.118, bf16[512,768]{1,0:T(8,128)(2,1)} %bitcast.115, bf16[2,2,768,384]{3,2,1,0:T(8,128)(2,1)} %bitcast.123, bf16[2,2,768,384]{3,2,1,0:T(8,128)(2,1)} %collective-permute-done.7.other_ref), custom_call_target="tpu_custom_call" | custom-call | flops 2415919104 | bytes 6291456 | tf_op jit(solution)/shard_map/pallas_call | solution.py:123
  167.1 2.2 copy.48
  169.3 0.7 fusion.4
  170.1 30.2 %all-to-all-done.3 = bf16[64,8,768]{2,1,0:T(8,128)(2,1)S(1)} async-done(((bf16[64,8,768]{2,1,0:T(8,128)(2,1)}), bf16[64,8,768]{2,1,0:T(8,128)(2,1)S(1)}, u32[]{:S(2)}, u32[]{:S(2)}) %all-to-all-start.3) | async-done | bytes 786464 | tf_op jit(solution)/shard_map/all_to_all | solution.py:47
  200.3 2.8 %fusion.9 = bf16[64,8,768]{2,1,0:T(8,128)(2,1)} fusion(bf16[512,512]{1,0:T(8,128)(2,1)} %fusion.11, bf16[512,768]{1,0:T(8,128)(2,1)S(1)} %bitcast.132), kind=kOutput, calls=%fused_computation.18 | convolution fusion | flops 403046400 | bytes 2097152 | tf_op jit(solution)/shard_map/dot_general | solution.py:32
  203.1 7.9 %all-to-all-start.4 = ((bf16[64,8,768]{2,1,0:T(8,128)(2,1)}), bf16[64,8,768]{2,1,0:T(8,128)(2,1)S(1)}, u32[]{:S(2)}, u32[]{:S(2)}) async-start(bf16[64,8,768]{2,1,0:T(8,128)(2,1)} %fusion.9), calls=%async_computation.4 | async-start | bytes 1572864 | tf_op jit(solution)/shard_map/all_to_all | solution.py:47
  211.0 2.2 fusion.13
  213.5 36.6 %all-to-all-done.4 = bf16[64,8,768]{2,1,0:T(8,128)(2,1)S(1)} async-done(((bf16[64,8,768]{2,1,0:T(8,128)(2,1)}), bf16[64,8,768]{2,1,0:T(8,128)(2,1)S(1)}, u32[]{:S(2)}, u32[]{:S(2)}) %all-to-all-start.4) | async-done | bytes 786464 | tf_op jit(solution)/shard_map/all_to_all | solution.py:47
  251.1 2.5 collective-permute-start.8
  253.6 1.2 collective-permute-done.8
  254.8 0.8 fusion.16
  255.6 3.5 %all-to-all-start.5 = ((bf16[4,72,512]{2,1,0:T(8,128)(2,1)}), bf16[4,72,512]{2,1,0:T(8,128)(2,1)S(1)}, u32[]{:S(2)}, u32[]{:S(2)}) async-start(bf16[4,72,512]{2,1,0:T(8,128)(2,1)} %fusion.16), calls=%async_computation.5 | async-start | bytes 589824 | tf_op jit(solution)/shard_map/all_to_all | solution.py:242
  259.5 1.9 fusion.10
  261.4 1.2 copy.54
  262.6 4.5 %all-to-all-done.5 = bf16[4,72,512]{2,1,0:T(8,128)(2,1)S(1)} async-done(((bf16[4,72,512]{2,1,0:T(8,128)(2,1)}), bf16[4,72,512]{2,1,0:T(8,128)(2,1)S(1)}, u32[]{:S(2)}, u32[]{:S(2)}) %all-to-all-start.5) | async-done | bytes 294944 | tf_op jit(solution)/shard_map/all_to_all | solution.py:242
  267.8 0.7 convert_reduce_fusion
  (64 shorter events, 3.5 us)
Async XLA Ops:
  0.6 8.1 %copy-start.12 = (bf16[1,512,512]{2,1,0:T(8,128)(2,1)S(1)}, bf16[1,512,512]{2,1,0:T(8,128)(2,1)}, u32[]{:S(2)}) copy-start(bf16[1,512,512]{2,1,0:T(8,128)(2,1)} %param.8) | copy-start | bytes 1572868
  0.6 9.0 %copy-start.9 = (bf16[1,512,768]{2,1,0:T(8,128)(2,1)S(1)}, bf16[1,512,768]{2,1,0:T(8,128)(2,1)}, u32[]{:S(2)}) copy-start(bf16[1,512,768]{2,1,0:T(8,128)(2,1)} %param.6) | copy-start | bytes 2359300
  2.3 12.3 %all-to-all-start = ((bf16[4,2,2,24,384]{4,3,2,1,0:T(8,128)(2,1)}), bf16[4,2,2,24,384]{4,3,2,1,0:T(8,128)(2,1)S(1)}, u32[]{:S(2)}, u32[]{:S(2)}) async-start(bf16[4,2,2,24,384]{4,3,2,1,0:T(8,128)(2,1)} %broadcast_in_dim.17), calls=%async_computation | async-start | bytes 589824 | tf_op jit(solution)/shard_map/all_to_all | solution.py:144
  8.8 0.8 copy-start.4
  9.6 26.1 %copy-start.20 = (bf16[8,64,64]{2,1,0:T(8,128)(2,1)S(1)}, bf16[8,64,64]{2,1,0:T(8,128)(2,1)}, u32[]{:S(2)}) copy-start(bf16[8,64,64]{2,1,0:T(8,128)(2,1)} %param.9) | copy-start | bytes 196612
  14.6 22.1 %copy-start.8 = (bf16[1,512,768]{2,1,0:T(8,128)(2,1)S(1)}, bf16[1,512,768]{2,1,0:T(8,128)(2,1)}, u32[]{:S(2)}) copy-start(bf16[1,512,768]{2,1,0:T(8,128)(2,1)} %param.7) | copy-start | bytes 2359300
  14.7 62.0 %all-to-all-start.1 = ((bf16[64,8,768]{2,1,0:T(8,128)(2,1)}), bf16[64,8,768]{2,1,0:T(8,128)(2,1)S(1)}, u32[]{:S(2)}, u32[]{:S(2)}) async-start(bf16[64,8,768]{2,1,0:T(8,128)(2,1)} %bitcast.134), calls=%async_computation.1 | async-start | bytes 1572864 | tf_op jit(solution)/shard_map/all_to_all | solution.py:47
  39.7 50.7 %collective-permute-start = (bf16[2,2,3,24,384]{4,3,2,1,0:T(8,128)(2,1)}, bf16[2,2,3,24,384]{4,3,2,1,0:T(8,128)(2,1)}, u32[]{:S(2)}, u32[]{:S(2)}) collective-permute-start(bf16[2,2,3,24,384]{4,3,2,1,0:T(8,128)(2,1)} %get-tuple-element.48), channel_id=1, source_target_pairs={{0,17},{1,16},{2,19},{3,18},{16,1},{17,0},{18,3},{19,2},{32,49},{3... | collective-permute-start | bytes 663560 | tf_op jit(solution)/shard_map/ppermute | solution.py:169
  76.7 13.7 %copy-start.10 = (bf16[64,8,768]{2,1,0:T(8,128)(2,1)}, bf16[64,8,768]{2,1,0:T(8,128)(2,1)S(1)}, u32[]{:S(2)}) copy-start(bf16[64,8,768]{2,1,0:T(8,128)(2,1)S(1)} %all-to-all-done.1) | copy-start | bytes 2359300
  79.5 33.6 %copy-start.13 = (bf16[2,192,384]{2,1,0:T(8,128)(2,1)S(1)}, bf16[2,192,384]{2,1,0:T(8,128)(2,1)}, u32[]{:S(2)}) copy-start(bf16[2,192,384]{2,1,0:T(8,128)(2,1)} %param.11) | copy-start | bytes 884740
  79.5 33.6 %copy-start.14 = (bf16[2,384,192]{1,2,0:T(8,128)(2,1)S(1)}, bf16[2,384,192]{1,2,0:T(8,128)(2,1)}, u32[]{:S(2)}) copy-start(bf16[2,384,192]{1,2,0:T(8,128)(2,1)} %param.10) | copy-start | bytes 884740
  79.5 54.2 %all-to-all-start.2 = ((bf16[64,8,768]{2,1,0:T(8,128)(2,1)}), bf16[64,8,768]{2,1,0:T(8,128)(2,1)S(1)}, u32[]{:S(2)}, u32[]{:S(2)}) async-start(bf16[64,8,768]{2,1,0:T(8,128)(2,1)} %fusion.8), calls=%async_computation.2 | async-start | bytes 1572864 | tf_op jit(solution)/shard_map/all_to_all | solution.py:47
  91.4 30.0 %copy-start.6 = (bf16[2,2,3,24,384]{4,3,2,1,0:T(8,128)(2,1)}, bf16[2,2,3,24,384]{4,3,2,1,0:T(8,128)(2,1)S(1)}, u32[]{:S(2)}) copy-start(bf16[2,2,3,24,384]{4,3,2,1,0:T(8,128)(2,1)S(1)} %get-tuple-element.46.refs_4_) | copy-start | bytes 663556
  91.4 30.0 %copy-start.7 = (bf16[2,2,3,24,384]{4,3,2,1,0:T(8,128)(2,1)}, bf16[2,2,3,24,384]{4,3,2,1,0:T(8,128)(2,1)S(1)}, u32[]{:S(2)}) copy-start(bf16[2,2,3,24,384]{4,3,2,1,0:T(8,128)(2,1)S(1)} %get-tuple-element.47.refs_0_) | copy-start | bytes 663556
  91.4 18.0 %collective-permute-start.1 = (bf16[2,2,3,24,384]{4,3,2,1,0:T(8,128)(2,1)S(1)}, bf16[2,2,3,24,384]{4,3,2,1,0:T(8,128)(2,1)S(1)}, u32[]{:S(2)}, u32[]{:S(2)}) collective-permute-start(bf16[2,2,3,24,384]{4,3,2,1,0:T(8,128)(2,1)S(1)} %get-tuple-element.47.refs_0_), channel_id=1, source_target_pairs={{0,16},{16,32},{32,48},{48,0},{1,17},{17,33},{33,49},{49,1},{2,18}... | collective-permute-start | bytes 663560 | tf_op jit(solution)/shard_map/ppermute | solution.py:54
  94.3 19.6 %collective-permute-start.2 = (bf16[2,2,3,24,384]{4,3,2,1,0:T(8,128)(2,1)S(1)}, bf16[2,2,3,24,384]{4,3,2,1,0:T(8,128)(2,1)S(1)}, u32[]{:S(2)}, u32[]{:S(2)}) collective-permute-start(bf16[2,2,3,24,384]{4,3,2,1,0:T(8,128)(2,1)S(1)} %get-tuple-element.47.refs_0_), channel_id=1, source_target_pairs={{0,32},{16,48},{32,0},{48,16},{1,33},{17,49},{33,1},{49,17},{2,34}... | collective-permute-start | bytes 663560 | tf_op jit(solution)/shard_map/ppermute | solution.py:54
  98.6 15.3 %collective-permute-start.3 = (bf16[2,2,3,24,384]{4,3,2,1,0:T(8,128)(2,1)S(1)}, bf16[2,2,3,24,384]{4,3,2,1,0:T(8,128)(2,1)S(1)}, u32[]{:S(2)}, u32[]{:S(2)}) collective-permute-start(bf16[2,2,3,24,384]{4,3,2,1,0:T(8,128)(2,1)S(1)} %get-tuple-element.47.refs_0_), channel_id=1, source_target_pairs={{0,48},{16,0},{32,16},{48,32},{1,49},{17,1},{33,17},{49,33},{2,50}... | collective-permute-start | bytes 663560 | tf_op jit(solution)/shard_map/ppermute | solution.py:54
  101.7 12.2 %collective-permute-start.4 = (bf16[2,2,3,24,384]{4,3,2,1,0:T(8,128)(2,1)S(1)}, bf16[2,2,3,24,384]{4,3,2,1,0:T(8,128)(2,1)S(1)}, u32[]{:S(2)}, u32[]{:S(2)}) collective-permute-start(bf16[2,2,3,24,384]{4,3,2,1,0:T(8,128)(2,1)S(1)} %get-tuple-element.46.refs_4_), channel_id=1, source_target_pairs={{0,1},{1,2},{2,3},{3,0},{4,5},{5,6},{6,7},{7,4},{8,9},{9,10},{10,1... | collective-permute-start | bytes 663560 | tf_op jit(solution)/shard_map/ppermute | solution.py:54
  104.9 14.6 %collective-permute-start.5 = (bf16[2,2,3,24,384]{4,3,2,1,0:T(8,128)(2,1)S(1)}, bf16[2,2,3,24,384]{4,3,2,1,0:T(8,128)(2,1)S(1)}, u32[]{:S(2)}, u32[]{:S(2)}) collective-permute-start(bf16[2,2,3,24,384]{4,3,2,1,0:T(8,128)(2,1)S(1)} %get-tuple-element.46.refs_4_), channel_id=1, source_target_pairs={{0,2},{1,3},{2,0},{3,1},{4,6},{5,7},{6,4},{7,5},{8,10},{9,11},{10,... | collective-permute-start | bytes 663560 | tf_op jit(solution)/shard_map/ppermute | solution.py:54
  109.4 12.0 %copy-start.15 = (bf16[2,2,3,24,384]{4,3,2,1,0:T(8,128)(2,1)}, bf16[2,2,3,24,384]{4,3,2,1,0:T(8,128)(2,1)S(1)}, u32[]{:S(2)}) copy-start(bf16[2,2,3,24,384]{4,3,2,1,0:T(8,128)(2,1)S(1)} %collective-permute-done.1.refs_1_) | copy-start | bytes 663556
  109.4 12.0 %collective-permute-start.6 = (bf16[2,2,3,24,384]{4,3,2,1,0:T(8,128)(2,1)S(1)}, bf16[2,2,3,24,384]{4,3,2,1,0:T(8,128)(2,1)}, u32[]{:S(2)}, u32[]{:S(2)}) collective-permute-start(bf16[2,2,3,24,384]{4,3,2,1,0:T(8,128)(2,1)S(1)} %get-tuple-element.46.refs_4_), channel_id=1, source_target_pairs={{0,3},{1,0},{2,1},{3,2},{4,7},{5,4},{6,5},{7,6},{8,11},{9,8},{10,9... | collective-permute-start | bytes 663560 | tf_op jit(solution)/shard_map/ppermute | solution.py:54
  113.9 7.4 %copy-start.16 = (bf16[2,2,3,24,384]{4,3,2,1,0:T(8,128)(2,1)}, bf16[2,2,3,24,384]{4,3,2,1,0:T(8,128)(2,1)S(1)}, u32[]{:S(2)}) copy-start(bf16[2,2,3,24,384]{4,3,2,1,0:T(8,128)(2,1)S(1)} %collective-permute-done.2.refs_2_) | copy-start | bytes 663556
  113.9 5.5 %copy-start.17 = (bf16[2,2,3,24,384]{4,3,2,1,0:T(8,128)(2,1)}, bf16[2,2,3,24,384]{4,3,2,1,0:T(8,128)(2,1)S(1)}, u32[]{:S(2)}) copy-start(bf16[2,2,3,24,384]{4,3,2,1,0:T(8,128)(2,1)S(1)} %collective-permute-done.3.refs_3_) | copy-start | bytes 663556
  114.0 5.5 %copy-start.18 = (bf16[2,2,3,24,384]{4,3,2,1,0:T(8,128)(2,1)}, bf16[2,2,3,24,384]{4,3,2,1,0:T(8,128)(2,1)S(1)}, u32[]{:S(2)}) copy-start(bf16[2,2,3,24,384]{4,3,2,1,0:T(8,128)(2,1)S(1)} %collective-permute-done.4.refs_5_) | copy-start | bytes 663556
  119.5 0.7 copy-start.19
  124.7 8.9 %collective-permute-start.7 = (bf16[2,2,768,384]{3,2,1,0:T(8,128)(2,1)}, bf16[2,2,768,384]{3,2,1,0:T(8,128)(2,1)}, u32[]{:S(2)}, u32[]{:S(2)}) collective-permute-start(bf16[2,2,768,384]{3,2,1,0:T(8,128)(2,1)} %bitcast.121), channel_id=1, source_target_pairs={{0,64},{64,0},{1,65},{65,1},{2,66},{66,2},{3,67},{67,3},{4,68},{68... | collective-permute-start | bytes 7077896 | tf_op jit(solution)/shard_map/ppermute | solution.py:187
  133.7 0.9 copy-start.1
  144.7 55.7 %all-to-all-start.3 = ((bf16[64,8,768]{2,1,0:T(8,128)(2,1)}), bf16[64,8,768]{2,1,0:T(8,128)(2,1)S(1)}, u32[]{:S(2)}, u32[]{:S(2)}) async-start(bf16[64,8,768]{2,1,0:T(8,128)(2,1)} %bitcast.135), calls=%async_computation.3 | async-start | bytes 1572864 | tf_op jit(solution)/shard_map/all_to_all | solution.py:47
  159.0 10.3 %copy-start.5 = (f32[512,768]{1,0:T(8,128)S(1)}, f32[512,768]{1,0:T(8,128)}, u32[]{:S(2)}) copy-start(f32[512,768]{1,0:T(8,128)} %get-tuple-element.24) | copy-start | bytes 4718596
  167.1 2.2 copy-start
  167.1 2.2 copy-start.2
  200.3 2.8 %copy-start.11 = (bf16[64,8,768]{2,1,0:T(8,128)(2,1)}, bf16[64,8,768]{2,1,0:T(8,128)(2,1)S(1)}, u32[]{:S(2)}) copy-start(bf16[64,8,768]{2,1,0:T(8,128)(2,1)S(1)} %all-to-all-done.3) | copy-start | bytes 2359300
  203.1 47.0 %all-to-all-start.4 = ((bf16[64,8,768]{2,1,0:T(8,128)(2,1)}), bf16[64,8,768]{2,1,0:T(8,128)(2,1)S(1)}, u32[]{:S(2)}, u32[]{:S(2)}) async-start(bf16[64,8,768]{2,1,0:T(8,128)(2,1)} %fusion.9), calls=%async_computation.4 | async-start | bytes 1572864 | tf_op jit(solution)/shard_map/all_to_all | solution.py:47
  250.1 0.9 copy-start.3
  251.1 3.7 %collective-permute-start.8 = (bf16[4,72,512]{2,1,0:T(8,128)(2,1)S(1)}, bf16[4,72,512]{2,1,0:T(8,128)(2,1)S(1)}, u32[]{:S(2)}, u32[]{:S(2)}) collective-permute-start(bf16[4,72,512]{2,1,0:T(8,128)(2,1)S(1)} %fusion.21), channel_id=1, source_target_pairs={{0,64},{64,0},{1,65},{65,1},{2,66},{66,2},{3,67},{67,3},{4,68},{68... | collective-permute-start | bytes 884744 | tf_op jit(solution)/shard_map/ppermute | solution.py:240
  255.6 11.5 %all-to-all-start.5 = ((bf16[4,72,512]{2,1,0:T(8,128)(2,1)}), bf16[4,72,512]{2,1,0:T(8,128)(2,1)S(1)}, u32[]{:S(2)}, u32[]{:S(2)}) async-start(bf16[4,72,512]{2,1,0:T(8,128)(2,1)} %fusion.16), calls=%async_computation.5 | async-start | bytes 589824 | tf_op jit(solution)/shard_map/all_to_all | solution.py:242

commit v6 on v1

--- a/solution.py
+++ b/solution.py
@@ -203,12 +203,17 @@
     grad_one, term_two = lax.optimization_barrier((grad_one, term_two))
 
     term_one = swap(nt(grad_one, x_nat).astype(BF16)).reshape(n_dp, block // n_dp, block)
-    summed = lax.all_to_all(
-        jnp.concatenate([term_one, term_two], axis=1), ("lo", "core"), split_axis=0, concat_axis=0, tiled=True
-    )
-    summed = jnp.sum(summed.astype(F32), axis=0)
-    grad_first = summed[: block // n_dp][None]
-    grad_second = jnp.transpose(summed[block // n_dp :].reshape(blocks // n_dp, own_p, blocks), (1, 0, 2))
+    terms = jnp.concatenate([term_one, term_two], axis=1)
+    terms = terms.reshape(SIDE, CORES, *terms.shape[1:])
+    core = lax.axis_index("core")
+    kept = lax.dynamic_index_in_dim(terms, core, axis=1, keepdims=False)
+    other = lax.ppermute(lax.dynamic_index_in_dim(terms, 1 - core, axis=1, keepdims=False), "core", [(0, 1), (1, 0)])
+    terms = (kept.astype(F32) + other.astype(F32)).astype(BF16)
+    terms = lax.all_to_all(terms, "lo", split_axis=0, concat_axis=0, tiled=True)
+    chunk = block // n_dp
+    grad_first = jnp.sum(terms[:, :chunk].astype(F32), axis=0)[None]
+    grad_second = jnp.sum(terms[:, chunk:].astype(F32), axis=0).reshape(blocks // n_dp, own_p, blocks)
+    grad_second = jnp.transpose(grad_second, (1, 0, 2))
 
     grad_inputs = (gate_in + tn(one, grad_one)).astype(BF16)[None]
     return outputs, grad_inputs, grad_first, grad_second

time: 274 us -> 267 us (0.974)
  waiting for transfers between devices: 145 us -> 138 us
    all_to_all x1, waiting for transfers between devices: 12.4 us -> 4.55 us  [layer(): terms = lax.all_to_all(terms, 'lo', split_axis=0, concat_axis=0, tiled=True)]
  transfers between devices with their start and end apart: 13 -> 14, of which waited for: 10 -> 11; matrix products, arithmetic and copies ran while one was open for 7% -> 7% of each run, Pallas kernels for 3% -> 3%
where the time goes in v6:
time: 267 us; the launch traced here: 266 us
  waiting for transfers between devices  138 us (52%)
  starting transfers between devices  79.3 us (30%)
  Pallas kernels  18.2 us (7%)
  local copies, waits for them, and re-layouts  15.6 us (6%)
  matrix products  10.7 us (4%)
  other arithmetic  3.18 us (1%)
    all_to_all x4, waiting for transfers between devices, exchange(): lax.all_to_all(x.reshape(blocks, x.shape[0] // blocks, x.shape[1]), TO, s...  104 us
    all_to_all x4, starting transfers between devices, exchange(): lax.all_to_all(x.reshape(blocks, x.shape[0] // blocks, x.shape[1]), TO, s...  42 us
    ppermute x3, waiting for transfers between devices, shift(): return lax.ppermute(x, axis, [(i, (i + step) % SIDE) for i in range(SIDE)])  18.5 us
    pallas_call x2, Pallas kernels, mlp_call(): pl.pallas_call(kernel, grid=(groups, len(weights)), in_specs=[cols] * len...  18.2 us
    ppermute x3, starting transfers between devices, along_z(): lax.ppermute(x, ('lo', 'hi'), [(at[z], at[(z + step) % RING]) for z in ra...  15.8 us
    ppermute x3, starting transfers between devices, shift(): return lax.ppermute(x, axis, [(i, (i + step) % SIDE) for i in range(SIDE)])  9.31 us
    unnamed x36, local copies, waits for them, and re-layouts  8.35 us
  transfers between devices with their start and end apart: 14, of which 11 were waited for; matrix products, arithmetic and copies ran while one was open for 7% of the time, Pallas kernels for 3%

profile of v6, /device:TPU:1, one launch (start us, length us, event | category | flops | bytes accessed | tf_op | source)
XLA Modules:
  0.0 266.0 jit_solution(16817127197493289569)
XLA Ops:
  0.7 0.9 fusion.37
  1.5 5.7 %collective-permute-start.2 = (bf16[2,2,24,384]{3,2,1,0:T(8,128)(2,1)S(1)}, bf16[2,2,24,384]{3,2,1,0:T(8,128)(2,1)S(1)}, u32[]{:S(2)}, u32[]{:S(2)}) collective-permute-start(bf16[2,2,24,384]{3,2,1,0:T(8,128)(2,1)S(1)} %fusion.37), channel_id=1, source_target_pairs={{0,256},{128,384},{256,4},{384,132},{4,260},{132,388},{260,8},{388... | collective-permute-start | bytes 221192 | tf_op jit(solution)/shard_map/ppermute | solution.py:51
  7.2 8.1 %collective-permute-start.1 = (bf16[2,2,24,384]{3,2,1,0:T(8,128)(2,1)S(1)}, bf16[2,2,24,384]{3,2,1,0:T(8,128)(2,1)S(1)}, u32[]{:S(2)}, u32[]{:S(2)}) collective-permute-start(bf16[2,2,24,384]{3,2,1,0:T(8,128)(2,1)S(1)} %fusion.37), channel_id=1, source_target_pairs={{0,396},{128,0},{256,128},{384,256},{4,384},{132,4},{260,132},{388... | collective-permute-start | bytes 221192 | tf_op jit(solution)/shard_map/ppermute | solution.py:51
  15.4 1.9 collective-permute-start
  17.3 1.1 copy.26
  18.4 0.8 copy-done.4
  19.2 1.5 convolution_convert_fusion.2
  20.7 1.0 collective-permute-done
  21.7 15.0 %all-to-all-start = ((bf16[64,8,768]{2,1,0:T(8,128)(2,1)}), bf16[64,8,768]{2,1,0:T(8,128)(2,1)S(1)}, u32[]{:S(2)}, u32[]{:S(2)}) async-start(bf16[64,8,768]{2,1,0:T(8,128)(2,1)} %bitcast.111), calls=%async_computation | async-start | bytes 1572864 | tf_op jit(solution)/shard_map/all_to_all | solution.py:43
  36.8 1.0 copy.28
  37.8 1.0 copy.29
  39.2 2.9 %collective-permute-start.3 = (bf16[2,2,72,384]{3,2,1,0:T(8,128)(2,1)S(1)}, bf16[2,2,72,384]{3,2,1,0:T(8,128)(2,1)S(1)}, u32[]{:S(2)}, u32[]{:S(2)}) collective-permute-start(bf16[2,2,72,384]{3,2,1,0:T(8,128)(2,1)S(1)} %pad_maximum_fusion.1), channel_id=1, source_target_pairs={{0,1},{1,0},{2,3},{3,2},{4,5},{5,4},{6,7},{7,6},{8,9},{9,8},{10,11... | collective-permute-start | bytes 663560 | tf_op jit(solution)/shard_map/ppermute | solution.py:150
  42.2 0.7 constant_dynamic-update-slice_fusion.6
  42.9 4.7 %collective-permute-done.3 = bf16[2,2,72,384]{3,2,1,0:T(8,128)(2,1)S(1)} collective-permute-done((bf16[2,2,72,384]{3,2,1,0:T(8,128)(2,1)S(1)}, bf16[2,2,72,384]{3,2,1,0:T(8,128)(2,1)S(1)}, u32[]{:S(2)}, u32[]{:S(2)}) %collective-permute-start.3) | collective-permute-done | bytes 221216 | tf_op jit(solution)/shard_map/ppermute | solution.py:150
  47.7 0.8 constant_dynamic-update-slice_fusion.5
  48.4 1.4 copy-done.12
  49.9 2.1 collective-permute-start.4
  52.0 25.4 %all-to-all-done = bf16[64,8,768]{2,1,0:T(8,128)(2,1)S(1)} async-done(((bf16[64,8,768]{2,1,0:T(8,128)(2,1)}), bf16[64,8,768]{2,1,0:T(8,128)(2,1)S(1)}, u32[]{:S(2)}, u32[]{:S(2)}) %all-to-all-start) | async-done | bytes 786464 | tf_op jit(solution)/shard_map/all_to_all | solution.py:43
  77.4 1.5 fusion.8
  78.9 11.0 %all-to-all-start.1 = ((bf16[64,8,768]{2,1,0:T(8,128)(2,1)}), bf16[64,8,768]{2,1,0:T(8,128)(2,1)S(1)}, u32[]{:S(2)}, u32[]{:S(2)}) async-start(bf16[64,8,768]{2,1,0:T(8,128)(2,1)} %fusion.8), calls=%async_computation.1 | async-start | bytes 1572864 | tf_op jit(solution)/shard_map/all_to_all | solution.py:43
  89.9 4.4 %collective-permute-start.5 = (bf16[2,2,144,384]{3,2,1,0:T(8,128)(2,1)}, bf16[2,2,144,384]{3,2,1,0:T(8,128)(2,1)S(1)}, u32[]{:S(2)}, u32[]{:S(2)}) collective-permute-start(bf16[2,2,144,384]{3,2,1,0:T(8,128)(2,1)} %get-tuple-element.43), channel_id=1, source_target_pairs={{0,32},{16,48},{32,0},{48,16},{1,33},{17,49},{33,1},{49,17},{2,34}... | collective-permute-start | bytes 1327112 | tf_op jit(solution)/shard_map/ppermute | solution.py:55
  94.3 2.8 %collective-permute-start.6 = (bf16[2,2,144,384]{3,2,1,0:T(8,128)(2,1)}, bf16[2,2,144,384]{3,2,1,0:T(8,128)(2,1)S(1)}, u32[]{:S(2)}, u32[]{:S(2)}) collective-permute-start(bf16[2,2,144,384]{3,2,1,0:T(8,128)(2,1)} %get-tuple-element.43), channel_id=1, source_target_pairs={{0,48},{16,0},{32,16},{48,32},{1,49},{17,1},{33,17},{49,33},{2,50}... | collective-permute-start | bytes 1327112 | tf_op jit(solution)/shard_map/ppermute | solution.py:55
  97.2 0.8 constant_dynamic-update-slice_fusion.4
  98.0 8.8 %collective-permute-done.5 = bf16[2,2,144,384]{3,2,1,0:T(8,128)(2,1)S(1)} collective-permute-done((bf16[2,2,144,384]{3,2,1,0:T(8,128)(2,1)}, bf16[2,2,144,384]{3,2,1,0:T(8,128)(2,1)S(1)}, u32[]{:S(2)}, u32[]{:S(2)}) %collective-permute-start.5) | collective-permute-done | bytes 442400 | tf_op jit(solution)/shard_map/ppermute | solution.py:55
  106.8 0.8 constant_dynamic-update-slice_fusion.3
  107.6 9.7 %collective-permute-done.6 = bf16[2,2,144,384]{3,2,1,0:T(8,128)(2,1)S(1)} collective-permute-done((bf16[2,2,144,384]{3,2,1,0:T(8,128)(2,1)}, bf16[2,2,144,384]{3,2,1,0:T(8,128)(2,1)S(1)}, u32[]{:S(2)}, u32[]{:S(2)}) %collective-permute-start.6) | collective-permute-done | bytes 442400 | tf_op jit(solution)/shard_map/ppermute | solution.py:55
  117.4 0.8 constant_dynamic-update-slice_fusion.2.own_ref
  118.2 3.3 %collective-permute-start.7 = (bf16[2,2,768,384]{3,2,1,0:T(8,128)(2,1)}, bf16[2,2,768,384]{3,2,1,0:T(8,128)(2,1)}, u32[]{:S(2)}, u32[]{:S(2)}) collective-permute-start(bf16[2,2,768,384]{3,2,1,0:T(8,128)(2,1)} %constant_dynamic-update-slice_fusion.2.own_ref), channel_id=1, source_target_pairs={{0,64},{64,0},{1,65},{65,1},{2,66},{66,2},{3,67},{67,3},{4,68},{68... | collective-permute-start | bytes 7077896 | tf_op jit(solution)/shard_map/ppermute | solution.py:157
  121.5 4.5 %collective-permute-done.7.other_ref = bf16[2,2,768,384]{3,2,1,0:T(8,128)(2,1)} collective-permute-done((bf16[2,2,768,384]{3,2,1,0:T(8,128)(2,1)}, bf16[2,2,768,384]{3,2,1,0:T(8,128)(2,1)}, u32[]{:S(2)}, u32[]{:S(2)}) %collective-permute-start.7) | collective-permute-done | bytes 2359328 | tf_op jit(solution)/shard_map/ppermute | solution.py:157
  126.0 7.9 %all-to-all-done.1 = bf16[64,8,768]{2,1,0:T(8,128)(2,1)S(1)} async-done(((bf16[64,8,768]{2,1,0:T(8,128)(2,1)}), bf16[64,8,768]{2,1,0:T(8,128)(2,1)S(1)}, u32[]{:S(2)}, u32[]{:S(2)}) %all-to-all-start.1) | async-done | bytes 786464 | tf_op jit(solution)/shard_map/all_to_all | solution.py:43
  133.9 0.9 copy-done.2
  134.7 10.1 %shard_map.93 = (bf16[512,768]{1,0:T(8,128)(2,1)}, f32[512,768]{1,0:T(8,128)}) custom-call(bf16[512,768]{1,0:T(8,128)(2,1)} %bitcast.97, bf16[512,768]{1,0:T(8,128)(2,1)} %bitcast.92, bf16[512,768]{1,0:T(8,128)(2,1)} %bitcast.110, bf16[2,2,768,384]{3,2,1,0:T(8,128)(2,1)} %constant_dynamic-update-slice_fusion.2.own_ref, ...), custom_call_target="tpu_custom_call" | custom-call | flops 3623878656 | bytes 7077888 | tf_op jit(solution)/shard_map/pallas_call | solution.py:124
  144.8 10.7 %all-to-all-start.2 = ((bf16[64,8,768]{2,1,0:T(8,128)(2,1)}), bf16[64,8,768]{2,1,0:T(8,128)(2,1)S(1)}, u32[]{:S(2)}, u32[]{:S(2)}) async-start(bf16[64,8,768]{2,1,0:T(8,128)(2,1)} %bitcast.114), calls=%async_computation.2 | async-start | bytes 1572864 | tf_op jit(solution)/shard_map/all_to_all | solution.py:43
  155.5 8.1 %shard_map.94 = bf16[512,768]{1,0:T(8,128)(2,1)} custom-call(bf16[512,768]{1,0:T(8,128)(2,1)} %bitcast.98, bf16[512,768]{1,0:T(8,128)(2,1)} %bitcast.93, bf16[2,2,768,384]{3,2,1,0:T(8,128)(2,1)} %constant_dynamic-update-slice_fusion.2.own_ref, bf16[2,2,768,384]{3,2,1,0:T(8,128)(2,1)} %collective-permute-done.7.other_ref), custom_call_target="tpu_custom_call" | custom-call | flops 2415919104 | bytes 6291456 | tf_op jit(solution)/shard_map/pallas_call | solution.py:124
  163.6 2.2 copy.30
  165.8 0.7 fusion.4
  166.6 32.4 %all-to-all-done.2 = bf16[64,8,768]{2,1,0:T(8,128)(2,1)S(1)} async-done(((bf16[64,8,768]{2,1,0:T(8,128)(2,1)}), bf16[64,8,768]{2,1,0:T(8,128)(2,1)S(1)}, u32[]{:S(2)}, u32[]{:S(2)}) %all-to-all-start.2) | async-done | bytes 786464 | tf_op jit(solution)/shard_map/all_to_all | solution.py:43
  199.0 2.8 %fusion.9 = bf16[64,8,768]{2,1,0:T(8,128)(2,1)} fusion(bf16[512,512]{0,1:T(8,128)(2,1)} %copy-done.14, bf16[512,768]{1,0:T(8,128)(2,1)S(1)} %bitcast.112), kind=kOutput, calls=%fused_computation.18 | convolution fusion | flops 403046400 | bytes 2097152 | tf_op jit(solution)/shard_map/dot_general | solution.py:32
  201.8 5.3 %all-to-all-start.3 = ((bf16[64,8,768]{2,1,0:T(8,128)(2,1)}), bf16[64,8,768]{2,1,0:T(8,128)(2,1)S(1)}, u32[]{:S(2)}, u32[]{:S(2)}) async-start(bf16[64,8,768]{2,1,0:T(8,128)(2,1)} %fusion.9), calls=%async_computation.3 | async-start | bytes 1572864 | tf_op jit(solution)/shard_map/all_to_all | solution.py:43
  207.1 2.1 fusion.13
  209.6 38.0 %all-to-all-done.3 = bf16[64,8,768]{2,1,0:T(8,128)(2,1)S(1)} async-done(((bf16[64,8,768]{2,1,0:T(8,128)(2,1)}), bf16[64,8,768]{2,1,0:T(8,128)(2,1)S(1)}, u32[]{:S(2)}, u32[]{:S(2)}) %all-to-all-start.3) | async-done | bytes 786464 | tf_op jit(solution)/shard_map/all_to_all | solution.py:43
  248.6 2.5 collective-permute-start.8
  251.1 1.2 collective-permute-done.8
  252.3 0.8 fusion.17
  253.1 3.5 %all-to-all-start.4 = ((bf16[4,72,512]{2,1,0:T(8,128)(2,1)}), bf16[4,72,512]{2,1,0:T(8,128)(2,1)S(1)}, u32[]{:S(2)}, u32[]{:S(2)}) async-start(bf16[4,72,512]{2,1,0:T(8,128)(2,1)} %fusion.17), calls=%async_computation.4 | async-start | bytes 589824 | tf_op jit(solution)/shard_map/all_to_all | solution.py:212
  257.0 1.9 fusion.10
  258.9 1.2 copy.37
  260.0 4.5 %all-to-all-done.4 = bf16[4,72,512]{2,1,0:T(8,128)(2,1)S(1)} async-done(((bf16[4,72,512]{2,1,0:T(8,128)(2,1)}), bf16[4,72,512]{2,1,0:T(8,128)(2,1)S(1)}, u32[]{:S(2)}, u32[]{:S(2)}) %all-to-all-start.4) | async-done | bytes 294944 | tf_op jit(solution)/shard_map/all_to_all | solution.py:212
  (50 shorter events, 3.9 us)
Async XLA Ops:
  0.6 18.6 %copy-start.9 = (bf16[1,512,768]{2,1,0:T(8,128)(2,1)S(1)}, bf16[1,512,768]{2,1,0:T(8,128)(2,1)}, u32[]{:S(2)}) copy-start(bf16[1,512,768]{2,1,0:T(8,128)(2,1)} %param.6) | copy-start | bytes 2359300
  1.5 19.1 %collective-permute-start.2 = (bf16[2,2,24,384]{3,2,1,0:T(8,128)(2,1)S(1)}, bf16[2,2,24,384]{3,2,1,0:T(8,128)(2,1)S(1)}, u32[]{:S(2)}, u32[]{:S(2)}) collective-permute-start(bf16[2,2,24,384]{3,2,1,0:T(8,128)(2,1)S(1)} %fusion.37), channel_id=1, source_target_pairs={{0,256},{128,384},{256,4},{384,132},{4,260},{132,388},{260,8},{388... | collective-permute-start | bytes 221192 | tf_op jit(solution)/shard_map/ppermute | solution.py:51
  7.2 13.4 %collective-permute-start.1 = (bf16[2,2,24,384]{3,2,1,0:T(8,128)(2,1)S(1)}, bf16[2,2,24,384]{3,2,1,0:T(8,128)(2,1)S(1)}, u32[]{:S(2)}, u32[]{:S(2)}) collective-permute-start(bf16[2,2,24,384]{3,2,1,0:T(8,128)(2,1)S(1)} %fusion.37), channel_id=1, source_target_pairs={{0,396},{128,0},{256,128},{384,256},{4,384},{132,4},{260,132},{388... | collective-permute-start | bytes 221192 | tf_op jit(solution)/shard_map/ppermute | solution.py:51
  15.4 6.3 %collective-permute-start = (bf16[2,2,24,384]{3,2,1,0:T(8,128)(2,1)S(1)}, bf16[2,2,24,384]{3,2,1,0:T(8,128)(2,1)S(1)}, u32[]{:S(2)}, u32[]{:S(2)}) collective-permute-start(bf16[2,2,24,384]{3,2,1,0:T(8,128)(2,1)S(1)} %fusion.37), channel_id=1, source_target_pairs={{0,128},{128,256},{256,384},{384,4},{4,132},{132,260},{260,388},{3... | collective-permute-start | bytes 221192 | tf_op jit(solution)/shard_map/ppermute | solution.py:51
  18.4 0.8 copy-start.4
  19.2 17.5 %copy-start.13 = (bf16[8,64,64]{2,1,0:T(8,128)(2,1)S(1)}, bf16[8,64,64]{2,1,0:T(8,128)(2,1)}, u32[]{:S(2)}) copy-start(bf16[8,64,64]{2,1,0:T(8,128)(2,1)} %param.9) | copy-start | bytes 196612
  21.7 16.1 %copy-start.8 = (bf16[1,512,768]{2,1,0:T(8,128)(2,1)S(1)}, bf16[1,512,768]{2,1,0:T(8,128)(2,1)}, u32[]{:S(2)}) copy-start(bf16[1,512,768]{2,1,0:T(8,128)(2,1)} %param.7) | copy-start | bytes 2359300
  21.7 55.6 %all-to-all-start = ((bf16[64,8,768]{2,1,0:T(8,128)(2,1)}), bf16[64,8,768]{2,1,0:T(8,128)(2,1)S(1)}, u32[]{:S(2)}, u32[]{:S(2)}) async-start(bf16[64,8,768]{2,1,0:T(8,128)(2,1)} %bitcast.111), calls=%async_computation | async-start | bytes 1572864 | tf_op jit(solution)/shard_map/all_to_all | solution.py:43
  38.8 3.3 %copy-start.6 = (bf16[2,192,384]{2,1,0:T(8,128)(2,1)S(1)}, bf16[2,192,384]{2,1,0:T(8,128)(2,1)}, u32[]{:S(2)}) copy-start(bf16[2,192,384]{2,1,0:T(8,128)(2,1)} %param.11) | copy-start | bytes 884740
  38.8 3.4 %copy-start.7 = (bf16[2,384,192]{1,2,0:T(8,128)(2,1)S(1)}, bf16[2,384,192]{1,2,0:T(8,128)(2,1)}, u32[]{:S(2)}) copy-start(bf16[2,384,192]{1,2,0:T(8,128)(2,1)} %param.10) | copy-start | bytes 884740
  39.2 39.7 %copy-start.14 = (bf16[512,512]{0,1:T(8,128)(2,1)}, bf16[512,512]{0,1:T(8,128)(2,1)S(1)}, u32[]{:S(2)}) copy-start(bf16[512,512]{0,1:T(8,128)(2,1)S(1)} %fusion.11) | copy-start | bytes 1572868
  39.2 8.5 %collective-permute-start.3 = (bf16[2,2,72,384]{3,2,1,0:T(8,128)(2,1)S(1)}, bf16[2,2,72,384]{3,2,1,0:T(8,128)(2,1)S(1)}, u32[]{:S(2)}, u32[]{:S(2)}) collective-permute-start(bf16[2,2,72,384]{3,2,1,0:T(8,128)(2,1)S(1)} %pad_maximum_fusion.1), channel_id=1, source_target_pairs={{0,1},{1,0},{2,3},{3,2},{4,5},{5,4},{6,7},{7,6},{8,9},{9,8},{10,11... | collective-permute-start | bytes 663560 | tf_op jit(solution)/shard_map/ppermute | solution.py:150
  48.4 1.4 copy-start.12
  49.9 47.3 %collective-permute-start.4 = (bf16[2,2,144,384]{3,2,1,0:T(8,128)(2,1)}, bf16[2,2,144,384]{3,2,1,0:T(8,128)(2,1)S(1)}, u32[]{:S(2)}, u32[]{:S(2)}) collective-permute-start(bf16[2,2,144,384]{3,2,1,0:T(8,128)(2,1)} %get-tuple-element.43), channel_id=1, source_target_pairs={{0,16},{16,32},{32,48},{48,0},{1,17},{17,33},{33,49},{49,1},{2,18}... | collective-permute-start | bytes 1327112 | tf_op jit(solution)/shard_map/ppermute | solution.py:55
  77.4 67.5 %copy-start.10 = (bf16[64,8,768]{2,1,0:T(8,128)(2,1)}, bf16[64,8,768]{2,1,0:T(8,128)(2,1)S(1)}, u32[]{:S(2)}) copy-start(bf16[64,8,768]{2,1,0:T(8,128)(2,1)S(1)} %all-to-all-done) | copy-start | bytes 2359300
  78.9 55.0 %all-to-all-start.1 = ((bf16[64,8,768]{2,1,0:T(8,128)(2,1)}), bf16[64,8,768]{2,1,0:T(8,128)(2,1)S(1)}, u32[]{:S(2)}, u32[]{:S(2)}) async-start(bf16[64,8,768]{2,1,0:T(8,128)(2,1)} %fusion.8), calls=%async_computation.1 | async-start | bytes 1572864 | tf_op jit(solution)/shard_map/all_to_all | solution.py:43
  89.9 16.9 %collective-permute-start.5 = (bf16[2,2,144,384]{3,2,1,0:T(8,128)(2,1)}, bf16[2,2,144,384]{3,2,1,0:T(8,128)(2,1)S(1)}, u32[]{:S(2)}, u32[]{:S(2)}) collective-permute-start(bf16[2,2,144,384]{3,2,1,0:T(8,128)(2,1)} %get-tuple-element.43), channel_id=1, source_target_pairs={{0,32},{16,48},{32,0},{48,16},{1,33},{17,49},{33,1},{49,17},{2,34}... | collective-permute-start | bytes 1327112 | tf_op jit(solution)/shard_map/ppermute | solution.py:55
  94.3 23.0 %collective-permute-start.6 = (bf16[2,2,144,384]{3,2,1,0:T(8,128)(2,1)}, bf16[2,2,144,384]{3,2,1,0:T(8,128)(2,1)S(1)}, u32[]{:S(2)}, u32[]{:S(2)}) collective-permute-start(bf16[2,2,144,384]{3,2,1,0:T(8,128)(2,1)} %get-tuple-element.43), channel_id=1, source_target_pairs={{0,48},{16,0},{32,16},{48,32},{1,49},{17,1},{33,17},{49,33},{2,50}... | collective-permute-start | bytes 1327112 | tf_op jit(solution)/shard_map/ppermute | solution.py:55
  118.2 7.8 %collective-permute-start.7 = (bf16[2,2,768,384]{3,2,1,0:T(8,128)(2,1)}, bf16[2,2,768,384]{3,2,1,0:T(8,128)(2,1)}, u32[]{:S(2)}, u32[]{:S(2)}) collective-permute-start(bf16[2,2,768,384]{3,2,1,0:T(8,128)(2,1)} %constant_dynamic-update-slice_fusion.2.own_ref), channel_id=1, source_target_pairs={{0,64},{64,0},{1,65},{65,1},{2,66},{66,2},{3,67},{67,3},{4,68},{68... | collective-permute-start | bytes 7077896 | tf_op jit(solution)/shard_map/ppermute | solution.py:157
  133.9 0.9 copy-start.2
  144.8 54.2 %all-to-all-start.2 = ((bf16[64,8,768]{2,1,0:T(8,128)(2,1)}), bf16[64,8,768]{2,1,0:T(8,128)(2,1)S(1)}, u32[]{:S(2)}, u32[]{:S(2)}) async-start(bf16[64,8,768]{2,1,0:T(8,128)(2,1)} %bitcast.114), calls=%async_computation.2 | async-start | bytes 1572864 | tf_op jit(solution)/shard_map/all_to_all | solution.py:43
  155.5 10.3 %copy-start.5 = (f32[512,768]{1,0:T(8,128)S(1)}, f32[512,768]{1,0:T(8,128)}, u32[]{:S(2)}) copy-start(f32[512,768]{1,0:T(8,128)} %get-tuple-element.24) | copy-start | bytes 4718596
  163.6 2.2 copy-start
  163.6 2.2 copy-start.3
  199.0 2.8 %copy-start.11 = (bf16[64,8,768]{2,1,0:T(8,128)(2,1)}, bf16[64,8,768]{2,1,0:T(8,128)(2,1)S(1)}, u32[]{:S(2)}) copy-start(bf16[64,8,768]{2,1,0:T(8,128)(2,1)S(1)} %all-to-all-done.2) | copy-start | bytes 2359300
  201.8 45.8 %all-to-all-start.3 = ((bf16[64,8,768]{2,1,0:T(8,128)(2,1)}), bf16[64,8,768]{2,1,0:T(8,128)(2,1)S(1)}, u32[]{:S(2)}, u32[]{:S(2)}) async-start(bf16[64,8,768]{2,1,0:T(8,128)(2,1)} %fusion.9), calls=%async_computation.3 | async-start | bytes 1572864 | tf_op jit(solution)/shard_map/all_to_all | solution.py:43
  247.6 0.9 copy-start.1
  248.6 3.7 %collective-permute-start.8 = (bf16[4,72,512]{2,1,0:T(8,128)(2,1)S(1)}, bf16[4,72,512]{2,1,0:T(8,128)(2,1)S(1)}, u32[]{:S(2)}, u32[]{:S(2)}) collective-permute-start(bf16[4,72,512]{2,1,0:T(8,128)(2,1)S(1)} %fusion.22), channel_id=1, source_target_pairs={{0,64},{64,0},{1,65},{65,1},{2,66},{66,2},{3,67},{67,3},{4,68},{68... | collective-permute-start | bytes 884744 | tf_op jit(solution)/shard_map/ppermute | solution.py:210
  253.1 11.5 %all-to-all-start.4 = ((bf16[4,72,512]{2,1,0:T(8,128)(2,1)}), bf16[4,72,512]{2,1,0:T(8,128)(2,1)S(1)}, u32[]{:S(2)}, u32[]{:S(2)}) async-start(bf16[4,72,512]{2,1,0:T(8,128)(2,1)} %fusion.17), calls=%async_computation.4 | async-start | bytes 589824 | tf_op jit(solution)/shard_map/all_to_all | solution.py:212
